TPU v7x, 128 devices: a whole 4x4x4 slice. The times are simulated.
128 devices in a mesh: planes: 16 (over y, x_lo, core), rows: 8 (over x_hi, z).
Axes of the slice: x: 4 (x_hi: 2, x_lo: 2; x = x_hi * 2 + x_lo), y: 4, z: 4, core: 2. Of those that a mesh axis runs over, the one named last changes fastest.
Arguments:
- observed: float32 [16, 1024, 1024], P('planes', 'rows'), may hold values from -6 to 6
- estimate: float32 [16, 1024, 1024], P('planes', 'rows'), may hold values from -6 to 6
- spectrum: float32 [16, 1024, 1024], P('planes', 'rows'), may hold values from 0.1 to 1
Outputs:
- restored: float32 [16, 1024, 1024], P('planes', 'rows')
- residual: float32 [16, 1024, 1024], P('planes', 'rows')
All inputs are finite; a program needn't handle non-finite values.
Results may differ from a plain program's by a relative error of at most 0.00014.
Values sent between devices are 32-bit elements; how exact they have to be, the bound alone decides.
No kernel may reach another device: no remote copies, remote signals or barrier semaphores. Data moves between devices by JAX's collectives and lax.ppermute only.
A program may use at most 128 MiB of HBM per device.

v0:
```python
import math

import jax
import jax.numpy as jnp
import numpy as np
from jax import lax
from jax.experimental import pallas as pl
from jax.experimental.pallas import tpu as pltpu
from jax.sharding import Mesh
from jax.sharding import PartitionSpec as P

PLANES = ("planes_0", "planes_1", "planes_2")
ROWS = ("rows_0", "rows_1")
ALL = PLANES + ROWS
N = 1024
R = 128
G = 8
HUBER_EDGE = 0.5
SMOOTHING = 0.3
F32 = jnp.float32
BF16 = jnp.bfloat16
VMEM = pl.BlockSpec(memory_space=pltpu.VMEM)
SMEM = pl.BlockSpec(memory_space=pltpu.SMEM)


def call(body, outs, name, flops, scratch=(), limit=24):
    def run(*args):
        size = sum(math.prod(a.shape) * a.dtype.itemsize for a in args)
        size += sum(math.prod(o.shape) * o.dtype.itemsize for o in outs)
        return pl.pallas_call(
            body,
            out_shape=tuple(outs),
            in_specs=[SMEM if a.dtype == jnp.int32 else VMEM for a in args],
            out_specs=tuple(VMEM for _ in outs),
            scratch_shapes=list(scratch),
            compiler_params=pltpu.CompilerParams(vmem_limit_bytes=limit << 20),
            cost_estimate=pl.CostEstimate(flops=flops, bytes_accessed=size, transcendentals=0),
            name=name,
        )(*args)

    return run


def shape(*dims, dtype=F32):
    return jax.ShapeDtypeStruct(dims, dtype)


def angle_tables():
    step = math.pi / (2.0 * N)
    coarse = np.arange(32)[:, None]
    fine = np.arange(32)[:, None]
    lane = np.arange(N)[None, :]
    norm = np.where(lane == 0, math.sqrt(1.0 / N), math.sqrt(2.0 / N))
    a_t = (lane * 64 * coarse) % (4 * N) * step
    b_t = (lane * (2 * fine + 1)) % (4 * N) * step
    sample_major = (np.cos(a_t), np.sin(a_t), np.cos(b_t) * norm, np.sin(b_t) * norm)
    odd = 2 * lane + 1
    a = (odd * 32 * coarse) % (4 * N) * step
    b = (odd * fine) % (4 * N) * step
    scale = math.sqrt(2.0 / N)
    freq_major = (np.cos(a), np.sin(a), np.cos(b) * scale, np.sin(b) * scale)
    return (
        np.stack(sample_major).astype(np.float32),
        np.stack(freq_major).astype(np.float32),
    )


def split(x):
    high = x.astype(BF16)
    low = (x - high.astype(F32)).astype(BF16)
    return high, low


def build_matrix(table, high, low, first_row):
    for a in range(32):
        rows = slice(32 * a, 32 * a + 32)
        value = table[0, a : a + 1, :] * table[2] - table[1, a : a + 1, :] * table[3]
        if first_row is not None and a == 0:
            row = lax.broadcasted_iota(jnp.int32, (32, N), 0)
            value = jnp.where(row == 0, first_row, value)
        high[rows, :], low[rows, :] = split(value)


def dot(a, b):
    return jnp.dot(a, b, preferred_element_type=F32)


def stacked_times(stack, rows, high, low, columns):
    both = dot(stack[0 : 2 * rows, :], high[:, columns])
    return both[:rows] + both[rows:] + dot(stack[0:rows, :], low[:, columns])


def matrix_times(high, low, rows, pair, width):
    both = dot(high[rows, :], pair[:, 0 : 2 * width])
    return both[:, :width] + both[:, width:] + dot(low[rows, :], pair[:, 0:width])


def first_kernel(observed, estimate, spectrum, table, sent, high, low, stack):
    build_matrix(table, high, low, None)
    stack[0:R, :], stack[2 * R : 3 * R, :] = split(observed[0])
    stack[R : 2 * R, :], stack[3 * R : 4 * R, :] = split(estimate[0])
    for d in range(G // 2):
        out = stacked_times(stack, 2 * R, high, low, slice(256 * d, 256 * d + 256))
        for h in range(2):
            lanes = slice(128 * h, 128 * h + 128)
            sent[2 * d + h, 0] = spectrum[0, :, 256 * d + 128 * h : 256 * d + 128 * h + 128]
            sent[2 * d + h, 1] = out[:R, lanes]
            sent[2 * d + h, 2] = out[R:, lanes]


def second_matrix_kernel(table, high, low):
    build_matrix(table, high, low, math.sqrt(1.0 / N))


def left(x):
    return pltpu.roll(x, N - 1, 1)


def weight_of(plane, row, value, last):
    column = jnp.where(last, 0.0, left(value) - value)
    square = plane * plane + row * row + column * column
    return 1.0 / jnp.maximum(jnp.sqrt(square), HUBER_EDGE)


def divergence(value, ahead_plane, behind_plane, ahead_row, behind_row, w_plane, w_back, w_row, w_row_back, w_col):
    flux_col = w_col * (left(value) - value)
    total = w_back * (value - behind_plane) - w_plane * (ahead_plane - value)
    total += w_row_back * (value - behind_row) - w_row * (ahead_row - value)
    total += pltpu.roll(flux_col, 1, 1) - flux_col
    return SMOOTHING * total


CHUNK = 16


def weights_kernel(
    place, estimate, behind, ahead, top, bottom, behind_bottom, ahead_top, high, low,
    reg, reg_sent, w_all, w_back_all, w_top, ext, ext_w, ext_back, stack,
):
    plane, row = place[0], place[1]
    ok_plane = jnp.where(plane < 15, 1.0, 0.0)
    ok_back = jnp.where(plane > 0, 1.0, 0.0)
    ok_top = jnp.where(row > 0, 1.0, 0.0)
    ok_bottom = jnp.where(row < G - 1, 1.0, 0.0)
    ext[7:8, :] = top[0]
    ext[8 : 8 + R, :] = estimate[0]
    ext[8 + R : 9 + R, :] = jnp.where(row < G - 1, bottom[0], estimate[0, R - 1 : R, :])
    ext_back[0:R, :] = behind[0]
    ext_back[R : R + 1, :] = jnp.where(row < G - 1, behind_bottom[0], behind[0, R - 1 : R, :])
    last1 = lax.broadcasted_iota(jnp.int32, (1, N), 1) == N - 1
    edge = ext[7:8, :]
    w_edge = weight_of(
        (ahead_top[0] - edge) * ok_plane, (ext[8:9, :] - edge) * ok_top, edge, last1
    ) * ok_top
    w_top[...] = w_edge
    ext_w[7:8, :] = w_edge
    last = lax.broadcasted_iota(jnp.int32, (CHUNK, N), 1) == N - 1
    for c in range(0, R, CHUNK):
        value = ext[8 + c : 8 + c + CHUNK, :]
        back = ext_back[c : c + CHUNK, :]
        w = weight_of(
            (ahead[0, c : c + CHUNK, :] - value) * ok_plane,
            ext[9 + c : 9 + c + CHUNK, :] - value,
            value,
            last,
        )
        ext_w[8 + c : 8 + c + CHUNK, :] = w
        w_all[c : c + CHUNK, :] = w
        w_back = weight_of(
            (value - back) * ok_back, ext_back[1 + c : 1 + c + CHUNK, :] - back, back, last
        ) * ok_back
        w_back_all[c : c + CHUNK, :] = w_back
    for c in range(0, R, CHUNK):
        value = ext[8 + c : 8 + c + CHUNK, :]
        w = ext_w[8 + c : 8 + c + CHUNK, :]
        out = divergence(
            value,
            ahead[0, c : c + CHUNK, :],
            behind[0, c : c + CHUNK, :],
            ext[9 + c : 9 + c + CHUNK, :],
            ext[7 + c : 7 + c + CHUNK, :],
            w * ok_plane,
            w_back_all[c : c + CHUNK, :],
            w,
            ext_w[7 + c : 7 + c + CHUNK, :],
            jnp.where(last, 0.0, w),
        )
        reg[c : c + CHUNK, :] = out
        stack[c : c + CHUNK, :], stack[R + c : R + c + CHUNK, :] = split(out)
    for d in range(G // 2):
        out = stacked_times(stack, R, high, low, slice(256 * d, 256 * d + 256))
        reg_sent[2 * d] = out[:, :128]
        reg_sent[2 * d + 1] = out[:, 128:]


def middle_kernel(got, reg_sent, f_high, f_low, s_high, s_low, sent, spectral, pair):
    for d in range(G):
        rows = slice(R * d, R * d + R)
        pair[rows, 0:128], pair[rows, 256:384] = split(got[d, 1])
        pair[rows, 128:256], pair[rows, 384:512] = split(got[d, 2])
    parts = []
    for m in range(4):
        rows = slice(256 * m, 256 * m + 256)
        out = matrix_times(f_high, f_low, rows, pair, 256)
        gain = jnp.concatenate([got[2 * m, 0], got[2 * m + 1, 0]], axis=0)
        spectral[rows, :] = gain * (out[:, :128] - gain * out[:, 128:])
    for d in range(G):
        rows = slice(R * d, R * d + R)
        pair[rows, 0:128], pair[rows, 128:256] = split(spectral[rows, :])
    for m in range(4):
        rows = slice(256 * m, 256 * m + 256)
        out = matrix_times(s_high, s_low, rows, pair, 128)
        parts.append(out)
        sent[2 * m, 0:R] = out[:R]
        sent[2 * m + 1, 0:R] = out[R:]
    for d in range(G):
        sent[d, R : R + 8] = jnp.zeros((8, 128), F32)
        sent[d, R + 8 :] = reg_sent[d]
    for d in range(G):
        if d > 0:
            sent[d, R : R + 1] = sent[d - 1, R - 1 : R]
        if d < G - 1:
            sent[d, R + 1 : R + 2] = sent[d + 1, 0:1]


def residual_kernel(got, reg, reg_top, reg_bottom, f_high, f_low, residual, edges, stack):
    rows = R + 16
    for d in range(G):
        lanes = slice(128 * d, 128 * d + 128)
        high, low = split(got[d, 0 : R + 8])
        pad = jnp.zeros((8, 128), BF16)
        stack[0:rows, lanes] = jnp.concatenate([high, pad], axis=0)
        stack[rows : 2 * rows, lanes] = jnp.concatenate([low, pad], axis=0)
    for d in range(G // 2):
        lanes = slice(256 * d, 256 * d + 256)
        out = stacked_times(stack, rows, f_high, f_low, lanes)
        residual[0, :, lanes] = out[:R] - reg[:, lanes]
        edges[0:1, lanes] = out[R : R + 1] - reg_top[0, :, lanes]
        edges[1:2, lanes] = out[R + 1 : R + 2] - reg_bottom[0, :, lanes]


def curvature_kernel(got, first, spectral, f_high, f_low, s_high, s_low, sent, total, pair):
    for d in range(G):
        rows = slice(R * d, R * d + R)
        pair[rows, 0:128], pair[rows, 128:256] = split(got[d, R + 8 :])
    acc = jnp.zeros((8, 128), F32)
    for m in range(4):
        rows = slice(256 * m, 256 * m + 256)
        out = spectral[rows, :] - matrix_times(f_high, f_low, rows, pair, 128)
        gain = jnp.concatenate([first[2 * m, 0], first[2 * m + 1, 0]], axis=0)
        scaled = gain * gain * out
        acc += jnp.sum((scaled * out).reshape(32, 8, 128), axis=0)
        pair[rows, 256:384], pair[rows, 384:512] = split(scaled)
    total[...] = acc
    for m in range(4):
        rows = slice(256 * m, 256 * m + 256)
        both = dot(s_high[rows, :], pair[:, 256:512])
        out = both[:, :128] + both[:, 128:] + dot(s_low[rows, :], pair[:, 256:384])
        sent[2 * m] = out[:R]
        sent[2 * m + 1] = out[R:]


def inner_kernel(
    place, residual, behind, ahead, edges, w_all, w_back_all, w_top, half_sent, total,
    reg, sent, ext, ext_w,
):
    plane, row = place[0], place[1]
    ok_plane = jnp.where(plane < 15, 1.0, 0.0)
    ext[7:8, :] = edges[0:1, :]
    ext[8 : 8 + R, :] = residual[0]
    ext[8 + R : 9 + R, :] = jnp.where(row < G - 1, edges[1:2, :], residual[0, R - 1 : R, :])
    ext_w[7:8, :] = w_top[...]
    ext_w[8 : 8 + R, :] = w_all[...]
    last = lax.broadcasted_iota(jnp.int32, (CHUNK, N), 1) == N - 1
    norm = jnp.zeros((8, N), F32)
    product = jnp.zeros((8, N), F32)
    for c in range(0, R, CHUNK):
        value = ext[8 + c : 8 + c + CHUNK, :]
        w = ext_w[8 + c : 8 + c + CHUNK, :]
        out = divergence(
            value,
            ahead[0, c : c + CHUNK, :],
            behind[0, c : c + CHUNK, :],
            ext[9 + c : 9 + c + CHUNK, :],
            ext[7 + c : 7 + c + CHUNK, :],
            w * ok_plane,
            w_back_all[c : c + CHUNK, :],
            w,
            ext_w[7 + c : 7 + c + CHUNK, :],
            jnp.where(last, 0.0, w),
        )
        reg[c : c + CHUNK, :] = out
        square = value * value
        cross = value * out
        norm += square[:8] + square[8:]
        product += cross[:8] + cross[8:]
    norm = jnp.sum(jnp.sum(norm, axis=0, keepdims=True).reshape(8, 128), axis=0, keepdims=True)
    product = jnp.sum(
        jnp.sum(product, axis=0, keepdims=True).reshape(8, 128) + total[...],
        axis=0, keepdims=True,
    )
    tile = jnp.concatenate([norm, product, jnp.zeros((6, 128), F32)], axis=0)
    for d in range(G):
        sent[d, 0:R] = half_sent[d]
        sent[d, R:] = tile


def image_kernel(got, reg, f_high, f_low, image, stack):
    for d in range(G):
        lanes = slice(128 * d, 128 * d + 128)
        stack[0:R, lanes], stack[R : 2 * R, lanes] = split(got[d, 0:R])
    for d in range(G // 2):
        lanes = slice(256 * d, 256 * d + 256)
        image[:, lanes] = stacked_times(stack, R, f_high, f_low, lanes) + reg[:, lanes]


def last_kernel(sums, estimate, residual, image, restored, final):
    tile = jnp.sum(sums[...], axis=0)
    norm = jnp.sum(tile[0:1, :], axis=1, keepdims=True)
    product = jnp.sum(tile[1:2, :], axis=1, keepdims=True)
    step = norm / product
    restored[0] = estimate[0] + step * residual[0]
    final[0] = residual[0] - step * image[...]


def across(x, axes):
    return lax.all_to_all(x, axes, split_axis=0, concat_axis=0, tiled=True)


def shards(observed, estimate, spectrum):
    planes, groups = 16, G
    place = jnp.stack([lax.axis_index(PLANES), lax.axis_index(ROWS)]).astype(jnp.int32)
    sample_table, freq_table = angle_tables()
    up = [(i, i + 1) for i in range(planes - 1)]
    down = [(i + 1, i) for i in range(planes - 1)]
    row_up = [(i, i + 1) for i in range(groups - 1)]
    row_down = [(i + 1, i) for i in range(groups - 1)]

    def device(p, r):
        return p * groups + r

    diagonal_from_behind = [
        (device(p - 1, r + 1), device(p, r)) for p in range(1, planes) for r in range(groups - 1)
    ]
    diagonal_from_ahead = [
        (device(p + 1, r - 1), device(p, r)) for p in range(planes - 1) for r in range(1, groups)
    ]
    matrix = shape(N, N, dtype=BF16)
    big = 2 * N * N * R

    sent, s_high, s_low = call(
        first_kernel,
        (shape(G, 3, R, 128), matrix, matrix),
        "first", 6 * big,
        (pltpu.VMEM((4 * R, N), BF16),),
    )(observed, estimate, spectrum, jnp.asarray(sample_table))
    first = across(sent, ROWS)

    f_high, f_low = call(second_matrix_kernel, (matrix, matrix), "matrix", 4 * N * N)(
        jnp.asarray(freq_table)
    )
    behind = lax.ppermute(estimate, PLANES, up)
    ahead = lax.ppermute(estimate, PLANES, down)
    head, tail = estimate[:, :1], estimate[:, R - 1 :]
    top = lax.ppermute(tail, ROWS, row_up)
    bottom = lax.ppermute(head, ROWS, row_down)
    behind_bottom = lax.ppermute(head, ALL, diagonal_from_behind)
    ahead_top = lax.ppermute(tail, ALL, diagonal_from_ahead)
    block = shape(R, N)
    reg, reg_sent, w_all, w_back, w_top = call(
        weights_kernel,
        (block, shape(G, R, 128), block, block, shape(1, N)),
        "weights", 3 * big,
        (
            pltpu.VMEM((R + 16, N), F32),
            pltpu.VMEM((R + 16, N), F32),
            pltpu.VMEM((R + 8, N), F32),
            pltpu.VMEM((2 * R, N), BF16),
        ),
    )(place, estimate, behind, ahead, top, bottom, behind_bottom, ahead_top, s_high, s_low)
    reg_top = lax.ppermute(reg[None, R - 1 :], ROWS, row_up)
    reg_bottom = lax.ppermute(reg[None, :1], ROWS, row_down)

    sent, spectral = call(
        middle_kernel,
        (shape(G, 2 * R + 8, 128), shape(N, 128)),
        "middle", 9 * big,
        (pltpu.VMEM((N, 512), BF16),),
    )(first, reg_sent, f_high, f_low, s_high, s_low)
    second = across(sent, ROWS)

    residual, edges = call(
        residual_kernel,
        (shape(1, R, N), shape(8, N)),
        "residual", 3 * big,
        (pltpu.VMEM((2 * R + 32, N), BF16),),
    )(second, reg, reg_top, reg_bottom, f_high, f_low)
    behind = lax.ppermute(residual, PLANES, up)
    ahead = lax.ppermute(residual, PLANES, down)
    half_sent, total = call(
        curvature_kernel,
        (shape(G, R, 128), shape(8, 128)),
        "curvature", 6 * big,
        (pltpu.VMEM((N, 512), BF16),),
    )(second, first, spectral, f_high, f_low, s_high, s_low)
    reg_residual, sent = call(
        inner_kernel,
        (block, shape(G, R + 8, 128)),
        "inner", big // 16,
        (pltpu.VMEM((R + 16, N), F32), pltpu.VMEM((R + 16, N), F32)),
    )(place, residual, behind, ahead, edges, w_all, w_back, w_top, half_sent, total)
    third = across(sent, ROWS)

    tile = jnp.sum(third[:, R:], axis=0)
    sums = across(jnp.broadcast_to(tile[None], (planes, 8, 128)), PLANES)
    image = call(
        image_kernel, (block,), "image", 3 * big, (pltpu.VMEM((2 * R, N), BF16),)
    )(third, reg_residual, f_high, f_low)[0]
    return call(last_kernel, (shape(1, R, N), shape(1, R, N)), "last", R * N * 4)(
        sums, estimate, residual, image
    )


def solution(mesh):
    finer = Mesh(
        mesh.devices.reshape(4, 2, 2, 2, 4),
        ("planes_0", "planes_1", "planes_2", "rows_0", "rows_1"),
    )
    spec = P(PLANES, ROWS, None)
    return jax.shard_map(
        shards,
        mesh=finer,
        in_specs=(spec, spec, spec),
        out_specs=(spec, spec),
        check_vma=False,
    )
```

profile of v0, /device:TPU:1, one launch (start us, length us, event | category | flops | bytes accessed | tf_op | source)
XLA Modules:
  0.0 154.3 jit_solution(9791006242559806728)
XLA Ops:
  1.7 1.0 copy-done.34
  2.7 1.0 copy-done.35
  3.8 1.0 copy-done.36
  4.8 3.1 %first.1 = (f32[8,3,128,128]{3,2,1,0:T(8,128)}, bf16[1024,1024]{1,0:T(8,128)(2,1)S(1)}, bf16[1024,1024]{1,0:T(8,128)(2,1)S(1)}) custom-call(f32[1,128,1024]{2,1,0:T(8,128)S(1)} %copy-done.34, f32[1,128,1024]{2,1,0:T(8,128)S(1)} %copy-done.13, f32[1,128,1024]{2,1,0:T(8,128)S(1)} %copy-done.35, f32[4,32,1024]{2,1,0:T(8,128)S(1)} %copy-done.36), custom_call_target="tpu_custom_call" | custom-call | flops 1610612736 | bytes 7864320 | tf_op jit(solution)/shard_map/first/pallas_call | solution.py:30
  7.9 1.4 copy-done.5
  9.3 1.3 copy-done.9
  10.6 8.4 %all-to-all-start = ((f32[8,3,128,128]{3,2,1,0:T(8,128)}), f32[8,3,128,128]{3,2,1,0:T(8,128)}, u32[]{:S(2)}, u32[]{:S(2)}) async-start(f32[8,3,128,128]{3,2,1,0:T(8,128)} %get-tuple-element.20), calls=%async_computation | async-start | bytes 3145728 | tf_op jit(solution)/shard_map/all_to_all | solution.py:327
  19.1 3.1 %collective-permute-start = (f32[1,128,1024]{2,1,0:T(8,128)S(1)}, f32[1,128,1024]{2,1,0:T(8,128)S(1)}, u32[]{:S(2)}, u32[]{:S(2)}) collective-permute-start(f32[1,128,1024]{2,1,0:T(8,128)S(1)} %copy-done.14), channel_id=1, source_target_pairs={{0,8},{8,16},{16,24},{24,32},{32,40},{40,48},{48,56},{56,64},{64,7... | collective-permute-start | bytes 1572872 | tf_op jit(solution)/shard_map/ppermute | solution.py:362
  22.1 1.9 %collective-permute-start.1 = (f32[1,128,1024]{2,1,0:T(8,128)S(1)}, f32[1,128,1024]{2,1,0:T(8,128)}, u32[]{:S(2)}, u32[]{:S(2)}) collective-permute-start(f32[1,128,1024]{2,1,0:T(8,128)S(1)} %copy-done.14), channel_id=1, source_target_pairs={{8,0},{16,8},{24,16},{32,24},{40,32},{48,40},{56,48},{64,56},{72,6... | collective-permute-start | bytes 1572872 | tf_op jit(solution)/shard_map/ppermute | solution.py:363
  24.1 3.6 %collective-permute-start.2 = (f32[1,1,1024]{2,1,0:T(1,128)S(1)}, f32[1,1,1024]{2,1,0:T(1,128)S(1)}, u32[]{:S(2)}, u32[]{:S(2)}) collective-permute-start(f32[1,1,1024]{2,1,0:T(1,128)S(1)} %get-tuple-element.41), channel_id=1, source_target_pairs={{0,1},{1,2},{2,3},{3,4},{4,5},{5,6},{6,7},{8,9},{9,10},{10,11},{11... | collective-permute-start | bytes 12296 | tf_op jit(solution)/shard_map/ppermute | solution.py:365
  27.7 1.3 collective-permute-start.3
  29.0 1.3 collective-permute-start.4
  30.3 3.8 %collective-permute-done.2.top = f32[1,1,1024]{2,1,0:T(1,128)S(1)} collective-permute-done((f32[1,1,1024]{2,1,0:T(1,128)S(1)}, f32[1,1,1024]{2,1,0:T(1,128)S(1)}, u32[]{:S(2)}, u32[]{:S(2)}) %collective-permute-start.2) | collective-permute-done | bytes 4128 | tf_op jit(solution)/shard_map/ppermute | solution.py:365
  34.1 7.1 %collective-permute-start.5 = (f32[1,1,1024]{2,1,0:T(1,128)S(1)}, f32[1,1,1024]{2,1,0:T(1,128)S(1)}, u32[]{:S(2)}, u32[]{:S(2)}) collective-permute-start(f32[1,1,1024]{2,1,0:T(1,128)S(1)} %get-tuple-element.41), channel_id=1, source_target_pairs={{8,1},{9,2},{10,3},{11,4},{12,5},{13,6},{14,7},{16,9},{17,10},{18,... | collective-permute-start | bytes 12296 | tf_op jit(solution)/shard_map/ppermute | solution.py:368
  41.3 1.0 copy-done.27
  43.4 1.3 copy-done
  44.7 4.0 %collective-permute-done.1.ahead = f32[1,128,1024]{2,1,0:T(8,128)} collective-permute-done((f32[1,128,1024]{2,1,0:T(8,128)S(1)}, f32[1,128,1024]{2,1,0:T(8,128)}, u32[]{:S(2)}, u32[]{:S(2)}) %collective-permute-start.1) | collective-permute-done | bytes 524320 | tf_op jit(solution)/shard_map/ppermute | solution.py:363
  48.7 1.6 %copy-done.6 = bf16[1024,1024]{1,0:T(8,128)(2,1)S(1)} copy-done((bf16[1024,1024]{1,0:T(8,128)(2,1)S(1)}, bf16[1024,1024]{1,0:T(8,128)(2,1)}, u32[]{:S(2)}) %copy-start.6) | copy-done | bytes 2097176
  50.3 1.6 %copy-done.10 = bf16[1024,1024]{1,0:T(8,128)(2,1)S(1)} copy-done((bf16[1024,1024]{1,0:T(8,128)(2,1)S(1)}, bf16[1024,1024]{1,0:T(8,128)(2,1)}, u32[]{:S(2)}) %copy-start.10) | copy-done | bytes 2097176
  51.9 3.4 %weights.1 = (f32[128,1024]{1,0:T(8,128)S(1)}, f32[8,128,128]{2,1,0:T(8,128)S(1)}, f32[128,1024]{1,0:T(8,128)S(1)}, f32[128,1024]{1,0:T(8,128)S(1)}, f32[1,1024]{1,0:T(1,128)S(1)}) custom-call(s32[2]{0:T(128)S(1)} %pad_add_fusion.place, f32[1,128,1024]{2,1,0:T(8,128)S(1)} %copy-done.14, f32[1,128,1024]{2,1,0:T(8,128)S(1)} %collective-permute-done.behind, ...), custom_call_target="tpu_custom_call" | custom-call | flops 805306368 | bytes 7884808 | tf_op jit(solution)/shard_map/weights/pallas_call | solution.py:30
  58.5 1.6 %copy-done.1 = bf16[1024,1024]{1,0:T(8,128)(2,1)S(1)} copy-done((bf16[1024,1024]{1,0:T(8,128)(2,1)S(1)}, bf16[1024,1024]{1,0:T(8,128)(2,1)}, u32[]{:S(2)}) %copy-start.1) | copy-done | bytes 2097176
  60.1 1.6 %copy-done.7 = bf16[1024,1024]{1,0:T(8,128)(2,1)S(1)} copy-done((bf16[1024,1024]{1,0:T(8,128)(2,1)S(1)}, bf16[1024,1024]{1,0:T(8,128)(2,1)}, u32[]{:S(2)}) %copy-start.7) | copy-done | bytes 2097176
  61.7 1.6 %copy-done.11 = bf16[1024,1024]{1,0:T(8,128)(2,1)S(1)} copy-done((bf16[1024,1024]{1,0:T(8,128)(2,1)S(1)}, bf16[1024,1024]{1,0:T(8,128)(2,1)}, u32[]{:S(2)}) %copy-start.11) | copy-done | bytes 2097176
  63.3 1.0 copy-done.26
  64.4 4.4 %middle.1 = (f32[8,264,128]{2,1,0:T(8,128)S(1)}, f32[1024,128]{1,0:T(8,128)S(1)}) custom-call(f32[8,3,128,128]{3,2,1,0:T(8,128)} %all-to-all-done.got.first, f32[8,128,128]{2,1,0:T(8,128)S(1)} %copy-done.26, bf16[1024,1024]{1,0:T(8,128)(2,1)S(1)} %get-tuple-element.24.f_high, bf16[1024,1024]{1,0:T(8,128)(2,1)S(1)} %copy-done.1, ...), custom_call_target="tpu_custom_call" | custom-call | flops 2415919104 | bytes 12091392 | tf_op jit(solution)/shard_map/middle/pallas_call | solution.py:30
  68.8 1.1 copy-done.20
  70.6 11.9 %all-to-all-start.1 = ((f32[8,264,128]{2,1,0:T(8,128)}), f32[8,264,128]{2,1,0:T(8,128)S(1)}, u32[]{:S(2)}, u32[]{:S(2)}) async-start(f32[8,264,128]{2,1,0:T(8,128)} %copy-done.20), calls=%async_computation.1 | async-start | bytes 2162688 | tf_op jit(solution)/shard_map/all_to_all | solution.py:327
  83.3 3.4 %collective-permute-start.6 = (f32[1,1,1024]{2,1,0:T(1,128)S(1)}, f32[1,1,1024]{2,1,0:T(1,128)S(1)}, u32[]{:S(2)}, u32[]{:S(2)}) collective-permute-start(f32[1,1,1024]{2,1,0:T(1,128)S(1)} %get-tuple-element.39), channel_id=1, source_target_pairs={{0,1},{1,2},{2,3},{3,4},{4,5},{5,6},{6,7},{8,9},{9,10},{10,11},{11... | collective-permute-start | bytes 12296 | tf_op jit(solution)/shard_map/ppermute | solution.py:381
  86.7 1.3 collective-permute-start.7
  88.3 3.4 %collective-permute-done.7.reg_bottom = f32[1,1,1024]{2,1,0:T(1,128)S(1)} collective-permute-done((f32[1,1,1024]{2,1,0:T(1,128)S(1)}, f32[1,1,1024]{2,1,0:T(1,128)S(1)}, u32[]{:S(2)}, u32[]{:S(2)}) %collective-permute-start.7) | collective-permute-done | bytes 4128 | tf_op jit(solution)/shard_map/ppermute | solution.py:382
  91.7 2.5 %all-to-all-done.1.got = f32[8,264,128]{2,1,0:T(8,128)S(1)} async-done(((f32[8,264,128]{2,1,0:T(8,128)}), f32[8,264,128]{2,1,0:T(8,128)S(1)}, u32[]{:S(2)}, u32[]{:S(2)}) %all-to-all-start.1) | async-done | bytes 1081376 | tf_op jit(solution)/shard_map/all_to_all | solution.py:327
  94.2 1.6 %copy-done.2 = bf16[1024,1024]{1,0:T(8,128)(2,1)S(1)} copy-done((bf16[1024,1024]{1,0:T(8,128)(2,1)S(1)}, bf16[1024,1024]{1,0:T(8,128)(2,1)}, u32[]{:S(2)}) %copy-start.2) | copy-done | bytes 2097176
  95.8 1.0 copy-done.22
  96.8 1.1 residual.1
  97.9 10.6 %collective-permute-start.8 = (f32[1,128,1024]{2,1,0:T(8,128)S(1)}, f32[1,128,1024]{2,1,0:T(8,128)S(1)}, u32[]{:S(2)}, u32[]{:S(2)}) collective-permute-start(f32[1,128,1024]{2,1,0:T(8,128)S(1)} %get-tuple-element.28.residual), channel_id=1, source_target_pairs={{0,8},{8,16},{16,24},{24,32},{32,40},{40,48},{48,56},{56,64},{64,7... | collective-permute-start | bytes 1572872 | tf_op jit(solution)/shard_map/ppermute | solution.py:398
  108.5 2.1 %collective-permute-start.9 = (f32[1,128,1024]{2,1,0:T(8,128)S(1)}, f32[1,128,1024]{2,1,0:T(8,128)S(1)}, u32[]{:S(2)}, u32[]{:S(2)}) collective-permute-start(f32[1,128,1024]{2,1,0:T(8,128)S(1)} %get-tuple-element.28.residual), channel_id=1, source_target_pairs={{8,0},{16,8},{24,16},{32,24},{40,32},{48,40},{56,48},{64,56},{72,6... | collective-permute-start | bytes 1572872 | tf_op jit(solution)/shard_map/ppermute | solution.py:399
  110.6 1.6 %copy-done.12 = bf16[1024,1024]{1,0:T(8,128)(2,1)S(1)} copy-done((bf16[1024,1024]{1,0:T(8,128)(2,1)S(1)}, bf16[1024,1024]{1,0:T(8,128)(2,1)}, u32[]{:S(2)}) %copy-start.12) | copy-done | bytes 2097176
  112.2 3.9 %curvature.1 = (f32[8,128,128]{2,1,0:T(8,128)S(1)}, f32[8,128]{1,0:T(8,128)S(1)}) custom-call(f32[8,264,128]{2,1,0:T(8,128)S(1)} %all-to-all-done.1.got, f32[8,3,128,128]{3,2,1,0:T(8,128)} %all-to-all-done.got.first, f32[1024,128]{1,0:T(8,128)S(1)} %copy-done.24, bf16[1024,1024]{1,0:T(8,128)(2,1)S(1)} %get-tuple-element.24.f_high, ...), custom_call_target="tpu_custom_call" | custom-call | flops 1610612736 | bytes 12095488 | tf_op jit(solution)/shard_map/curvature/pallas_call | solution.py:30
  116.1 7.3 %collective-permute-done.9.ahead = f32[1,128,1024]{2,1,0:T(8,128)S(1)} collective-permute-done((f32[1,128,1024]{2,1,0:T(8,128)S(1)}, f32[1,128,1024]{2,1,0:T(8,128)S(1)}, u32[]{:S(2)}, u32[]{:S(2)}) %collective-permute-start.9) | collective-permute-done | bytes 524320 | tf_op jit(solution)/shard_map/ppermute | solution.py:399
  123.4 1.4 inner.1
  124.8 13.2 %all_to_all.20.got = f32[8,136,128]{2,1,0:T(8,128)S(1)} all-to-all(f32[8,136,128]{2,1,0:T(8,128)S(1)} %get-tuple-element.36), channel_id=1, replica_groups=mesh['planes_0'=4,'planes_1'=2,'planes_2'=2,'rows_0'=2,'rows_1'=4] {'row..., dimensions={0} | all-to-all | bytes 1114112 | tf_op jit(solution)/shard_map/all_to_all | solution.py:327
  138.6 6.6 %all-to-all-start.3 = ((f32[16,8,128]{2,1,0:T(8,128)}), f32[16,8,128]{2,1,0:T(8,128)S(1)}, u32[]{:S(2)}, u32[]{:S(2)}) async-start(f32[16,8,128]{2,1,0:T(8,128)} %broadcast_in_dim.14), calls=%async_computation.3 | async-start | bytes 131072 | tf_op jit(solution)/shard_map/all_to_all | solution.py:327
  145.2 1.6 %copy-done.4 = bf16[1024,1024]{1,0:T(8,128)(2,1)S(1)} copy-done((bf16[1024,1024]{1,0:T(8,128)(2,1)S(1)}, bf16[1024,1024]{1,0:T(8,128)(2,1)}, u32[]{:S(2)}) %copy-start.4) | copy-done | bytes 2097176
  146.8 1.0 copy-done.33
  149.6 1.4 all-to-all-done.3.sums
  151.0 1.0 copy-done.17
  152.1 1.0 copy-done.19
  153.1 1.2 last.1
  (67 shorter events, 9.7 us)
Async XLA Ops:
  0.6 1.0 copy-start.13
  1.7 1.0 copy-start.34
  2.7 1.0 copy-start.35
  3.8 1.0 copy-start.36
  7.9 1.4 copy-start.5
  9.3 1.3 copy-start.9
  10.6 8.4 %copy-start.14 = (f32[1,128,1024]{2,1,0:T(8,128)S(1)}, f32[1,128,1024]{2,1,0:T(8,128)}, u32[]{:S(2)}) copy-start(f32[1,128,1024]{2,1,0:T(8,128)} %estimate.5) | copy-start | bytes 1572868
  10.6 47.9 %all-to-all-start = ((f32[8,3,128,128]{3,2,1,0:T(8,128)}), f32[8,3,128,128]{3,2,1,0:T(8,128)}, u32[]{:S(2)}, u32[]{:S(2)}) async-start(f32[8,3,128,128]{3,2,1,0:T(8,128)} %get-tuple-element.20), calls=%async_computation | async-start | bytes 3145728 | tf_op jit(solution)/shard_map/all_to_all | solution.py:327
  19.1 25.6 %collective-permute-start = (f32[1,128,1024]{2,1,0:T(8,128)S(1)}, f32[1,128,1024]{2,1,0:T(8,128)S(1)}, u32[]{:S(2)}, u32[]{:S(2)}) collective-permute-start(f32[1,128,1024]{2,1,0:T(8,128)S(1)} %copy-done.14), channel_id=1, source_target_pairs={{0,8},{8,16},{16,24},{24,32},{32,40},{40,48},{48,56},{56,64},{64,7... | collective-permute-start | bytes 1572872 | tf_op jit(solution)/shard_map/ppermute | solution.py:362
  22.1 26.6 %collective-permute-start.1 = (f32[1,128,1024]{2,1,0:T(8,128)S(1)}, f32[1,128,1024]{2,1,0:T(8,128)}, u32[]{:S(2)}, u32[]{:S(2)}) collective-permute-start(f32[1,128,1024]{2,1,0:T(8,128)S(1)} %copy-done.14), channel_id=1, source_target_pairs={{8,0},{16,8},{24,16},{32,24},{40,32},{48,40},{56,48},{64,56},{72,6... | collective-permute-start | bytes 1572872 | tf_op jit(solution)/shard_map/ppermute | solution.py:363
  24.1 10.1 %collective-permute-start.2 = (f32[1,1,1024]{2,1,0:T(1,128)S(1)}, f32[1,1,1024]{2,1,0:T(1,128)S(1)}, u32[]{:S(2)}, u32[]{:S(2)}) collective-permute-start(f32[1,1,1024]{2,1,0:T(1,128)S(1)} %get-tuple-element.41), channel_id=1, source_target_pairs={{0,1},{1,2},{2,3},{3,4},{4,5},{5,6},{6,7},{8,9},{9,10},{10,11},{11... | collective-permute-start | bytes 12296 | tf_op jit(solution)/shard_map/ppermute | solution.py:365
  27.7 17.0 %collective-permute-start.3 = (f32[1,1,1024]{2,1,0:T(1,128)S(1)}, f32[1,1,1024]{2,1,0:T(1,128)S(1)}, u32[]{:S(2)}, u32[]{:S(2)}) collective-permute-start(f32[1,1,1024]{2,1,0:T(1,128)S(1)} %get-tuple-element.40), channel_id=1, source_target_pairs={{1,0},{2,1},{3,2},{4,3},{5,4},{6,5},{7,6},{9,8},{10,9},{11,10},{12... | collective-permute-start | bytes 12296 | tf_op jit(solution)/shard_map/ppermute | solution.py:366
  29.0 15.7 %collective-permute-start.4 = (f32[1,1,1024]{2,1,0:T(1,128)S(1)}, f32[1,1,1024]{2,1,0:T(1,128)S(1)}, u32[]{:S(2)}, u32[]{:S(2)}) collective-permute-start(f32[1,1,1024]{2,1,0:T(1,128)S(1)} %get-tuple-element.40), channel_id=1, source_target_pairs={{1,8},{2,9},{3,10},{4,11},{5,12},{6,13},{7,14},{9,16},{10,17},{11,... | collective-permute-start | bytes 12296 | tf_op jit(solution)/shard_map/ppermute | solution.py:367
  34.1 10.6 %collective-permute-start.5 = (f32[1,1,1024]{2,1,0:T(1,128)S(1)}, f32[1,1,1024]{2,1,0:T(1,128)S(1)}, u32[]{:S(2)}, u32[]{:S(2)}) collective-permute-start(f32[1,1,1024]{2,1,0:T(1,128)S(1)} %get-tuple-element.41), channel_id=1, source_target_pairs={{8,1},{9,2},{10,3},{11,4},{12,5},{13,6},{14,7},{16,9},{17,10},{18,... | collective-permute-start | bytes 12296 | tf_op jit(solution)/shard_map/ppermute | solution.py:368
  41.3 1.0 copy-start.27
  43.4 1.4 copy-start
  48.7 1.6 %copy-start.6 = (bf16[1024,1024]{1,0:T(8,128)(2,1)S(1)}, bf16[1024,1024]{1,0:T(8,128)(2,1)}, u32[]{:S(2)}) copy-start(bf16[1024,1024]{1,0:T(8,128)(2,1)} %copy-done.5) | copy-start | bytes 6291460
  50.3 1.6 %copy-start.10 = (bf16[1024,1024]{1,0:T(8,128)(2,1)S(1)}, bf16[1024,1024]{1,0:T(8,128)(2,1)}, u32[]{:S(2)}) copy-start(bf16[1024,1024]{1,0:T(8,128)(2,1)} %copy-done.9) | copy-start | bytes 6291460
  55.3 0.8 copy-start.21
  56.9 0.8 copy-start.28
  57.7 0.8 copy-start.30
  58.5 1.6 %copy-start.1 = (bf16[1024,1024]{1,0:T(8,128)(2,1)S(1)}, bf16[1024,1024]{1,0:T(8,128)(2,1)}, u32[]{:S(2)}) copy-start(bf16[1024,1024]{1,0:T(8,128)(2,1)} %copy-done) | copy-start | bytes 6291460
  60.1 1.6 %copy-start.7 = (bf16[1024,1024]{1,0:T(8,128)(2,1)S(1)}, bf16[1024,1024]{1,0:T(8,128)(2,1)}, u32[]{:S(2)}) copy-start(bf16[1024,1024]{1,0:T(8,128)(2,1)} %copy-done.5) | copy-start | bytes 6291460
  61.7 1.6 %copy-start.11 = (bf16[1024,1024]{1,0:T(8,128)(2,1)S(1)}, bf16[1024,1024]{1,0:T(8,128)(2,1)}, u32[]{:S(2)}) copy-start(bf16[1024,1024]{1,0:T(8,128)(2,1)} %copy-done.9) | copy-start | bytes 6291460
  63.3 1.0 copy-start.26
  68.8 1.1 copy-start.20
  70.6 23.5 %all-to-all-start.1 = ((f32[8,264,128]{2,1,0:T(8,128)}), f32[8,264,128]{2,1,0:T(8,128)S(1)}, u32[]{:S(2)}, u32[]{:S(2)}) async-start(f32[8,264,128]{2,1,0:T(8,128)} %copy-done.20), calls=%async_computation.1 | async-start | bytes 2162688 | tf_op jit(solution)/shard_map/all_to_all | solution.py:327
  83.3 4.9 %collective-permute-start.6 = (f32[1,1,1024]{2,1,0:T(1,128)S(1)}, f32[1,1,1024]{2,1,0:T(1,128)S(1)}, u32[]{:S(2)}, u32[]{:S(2)}) collective-permute-start(f32[1,1,1024]{2,1,0:T(1,128)S(1)} %get-tuple-element.39), channel_id=1, source_target_pairs={{0,1},{1,2},{2,3},{3,4},{4,5},{5,6},{6,7},{8,9},{9,10},{10,11},{11... | collective-permute-start | bytes 12296 | tf_op jit(solution)/shard_map/ppermute | solution.py:381
  86.7 5.0 %collective-permute-start.7 = (f32[1,1,1024]{2,1,0:T(1,128)S(1)}, f32[1,1,1024]{2,1,0:T(1,128)S(1)}, u32[]{:S(2)}, u32[]{:S(2)}) collective-permute-start(f32[1,1,1024]{2,1,0:T(1,128)S(1)} %get-tuple-element.38), channel_id=1, source_target_pairs={{1,0},{2,1},{3,2},{4,3},{5,4},{6,5},{7,6},{9,8},{10,9},{11,10},{12... | collective-permute-start | bytes 12296 | tf_op jit(solution)/shard_map/ppermute | solution.py:382
  94.2 1.6 %copy-start.2 = (bf16[1024,1024]{1,0:T(8,128)(2,1)S(1)}, bf16[1024,1024]{1,0:T(8,128)(2,1)}, u32[]{:S(2)}) copy-start(bf16[1024,1024]{1,0:T(8,128)(2,1)} %copy-done) | copy-start | bytes 6291460
  95.8 1.0 copy-start.22
  96.8 13.8 %copy-start.3 = (bf16[1024,1024]{1,0:T(8,128)(2,1)S(1)}, bf16[1024,1024]{1,0:T(8,128)(2,1)}, u32[]{:S(2)}) copy-start(bf16[1024,1024]{1,0:T(8,128)(2,1)} %copy-done) | copy-start | bytes 6291460
  96.8 13.8 %copy-start.8 = (bf16[1024,1024]{1,0:T(8,128)(2,1)S(1)}, bf16[1024,1024]{1,0:T(8,128)(2,1)}, u32[]{:S(2)}) copy-start(bf16[1024,1024]{1,0:T(8,128)(2,1)} %copy-done.5) | copy-start | bytes 6291460
  96.8 13.8 %copy-start.24 = (f32[1024,128]{1,0:T(8,128)S(1)}, f32[1024,128]{1,0:T(8,128)}, u32[]{:S(2)}) copy-start(f32[1024,128]{1,0:T(8,128)} %copy-done.23) | copy-start | bytes 1572868
  97.9 25.5 %copy-start.16 = (f32[1,128,1024]{2,1,0:T(8,128)}, f32[1,128,1024]{2,1,0:T(8,128)S(1)}, u32[]{:S(2)}) copy-start(f32[1,128,1024]{2,1,0:T(8,128)S(1)} %get-tuple-element.28.residual) | copy-start | bytes 1572868
  97.9 18.2 %collective-permute-start.8 = (f32[1,128,1024]{2,1,0:T(8,128)S(1)}, f32[1,128,1024]{2,1,0:T(8,128)S(1)}, u32[]{:S(2)}, u32[]{:S(2)}) collective-permute-start(f32[1,128,1024]{2,1,0:T(8,128)S(1)} %get-tuple-element.28.residual), channel_id=1, source_target_pairs={{0,8},{8,16},{16,24},{24,32},{32,40},{40,48},{48,56},{56,64},{64,7... | collective-permute-start | bytes 1572872 | tf_op jit(solution)/shard_map/ppermute | solution.py:398
  108.5 14.9 %collective-permute-start.9 = (f32[1,128,1024]{2,1,0:T(8,128)S(1)}, f32[1,128,1024]{2,1,0:T(8,128)S(1)}, u32[]{:S(2)}, u32[]{:S(2)}) collective-permute-start(f32[1,128,1024]{2,1,0:T(8,128)S(1)} %get-tuple-element.28.residual), channel_id=1, source_target_pairs={{8,0},{16,8},{24,16},{32,24},{40,32},{48,40},{56,48},{64,56},{72,6... | collective-permute-start | bytes 1572872 | tf_op jit(solution)/shard_map/ppermute | solution.py:399
  110.6 1.6 %copy-start.12 = (bf16[1024,1024]{1,0:T(8,128)(2,1)S(1)}, bf16[1024,1024]{1,0:T(8,128)(2,1)}, u32[]{:S(2)}) copy-start(bf16[1024,1024]{1,0:T(8,128)(2,1)} %copy-done.9) | copy-start | bytes 6291460
  112.2 11.2 %copy-start.29 = (f32[128,1024]{1,0:T(8,128)S(1)}, f32[128,1024]{1,0:T(8,128)}, u32[]{:S(2)}) copy-start(f32[128,1024]{1,0:T(8,128)} %copy-done.28) | copy-start | bytes 1572868
  112.2 11.2 %copy-start.31 = (f32[128,1024]{1,0:T(8,128)S(1)}, f32[128,1024]{1,0:T(8,128)}, u32[]{:S(2)}) copy-start(f32[128,1024]{1,0:T(8,128)} %copy-done.30) | copy-start | bytes 1572868
  124.8 13.2 %copy-start.32 = (f32[128,1024]{1,0:T(8,128)}, f32[128,1024]{1,0:T(8,128)S(1)}, u32[]{:S(2)}) copy-start(f32[128,1024]{1,0:T(8,128)S(1)} %get-tuple-element.37.reg) | copy-start | bytes 1572868
  138.6 12.4 %all-to-all-start.3 = ((f32[16,8,128]{2,1,0:T(8,128)}), f32[16,8,128]{2,1,0:T(8,128)S(1)}, u32[]{:S(2)}, u32[]{:S(2)}) async-start(f32[16,8,128]{2,1,0:T(8,128)} %broadcast_in_dim.14), calls=%async_computation.3 | async-start | bytes 131072 | tf_op jit(solution)/shard_map/all_to_all | solution.py:327
  145.2 1.6 %copy-start.4 = (bf16[1024,1024]{1,0:T(8,128)(2,1)S(1)}, bf16[1024,1024]{1,0:T(8,128)(2,1)}, u32[]{:S(2)}) copy-start(bf16[1024,1024]{1,0:T(8,128)(2,1)} %copy-done) | copy-start | bytes 6291460
  146.8 1.0 copy-start.33
  147.8 3.2 %copy-start.15 = (f32[1,128,1024]{2,1,0:T(8,128)S(1)}, f32[1,128,1024]{2,1,0:T(8,128)}, u32[]{:S(2)}) copy-start(f32[1,128,1024]{2,1,0:T(8,128)} %estimate.5) | copy-start | bytes 1572868
  148.8 0.8 copy-start.18
  151.0 1.0 copy-start.17
  152.1 1.0 copy-start.19
  (2 other events, 1.6 us)
where the time goes:
time: 156 us; the launch traced here: 154 us
  starting transfers between devices  62.5 us (40%)
  local copies, waits for them, and re-layouts  34.5 us (22%)
  waiting for transfers between devices  22.7 us (15%)
  Pallas kernels  20.4 us (13%)
  blocking collectives  13.2 us (8%)
    unnamed x74, local copies, waits for them, and re-layouts  33.1 us
    all_to_all x3, starting transfers between devices, across(): return lax.all_to_all(x, axes, split_axis=0, concat_axis=0, tiled=True)  26.9 us
    pallas_call x9, Pallas kernels, run(): pl.pallas_call(body, out_shape=tuple(outs), in_specs=[SMEM if a.dtype ==...  20.4 us
    all_to_all x1, blocking collectives, across(): return lax.all_to_all(x, axes, split_axis=0, concat_axis=0, tiled=True)  13.2 us
    ppermute x1, starting transfers between devices, shards(): behind = lax.ppermute(residual, PLANES, up)  10.6 us
    ppermute x1, waiting for transfers between devices, shards(): ahead = lax.ppermute(residual, PLANES, down)  7.33 us
    ppermute x1, starting transfers between devices, shards(): ahead_top = lax.ppermute(tail, ALL, diagonal_from_ahead)  7.06 us
    ppermute x1, waiting for transfers between devices, shards(): ahead = lax.ppermute(estimate, PLANES, down)  4 us
  transfers between devices with their start and end apart: 13, of which 7 were waited for; matrix products, arithmetic and copies ran while one was open for 1% of the time, Pallas kernels for 6%

commit v1 on v0

v1 whole, which is shorter than its diff:
```python
import math

import jax
import jax.numpy as jnp
from jax import lax
from jax.experimental import pallas as pl
from jax.experimental.pallas import tpu as pltpu
from jax.sharding import Mesh
from jax.sharding import PartitionSpec as P


PLANES = ("planes_0", "planes_1", "planes_2")
ROWS = ("rows_0", "rows_1")
N = 1024
R = 128
G = 8
HALO = R
EDGE = R + 8
REG = R + 16
HUBER_EDGE = 0.5
SMOOTHING = 0.3
F32 = jnp.float32
BF16 = jnp.bfloat16
VMEM = pl.BlockSpec(memory_space=pltpu.VMEM)
SMEM = pl.BlockSpec(memory_space=pltpu.SMEM)
ANY = pl.BlockSpec(memory_space=pl.ANY)
HBM = pl.BlockSpec(memory_space=pltpu.HBM)
DMA = pltpu.SemaphoreType.DMA
TABLE = pltpu.VMEM((4, 32, N), F32)
MATRIX = pltpu.VMEM((N, N), BF16)
CHUNK = 16


def shape(*dims, dtype=F32):
    return jax.ShapeDtypeStruct(dims, dtype)


def call(body, outs, flops, scratch=(), out_specs=None, aliases=None, limit=32):
    def place_of(a):
        if a.dtype == jnp.int32:
            return SMEM
        return ANY

    def launch(*args):
        size = sum(math.prod(a.shape) * a.dtype.itemsize for a in args)
        size += sum(math.prod(o.shape) * o.dtype.itemsize for o in outs)
        return pl.pallas_call(
            body,
            out_shape=tuple(outs),
            in_specs=[place_of(a) for a in args],
            out_specs=out_specs or tuple(VMEM for _ in outs),
            scratch_shapes=list(scratch),
            input_output_aliases=aliases or {},
            compiler_params=pltpu.CompilerParams(vmem_limit_bytes=limit << 20),
            cost_estimate=pl.CostEstimate(flops=flops, bytes_accessed=size, transcendentals=0),
        )(*args)

    return launch


def cos_sin(units):
    quarter = (units + 512) >> 10
    angle = (units - (quarter << 10)).astype(F32) * (math.pi / (2.0 * N))
    square = angle * angle
    sine = angle * (
        1.0 + square * (-1.0 / 6.0 + square * (1.0 / 120.0 + square * (-1.0 / 5040.0)))
    )
    cosine = 1.0 + square * (
        -0.5 + square * (1.0 / 24.0 + square * (-1.0 / 720.0 + square * (1.0 / 40320.0)))
    )
    odd = (quarter & 1) == 1
    cos_value = jnp.where(odd, sine, cosine)
    sin_value = jnp.where(odd, cosine, sine)
    cos_value = jnp.where(((quarter + 1) & 2) == 2, -cos_value, cos_value)
    sin_value = jnp.where((quarter & 2) == 2, -sin_value, sin_value)
    return cos_value, sin_value


def fill_table(table, samples):
    row = lax.broadcasted_iota(jnp.int32, (16, N), 0)
    lane = lax.broadcasted_iota(jnp.int32, (16, N), 1)
    if samples:
        shift = jnp.where(row < 5, row + 6, jnp.where(row < 10, row - 4, 0))
        value = lane
    else:
        shift = jnp.where(row < 5, row + 5, jnp.where(row < 10, row - 5, 0))
        value = 2 * lane + 1
    cos_bits, sin_bits = cos_sin((value << shift) & (4 * N - 1))
    norm = math.sqrt(2.0 / N)
    if samples:
        first = jnp.where(lane[:1] == 0, math.sqrt(1.0 / N), norm)
        fine = (cos_bits[10:11] * first, sin_bits[10:11] * first)
    else:
        fine = (jnp.full((1, N), norm, F32), jnp.zeros((1, N), F32))
    table[0, 0:1], table[1, 0:1] = jnp.ones((1, N), F32), jnp.zeros((1, N), F32)
    table[2, 0:1], table[3, 0:1] = fine
    for part in range(2):
        for bit in range(5):
            at = 5 * part + bit
            size = 1 << bit
            c, s = table[2 * part, 0:size], table[2 * part + 1, 0:size]
            cb, sb = cos_bits[at : at + 1], sin_bits[at : at + 1]
            table[2 * part, size : 2 * size] = c * cb - s * sb
            table[2 * part + 1, size : 2 * size] = s * cb + c * sb


def split(x):
    high = x.astype(BF16)
    low = (x - high.astype(F32)).astype(BF16)
    return high, low


def build(table, high, low, rows, lanes, first_row=None):
    for a in range(rows.start // 32, rows.stop // 32):
        value = table[0, a : a + 1, lanes] * table[2, :, lanes]
        value -= table[1, a : a + 1, lanes] * table[3, :, lanes]
        if first_row is not None and a == 0:
            row = lax.broadcasted_iota(jnp.int32, value.shape, 0)
            value = jnp.where(row == 0, first_row, value)
        block = slice(32 * a, 32 * a + 32)
        high[block, lanes], low[block, lanes] = split(value)


WHOLE = slice(0, N)


def build_samples(table, high, low, rows=WHOLE, lanes=WHOLE):
    build(table, high, low, rows, lanes)


def build_freqs(table, high, low, rows=WHOLE, lanes=WHOLE):
    build(table, high, low, rows, lanes, math.sqrt(1.0 / N))


def start(source, target, sem):
    copy = pltpu.make_async_copy(source, target, sem)
    copy.start()
    return copy


def dot(a, b):
    return jnp.dot(a, b, preferred_element_type=F32)


def stacked_times(stack, rows, high, low, columns):
    both = dot(stack[0 : 2 * rows, :], high[:, columns])
    return both[:rows] + both[rows:] + dot(stack[0:rows, :], low[:, columns])


def matrix_times(high, low, rows, pair, width, offset=0):
    both = dot(high[rows, :], pair[:, offset : offset + 2 * width])
    return both[:, :width] + both[:, width:] + dot(low[rows, :], pair[:, offset : offset + width])


def first_kernel(
    observed, estimate, spectrum, sent,
    table_v, observed_v, estimate_v, spectrum_v, sent_v, high, low, stack, sems,
):
    copies = [
        start(observed.at[0], observed_v, sems.at[1]),
        start(estimate.at[0], estimate_v, sems.at[2]),
        start(spectrum.at[0], spectrum_v, sems.at[3]),
    ]
    fill_table(table_v, True)
    copies[0].wait()
    stack[0:R, :], stack[2 * R : 3 * R, :] = split(observed_v[...])
    copies[1].wait()
    stack[R : 2 * R, :], stack[3 * R : 4 * R, :] = split(estimate_v[...])
    copies[2].wait()
    out_copies = []
    for d in range(G // 2):
        columns = slice(256 * d, 256 * d + 256)
        build_samples(table_v, high, low, WHOLE, columns)
        out = stacked_times(stack, 2 * R, high, low, columns)
        for h in range(2):
            lanes = slice(128 * h, 128 * h + 128)
            e = 2 * d + h
            sent_v[e, 0] = spectrum_v[:, 128 * e : 128 * e + 128]
            sent_v[e, 1] = out[:R, lanes]
            sent_v[e, 2] = out[R:, lanes]
        out_copies.append(
            start(sent_v.at[2 * d : 2 * d + 2], sent.at[2 * d : 2 * d + 2], sems.at[4 + d])
        )
    for copy in out_copies:
        copy.wait()


def left(x):
    return pltpu.roll(x, N - 1, 1)


def weight_of(plane, row, value, last):
    column = jnp.where(last, 0.0, left(value) - value)
    square = plane * plane + row * row + column * column
    return 1.0 / jnp.maximum(jnp.sqrt(square), HUBER_EDGE)


def divergence(value, ahead_plane, behind_plane, ahead_row, behind_row, w_plane, w_back, w_row, w_row_back, w_col):
    flux_col = w_col * (left(value) - value)
    total = w_back * (value - behind_plane) - w_plane * (ahead_plane - value)
    total += w_row_back * (value - behind_row) - w_row * (ahead_row - value)
    total += pltpu.roll(flux_col, 1, 1) - flux_col
    return SMOOTHING * total


def as_tile(row):
    return jnp.concatenate([row[:, 128 * i : 128 * i + 128] for i in range(8)], axis=0)


def weights_kernel(
    place, estimate, behind, ahead, from_above, from_below,
    reg, reg_sent, reg_rows, w_all, w_back_all, w_top,
    table_v, ext, ext_back, ahead_v, above_v, below_v, ext_w, high, low, stack, sems,
):
    copies = [
        start(estimate.at[0], ext.at[8 : 8 + R], sems.at[1]),
        start(behind.at[0], ext_back.at[0:R], sems.at[2]),
        start(ahead.at[0], ahead_v, sems.at[3]),
        start(from_above, above_v, sems.at[4]),
        start(from_below, below_v, sems.at[5]),
    ]
    fill_table(table_v, True)
    plane, row = place[0], place[1]
    ok_plane = jnp.where(plane < 15, 1.0, 0.0)
    ok_back = jnp.where(plane > 0, 1.0, 0.0)
    ok_top = jnp.where(row > 0, 1.0, 0.0)
    for copy in copies:
        copy.wait()
    ext[7:8, :] = above_v[0]
    ext[8 + R : 9 + R, :] = jnp.where(row < G - 1, below_v[0], ext[7 + R : 8 + R, :])
    ext_back[R : R + 1, :] = jnp.where(row < G - 1, below_v[1], ext_back[R - 1 : R, :])
    last1 = lax.broadcasted_iota(jnp.int32, (1, N), 1) == N - 1
    edge = ext[7:8, :]
    w_edge = weight_of(
        (above_v[1] - edge) * ok_plane, (ext[8:9, :] - edge) * ok_top, edge, last1
    ) * ok_top
    w_top[...] = w_edge
    ext_w[7:8, :] = w_edge
    last = lax.broadcasted_iota(jnp.int32, (CHUNK, N), 1) == N - 1
    for c in range(0, R, CHUNK):
        value = ext[8 + c : 8 + c + CHUNK, :]
        back = ext_back[c : c + CHUNK, :]
        w = weight_of(
            (ahead_v[c : c + CHUNK, :] - value) * ok_plane,
            ext[9 + c : 9 + c + CHUNK, :] - value,
            value,
            last,
        )
        ext_w[8 + c : 8 + c + CHUNK, :] = w
        w_all[c : c + CHUNK, :] = w
        w_back_all[c : c + CHUNK, :] = weight_of(
            (value - back) * ok_back, ext_back[1 + c : 1 + c + CHUNK, :] - back, back, last
        ) * ok_back
    for c in range(0, R, CHUNK):
        w = ext_w[8 + c : 8 + c + CHUNK, :]
        out = divergence(
            ext[8 + c : 8 + c + CHUNK, :],
            ahead_v[c : c + CHUNK, :],
            ext_back[c : c + CHUNK, :],
            ext[9 + c : 9 + c + CHUNK, :],
            ext[7 + c : 7 + c + CHUNK, :],
            w * ok_plane,
            w_back_all[c : c + CHUNK, :],
            w,
            ext_w[7 + c : 7 + c + CHUNK, :],
            jnp.where(last, 0.0, w),
        )
        reg[c : c + CHUNK, :] = out
        stack[c : c + CHUNK, :], stack[R + c : R + c + CHUNK, :] = split(out)
    reg_rows[0] = as_tile(reg[0:1, :])
    reg_rows[1] = as_tile(reg[R - 1 : R, :])
    for d in range(G // 2):
        columns = slice(256 * d, 256 * d + 256)
        build_samples(table_v, high, low, WHOLE, columns)
        out = stacked_times(stack, R, high, low, columns)
        reg_sent[2 * d] = out[:, :128]
        reg_sent[2 * d + 1] = out[:, 128:]


def middle_kernel(
    place, got, reg_sent, reg_rows, sent, spectral,
    freq_v, sample_v, got_v, rows_v, sent_v, f_high, f_low, s_high, s_low, pair, sems,
):
    copies = [
        start(got, got_v, sems.at[1]),
        start(reg_sent, sent_v.at[:, REG:], sems.at[3]),
        start(reg_rows, rows_v, sems.at[4]),
    ]
    row = place[1]
    fill_table(freq_v, False)
    fill_table(sample_v, True)
    copies[0].wait()
    for d in range(G):
        rows = slice(R * d, R * d + R)
        pair[rows, 0:128], pair[rows, 256:384] = split(got_v[d, 1])
        pair[rows, 128:256], pair[rows, 384:512] = split(got_v[d, 2])
    for m in range(4):
        rows = slice(256 * m, 256 * m + 256)
        build_freqs(freq_v, f_high, f_low, rows)
        out = matrix_times(f_high, f_low, rows, pair, 256)
        gain = jnp.concatenate([got_v[2 * m, 0], got_v[2 * m + 1, 0]], axis=0)
        value = gain * (out[:, :128] - gain * out[:, 128:])
        spectral[rows, :] = value
        pair[rows, 512:640], pair[rows, 640:768] = split(value)
    copies[2].wait()
    for d in range(G):
        sent_v[d, HALO:EDGE] = jnp.zeros((8, 128), F32)
        sent_v[d, EDGE:REG] = jnp.where(
            row == d - 1, rows_v[1], jnp.where(row == d + 1, rows_v[0], 0.0)
        )
    copies[1].wait()
    out_copies = []
    for m in range(4):
        rows = slice(256 * m, 256 * m + 256)
        build_samples(sample_v, s_high, s_low, rows)
        out = matrix_times(s_high, s_low, rows, pair, 128, 512)
        for h in range(2):
            d = 2 * m + h
            block = out[R * h : R * h + R]
            sent_v[d, 0:R] = block
            if d + 1 < G:
                sent_v[d + 1, HALO : HALO + 1] = block[R - 1 : R]
            if d > 0:
                sent_v[d - 1, HALO + 1 : HALO + 2] = block[0:1]
                out_copies.append(start(sent_v.at[d - 1], sent.at[d - 1], sems.at[5 + d - 1]))
    out_copies.append(start(sent_v.at[G - 1], sent.at[G - 1], sems.at[5 + G - 1]))
    for copy in out_copies:
        copy.wait()


def residual_kernel(
    place, got, reg, residual, edges,
    table_v, got_v, rows_v, reg_v, f_high, f_low, stack, sems,
):
    copies = [
        start(got.at[:, 0:REG], got_v, sems.at[1]),
        start(reg, reg_v, sems.at[2]),
    ]
    row = place[1]
    fill_table(table_v, False)
    for copy in copies:
        copy.wait()
    above = got_v[jnp.maximum(row - 1, 0), EDGE:REG, :]
    below = got_v[jnp.minimum(row + 1, G - 1), EDGE:REG, :]
    for i in range(G):
        rows_v[0:1, 128 * i : 128 * i + 128] = above[i : i + 1]
        rows_v[1:2, 128 * i : 128 * i + 128] = below[i : i + 1]
    rows = R + 16
    for d in range(G):
        lanes = slice(128 * d, 128 * d + 128)
        stack[0:rows, lanes], stack[rows : 2 * rows, lanes] = split(got_v[d])
    for d in range(G // 2):
        lanes = slice(256 * d, 256 * d + 256)
        build_freqs(table_v, f_high, f_low, WHOLE, lanes)
        out = stacked_times(stack, rows, f_high, f_low, lanes)
        residual[0, :, lanes] = out[:R] - reg_v[:, lanes]
        edges[0:2, lanes] = out[R : R + 2] - rows_v[0:2, lanes]


def curvature_kernel(
    got, first, spectral, sent, total,
    freq_v, sample_v, got_v, gain_v, spectral_v, sent_v, f_high, f_low, s_high, s_low, pair, sems,
):
    copies = [
        start(got.at[:, REG:], got_v, sems.at[1]),
        start(first.at[:, 0], gain_v, sems.at[3]),
        start(spectral, spectral_v, sems.at[4]),
    ]
    fill_table(freq_v, False)
    fill_table(sample_v, True)
    for copy in copies:
        copy.wait()
    for d in range(G):
        rows = slice(R * d, R * d + R)
        pair[rows, 0:128], pair[rows, 128:256] = split(got_v[d])
    acc = jnp.zeros((8, 128), F32)
    for m in range(4):
        rows = slice(256 * m, 256 * m + 256)
        build_freqs(freq_v, f_high, f_low, rows)
        out = spectral_v[rows, :] - matrix_times(f_high, f_low, rows, pair, 128)
        gain = jnp.concatenate([gain_v[2 * m], gain_v[2 * m + 1]], axis=0)
        scaled = gain * gain * out
        acc += jnp.sum((scaled * out).reshape(32, 8, 128), axis=0)
        pair[rows, 256:384], pair[rows, 384:512] = split(scaled)
    total[...] = acc
    out_copies = []
    for m in range(4):
        rows = slice(256 * m, 256 * m + 256)
        build_samples(sample_v, s_high, s_low, rows)
        out = matrix_times(s_high, s_low, rows, pair, 128, 256)
        sent_v[2 * m] = out[:R]
        sent_v[2 * m + 1] = out[R:]
        out_copies.append(
            start(sent_v.at[2 * m : 2 * m + 2], sent.at[2 * m : 2 * m + 2, 0:R], sems.at[5 + m])
        )
    for copy in out_copies:
        copy.wait()


def load_field(residual, edges, w_all, ext, ext_w, edges_v, sems):
    copies = [
        start(residual.at[0], ext.at[8 : 8 + R], sems.at[0]),
        start(edges, edges_v, sems.at[1]),
        start(w_all, ext_w.at[8 : 8 + R], sems.at[2]),
    ]
    return copies


def finish_field(place, copies, ext, edges_v):
    for copy in copies:
        copy.wait()
    row = place[1]
    ext[7:8, :] = edges_v[0:1, :]
    ext[8 + R : 9 + R, :] = jnp.where(row < G - 1, edges_v[1:2, :], ext[7 + R : 8 + R, :])


def product_kernel(
    place, residual, ahead, edges, w_all, total, half, sent,
    ext, ext_w, edges_v, ahead_v, total_v, tile_v, sems,
):
    copies = load_field(residual, edges, w_all, ext, ext_w, edges_v, sems)
    copies.append(start(ahead.at[0], ahead_v, sems.at[3]))
    copies.append(start(total, total_v, sems.at[4]))
    ok_plane = jnp.where(place[0] < 15, 1.0, 0.0)
    finish_field(place, copies, ext, edges_v)
    last = lax.broadcasted_iota(jnp.int32, (CHUNK, N), 1) == N - 1
    norm = jnp.zeros((8, N), F32)
    product = jnp.zeros((8, N), F32)
    for c in range(0, R, CHUNK):
        value = ext[8 + c : 8 + c + CHUNK, :]
        plane = (ahead_v[c : c + CHUNK, :] - value) * ok_plane
        row = ext[9 + c : 9 + c + CHUNK, :] - value
        column = jnp.where(last, 0.0, left(value) - value)
        cross = ext_w[8 + c : 8 + c + CHUNK, :] * (plane * plane + row * row + column * column)
        square = value * value
        norm += square[:8] + square[8:]
        product += cross[:8] + cross[8:]
    norm = jnp.sum(as_tile(jnp.sum(norm, axis=0, keepdims=True)), axis=0, keepdims=True)
    product = as_tile(SMOOTHING * jnp.sum(product, axis=0, keepdims=True)) + total_v[...]
    product = jnp.sum(product, axis=0, keepdims=True)
    tile_v[...] = jnp.concatenate([norm, product, jnp.zeros((6, 128), F32)], axis=0)
    out_copies = [start(tile_v, sent.at[d, R:], sems.at[5 + d]) for d in range(G)]
    for copy in out_copies:
        copy.wait()


def inner_kernel(
    place, residual, behind, ahead, edges, w_all, w_back_all, w_top, reg,
    ext, ext_w, edges_v, behind_v, ahead_v, back_v, sems,
):
    copies = load_field(residual, edges, w_all, ext, ext_w, edges_v, sems)
    copies += [
        start(behind.at[0], behind_v, sems.at[3]),
        start(ahead.at[0], ahead_v, sems.at[4]),
        start(w_back_all, back_v, sems.at[5]),
        start(w_top, ext_w.at[7:8], sems.at[6]),
    ]
    ok_plane = jnp.where(place[0] < 15, 1.0, 0.0)
    finish_field(place, copies, ext, edges_v)
    last = lax.broadcasted_iota(jnp.int32, (CHUNK, N), 1) == N - 1
    for c in range(0, R, CHUNK):
        w = ext_w[8 + c : 8 + c + CHUNK, :]
        reg[c : c + CHUNK, :] = divergence(
            ext[8 + c : 8 + c + CHUNK, :],
            ahead_v[c : c + CHUNK, :],
            behind_v[c : c + CHUNK, :],
            ext[9 + c : 9 + c + CHUNK, :],
            ext[7 + c : 7 + c + CHUNK, :],
            w * ok_plane,
            back_v[c : c + CHUNK, :],
            w,
            ext_w[7 + c : 7 + c + CHUNK, :],
            jnp.where(last, 0.0, w),
        )


def last_kernel(
    sums, got, reg, estimate, residual, restored, final,
    table_v, sums_v, got_v, reg_v, estimate_v, residual_v, restored_v, final_v,
    f_high, f_low, stack, sems,
):
    arrays = (
        (got.at[:, 0:R], got_v), (sums, sums_v), (reg, reg_v),
        (residual.at[0], residual_v), (estimate.at[0], estimate_v),
    )
    copies = [start(a, b, sems.at[i]) for i, (a, b) in enumerate(arrays)]
    fill_table(table_v, False)
    copies[0].wait()
    for d in range(G):
        lanes = slice(128 * d, 128 * d + 128)
        stack[0:R, lanes], stack[R : 2 * R, lanes] = split(got_v[d])
    for copy in copies[1:]:
        copy.wait()
    tile = jnp.sum(sums_v[...], axis=0)
    norm = jnp.sum(tile[0:1, :], axis=1, keepdims=True)
    product = jnp.sum(tile[1:2, :], axis=1, keepdims=True)
    step = norm / product
    restored_v[...] = estimate_v[...] + step * residual_v[...]
    out_copies = [start(restored_v, restored.at[0], sems.at[6])]
    for d in range(G // 2):
        lanes = slice(256 * d, 256 * d + 256)
        build_freqs(table_v, f_high, f_low, WHOLE, lanes)
        image = stacked_times(stack, R, f_high, f_low, lanes) + reg_v[:, lanes]
        final_v[:, lanes] = residual_v[:, lanes] - step * image
        out_copies.append(start(final_v.at[:, lanes], final.at[0, :, lanes], sems.at[7 + d]))
    for copy in out_copies:
        copy.wait()


def across(x, axes):
    return lax.all_to_all(x, axes, split_axis=0, concat_axis=0, tiled=True)


def field(rows=R):
    return pltpu.VMEM((rows, N), F32)


def step(observed, estimate, spectrum):
    planes, groups = 16, G
    place = jnp.stack([lax.axis_index(PLANES), lax.axis_index(ROWS)]).astype(jnp.int32)
    up = [(i, i + 1) for i in range(planes - 1)]
    down = [(i + 1, i) for i in range(planes - 1)]
    row_up = [(i, i + 1) for i in range(groups - 1)]
    row_down = [(i + 1, i) for i in range(groups - 1)]
    big = 2 * N * N * R
    block = shape(R, N)

    behind = lax.ppermute(estimate, PLANES, up)
    ahead = lax.ppermute(estimate, PLANES, down)
    sent = call(
        first_kernel,
        (shape(G, 3, R, 128),),
        6 * big,
        (TABLE, field(), field(), field(), pltpu.VMEM((G, 3, R, 128), F32), MATRIX, MATRIX,
         pltpu.VMEM((4 * R, N), BF16), DMA((8,))),
        (ANY,), limit=60,
    )(observed, estimate, spectrum)[0]
    first = across(sent, ROWS)

    tails = jnp.concatenate([estimate[:, R - 1 :], ahead[:, R - 1 :]], axis=0)
    heads = jnp.concatenate([estimate[:, :1], behind[:, :1]], axis=0)
    from_above = lax.ppermute(tails, ROWS, row_up)
    from_below = lax.ppermute(heads, ROWS, row_down)
    reg, reg_sent, reg_rows, w_all, w_back, w_top = call(
        weights_kernel,
        (block, shape(G, R, 128), shape(2, 8, 128), block, block, shape(1, N)),
        3 * big,
        (TABLE, field(R + 16), field(R + 8), field(), pltpu.VMEM((2, 1, N), F32),
         pltpu.VMEM((2, 1, N), F32), field(R + 16), MATRIX, MATRIX,
         pltpu.VMEM((2 * R, N), BF16), DMA((6,))),
    )(place, estimate, behind, ahead, from_above, from_below)

    sent, spectral = call(
        middle_kernel,
        (shape(G, REG + R, 128), shape(N, 128)),
        9 * big,
        (TABLE, TABLE, pltpu.VMEM((G, 3, R, 128), F32), pltpu.VMEM((2, 8, 128), F32),
         pltpu.VMEM((G, REG + R, 128), F32), MATRIX, MATRIX, MATRIX, MATRIX,
         pltpu.VMEM((N, 768), BF16), DMA((13,))),
        (ANY, VMEM),
    )(place, first, reg_sent, reg_rows)
    second = across(sent, ROWS)

    residual, edges = call(
        residual_kernel,
        (shape(1, R, N), shape(8, N)),
        3 * big,
        (TABLE, pltpu.VMEM((G, REG, 128), F32), field(8), field(), MATRIX, MATRIX,
         pltpu.VMEM((2 * R + 32, N), BF16), DMA((3,))),
    )(place, second, reg)
    ahead = lax.ppermute(residual, PLANES, down)
    half_sent, total = call(
        curvature_kernel,
        (shape(G, R + 8, 128), shape(8, 128)),
        6 * big,
        (TABLE, TABLE, pltpu.VMEM((G, R, 128), F32), pltpu.VMEM((G, R, 128), F32),
         pltpu.VMEM((N, 128), F32), pltpu.VMEM((G, R, 128), F32), MATRIX, MATRIX, MATRIX, MATRIX,
         pltpu.VMEM((N, 512), BF16), DMA((9,))),
        (ANY, VMEM),
    )(second, first, spectral)
    sent = call(
        product_kernel,
        (shape(G, R + 8, 128),),
        big // 16,
        (field(R + 16), field(R + 16), field(8), field(), pltpu.VMEM((8, 128), F32),
         pltpu.VMEM((8, 128), F32), DMA((13,))),
        (ANY,),
        {6: 0},
    )(place, residual, ahead, edges, w_all, total, half_sent)[0]
    third = across(sent, ROWS)

    late, _ = lax.optimization_barrier((residual, ahead))
    behind = lax.ppermute(late, PLANES, up)
    reg_residual = call(
        inner_kernel,
        (block,),
        big // 16,
        (field(R + 16), field(R + 16), field(8), field(), field(), field(), DMA((7,))),
    )(place, residual, behind, ahead, edges, w_all, w_back, w_top)[0]

    tile = jnp.sum(third[:, R:], axis=0)
    sums = across(jnp.broadcast_to(tile[None], (planes, 8, 128)), PLANES)
    return call(
        last_kernel,
        (shape(1, R, N), shape(1, R, N)),
        3 * big,
        (TABLE, pltpu.VMEM((16, 8, 128), F32), pltpu.VMEM((G, R, 128), F32), field(), field(),
         field(), field(), field(), MATRIX, MATRIX, pltpu.VMEM((2 * R, N), BF16), DMA((11,))),
        (ANY, ANY),
    )(sums, third, reg_residual, estimate, residual)


def solution(mesh):
    finer = Mesh(
        mesh.devices.reshape(4, 2, 2, 2, 4),
        ("planes_0", "planes_1", "planes_2", "rows_0", "rows_1"),
    )
    spec = P(PLANES, ROWS, None)
    return jax.shard_map(
        step,
        mesh=finer,
        in_specs=(spec, spec, spec),
        out_specs=(spec, spec),
        check_vma=False,
    )
```

time: 156 us -> 141 us (0.904)
  starting transfers between devices: 62.5 us -> 33.1 us
  local copies, waits for them, and re-layouts: 34.5 us -> 8.79 us
  waiting for transfers between devices: 22.7 us -> 47.8 us
  blocking collectives: 13.2 us -> 21.7 us
  Pallas kernels: 20.4 us -> 27.4 us
    unnamed x74 -> x24, local copies, waits for them, and re-layouts: 33.1 us -> 8.13 us
    ppermute x10 -> x6, starting transfers between devices: 35.6 us -> 14.1 us  [the longest x1 3.37 us: step(): from_above = lax.ppermute(tails, ROWS, row_up)]
    ppermute x10 -> x6, waiting for transfers between devices: 18.8 us -> 37.5 us  [the longest x1 23.9 us: step(): ahead = lax.ppermute(estimate, PLANES, down)]
    all_to_all x1, blocking collectives: 13.2 us -> 21.7 us  [across(): return lax.all_to_all(x, axes, split_axis=0, concat_axis=0, tiled=True)]
    all_to_all x3, starting transfers between devices: 26.9 us -> 19 us  [across(): return lax.all_to_all(x, axes, split_axis=0, concat_axis=0, tiled=True)]
    pallas_call x9 -> x8, Pallas kernels: 20.4 us -> 27.4 us  [launch(): pl.pallas_call(body, out_shape=tuple(outs), in_specs=[place_of(a) for a i...]
    all_to_all x3, waiting for transfers between devices: 3.87 us -> 10.3 us  [across(): return lax.all_to_all(x, axes, split_axis=0, concat_axis=0, tiled=True)]
  transfers between devices with their start and end apart: 13 -> 9, of which waited for: 7 -> 5; matrix products, arithmetic and copies ran while one was open for 1% -> 1% of each run, Pallas kernels for 6% -> 7%
where the time goes in v1:
time: 141 us; the launch traced here: 140 us
  waiting for transfers between devices  47.8 us (34%)
  starting transfers between devices  33.1 us (23%)
  Pallas kernels  27.4 us (19%)
  blocking collectives  21.7 us (15%)
  local copies, waits for them, and re-layouts  8.79 us (6%)
    pallas_call x8, Pallas kernels, launch(): pl.pallas_call(body, out_shape=tuple(outs), in_specs=[place_of(a) for a i...  27.4 us
    ppermute x1, waiting for transfers between devices, step(): ahead = lax.ppermute(estimate, PLANES, down)  23.9 us
    all_to_all x1, blocking collectives, across(): return lax.all_to_all(x, axes, split_axis=0, concat_axis=0, tiled=True)  21.7 us
    all_to_all x3, starting transfers between devices, across(): return lax.all_to_all(x, axes, split_axis=0, concat_axis=0, tiled=True)  19 us
    ppermute x1, waiting for transfers between devices, step(): ahead = lax.ppermute(residual, PLANES, down)  10.5 us
    all_to_all x3, waiting for transfers between devices, across(): return lax.all_to_all(x, axes, split_axis=0, concat_axis=0, tiled=True)  10.3 us
    unnamed x24, local copies, waits for them, and re-layouts  8.13 us
    ppermute x1, starting transfers between devices, step(): from_above = lax.ppermute(tails, ROWS, row_up)  3.37 us
  transfers between devices with their start and end apart: 9, of which 5 were waited for; matrix products, arithmetic and copies ran while one was open for 1% of the time, Pallas kernels for 7%

profile of v1, /device:TPU:1, one launch (start us, length us, event | category | flops | bytes accessed | tf_op | source)
XLA Modules:
  0.0 139.8 jit_solution(17088854537906770980)
XLA Ops:
  0.6 4.3 %shard_map.50 = f32[8,3,128,128]{3,2,1,0:T(8,128)} custom-call(f32[1,128,1024]{2,1,0:T(8,128)} %observed.1, f32[1,128,1024]{2,1,0:T(8,128)} %estimate.5, f32[1,128,1024]{2,1,0:T(8,128)} %spectrum.1), custom_call_target="tpu_custom_call" | custom-call | flops 1610612736 | bytes 3145728 | tf_op jit(solution)/shard_map/pallas_call | solution.py:47
  4.9 0.0 copy-start.4
  4.9 8.4 %all-to-all-start = ((f32[8,3,128,128]{3,2,1,0:T(8,128)}), f32[8,3,128,128]{3,2,1,0:T(8,128)S(1)}, u32[]{:S(2)}, u32[]{:S(2)}) async-start(f32[8,3,128,128]{3,2,1,0:T(8,128)} %shard_map.50), calls=%async_computation | async-start | bytes 3145728 | tf_op jit(solution)/shard_map/all_to_all | solution.py:511
  13.4 0.0 copy-done.4
  13.4 2.9 %collective-permute-start.1 = (f32[1,128,1024]{2,1,0:T(8,128)S(1)}, f32[1,128,1024]{2,1,0:T(8,128)S(1)}, u32[]{:S(2)}, u32[]{:S(2)}) collective-permute-start(f32[1,128,1024]{2,1,0:T(8,128)S(1)} %copy-done.4), channel_id=1, source_target_pairs={{8,0},{16,8},{24,16},{32,24},{40,32},{48,40},{56,48},{64,56},{72,6... | collective-permute-start | bytes 1572872 | tf_op jit(solution)/shard_map/ppermute | solution.py:529
  16.3 2.7 %collective-permute-start = (f32[1,128,1024]{2,1,0:T(8,128)S(1)}, f32[1,128,1024]{2,1,0:T(8,128)S(1)}, u32[]{:S(2)}, u32[]{:S(2)}) collective-permute-start(f32[1,128,1024]{2,1,0:T(8,128)S(1)} %copy-done.4), channel_id=1, source_target_pairs={{0,8},{8,16},{16,24},{24,32},{32,40},{40,48},{48,56},{56,64},{64,7... | collective-permute-start | bytes 1572872 | tf_op jit(solution)/shard_map/ppermute | solution.py:528
  19.0 23.9 %collective-permute-done.1.ahead = f32[1,128,1024]{2,1,0:T(8,128)S(1)} collective-permute-done((f32[1,128,1024]{2,1,0:T(8,128)S(1)}, f32[1,128,1024]{2,1,0:T(8,128)S(1)}, u32[]{:S(2)}, u32[]{:S(2)}) %collective-permute-start.1) | collective-permute-done | bytes 524320 | tf_op jit(solution)/shard_map/ppermute | solution.py:529
  43.0 3.4 %collective-permute-start.2 = (f32[2,1,1024]{2,1,0:T(1,128)S(1)}, f32[2,1,1024]{2,1,0:T(1,128)S(1)}, u32[]{:S(2)}, u32[]{:S(2)}) collective-permute-start(f32[2,1,1024]{2,1,0:T(1,128)S(1)} %pad_maximum_fusion), channel_id=1, source_target_pairs={{0,1},{1,2},{2,3},{3,4},{4,5},{5,6},{6,7},{8,9},{9,10},{10,11},{11... | collective-permute-start | bytes 24584 | tf_op jit(solution)/shard_map/ppermute | solution.py:542
  46.3 0.0 collective-permute-done.behind
  46.4 0.0 copy-start.6
  46.4 0.8 copy-done.6
  47.2 1.3 collective-permute-start.3
  48.5 0.1 pad_add_fusion.place
  48.6 0.0 collective-permute-done.2.from_above
  48.6 3.0 %collective-permute-done.3.from_below = f32[2,1,1024]{2,1,0:T(1,128)S(1)} collective-permute-done((f32[2,1,1024]{2,1,0:T(1,128)S(1)}, f32[2,1,1024]{2,1,0:T(1,128)S(1)}, u32[]{:S(2)}, u32[]{:S(2)}) %collective-permute-start.3) | collective-permute-done | bytes 8224 | tf_op jit(solution)/shard_map/ppermute | solution.py:543
  51.6 0.0 copy-start.7
  51.6 1.0 copy-done.7
  52.6 3.8 %shard_map.51 = (f32[128,1024]{1,0:T(8,128)S(1)}, f32[8,128,128]{2,1,0:T(8,128)S(1)}, f32[2,8,128]{2,1,0:T(8,128)S(1)}, f32[128,1024]{1,0:T(8,128)S(1)}, f32[128,1024]{1,0:T(8,128)S(1)}, /*index=5*/f32[1,1024]{1,0:T(1,128)S(1)}) custom-call(s32[2]{0:T(128)S(1)} %pad_add_fusion.place, f32[1,128,1024]{2,1,0:T(8,128)S(1)} %copy-done.4, ...), custom_call_target="tpu_custom_call" | custom-call | flops 805306368 | bytes 3698696 | tf_op jit(solution)/shard_map/pallas_call | solution.py:47
  56.4 0.0 copy-start
  56.4 0.8 copy-done
  57.2 0.0 copy-start.8
  57.2 0.8 copy-done.8
  58.0 0.8 copy-done.10
  58.8 0.0 all-to-all-done.got.first
  58.8 1.0 copy-done.11
  59.8 6.7 %shard_map.52 = (f32[8,272,128]{2,1,0:T(8,128)S(1)}, f32[1024,128]{1,0:T(8,128)S(1)}) custom-call(s32[2]{0:T(128)S(1)} %pad_add_fusion.place, f32[8,3,128,128]{3,2,1,0:T(8,128)S(1)} %all-to-all-done.got.first, f32[8,128,128]{2,1,0:T(8,128)S(1)} %copy-done.11, f32[2,8,128]{2,1,0:T(8,128)S(1)} %get-tuple-element.16.reg_rows), custom_call_target="tpu_custom_call" | custom-call | flops 2415919104 | bytes 3743752 | tf_op jit(solution)/shard_map/pallas_call | solution.py:47
  66.5 0.0 copy-start.9
  66.5 21.7 %all_to_all.20.got = f32[8,272,128]{2,1,0:T(8,128)S(1)} all-to-all(f32[8,272,128]{2,1,0:T(8,128)S(1)} %get-tuple-element.17), channel_id=1, replica_groups=mesh['planes_0'=4,'planes_1'=2,'planes_2'=2,'rows_0'=2,'rows_1'=4] {'row..., dimensions={0} | all-to-all | bytes 2228224 | tf_op jit(solution)/shard_map/all_to_all | solution.py:511
  88.2 0.0 copy-done.9
  88.2 2.4 %shard_map.53 = (f32[1,128,1024]{2,1,0:T(8,128)S(1)}, f32[8,1024]{1,0:T(8,128)S(1)}) custom-call(s32[2]{0:T(128)S(1)} %pad_add_fusion.place, f32[8,272,128]{2,1,0:T(8,128)S(1)} %all_to_all.20.got, f32[128,1024]{1,0:T(8,128)S(1)} %copy-done.9), custom_call_target="tpu_custom_call" | custom-call | flops 805306368 | bytes 2195464 | tf_op jit(solution)/shard_map/pallas_call | solution.py:47
  90.6 1.9 %collective-permute-start.4 = (f32[1,128,1024]{2,1,0:T(8,128)S(1)}, f32[1,128,1024]{2,1,0:T(8,128)S(1)}, u32[]{:S(2)}, u32[]{:S(2)}) collective-permute-start(f32[1,128,1024]{2,1,0:T(8,128)S(1)} %get-tuple-element.25.residual), channel_id=1, source_target_pairs={{8,0},{16,8},{24,16},{32,24},{40,32},{48,40},{56,48},{64,56},{72,6... | collective-permute-start | bytes 1572872 | tf_op jit(solution)/shard_map/ppermute | solution.py:571
  92.5 4.1 %shard_map.54 = (f32[8,136,128]{2,1,0:T(8,128)}, f32[8,128]{1,0:T(8,128)S(1)}) custom-call(f32[8,272,128]{2,1,0:T(8,128)S(1)} %all_to_all.20.got, f32[8,3,128,128]{3,2,1,0:T(8,128)S(1)} %all-to-all-done.got.first, f32[1024,128]{1,0:T(8,128)S(1)} %get-tuple-element.22.spectral), custom_call_target="tpu_custom_call" | custom-call | flops 1610612736 | bytes 3772416 | tf_op jit(solution)/shard_map/pallas_call | solution.py:47
  96.6 10.5 %collective-permute-done.4.ahead = f32[1,128,1024]{2,1,0:T(8,128)S(1)} collective-permute-done((f32[1,128,1024]{2,1,0:T(8,128)S(1)}, f32[1,128,1024]{2,1,0:T(8,128)S(1)}, u32[]{:S(2)}, u32[]{:S(2)}) %collective-permute-start.4) | collective-permute-done | bytes 524320 | tf_op jit(solution)/shard_map/ppermute | solution.py:571
  107.2 1.8 %shard_map.55 = f32[8,136,128]{2,1,0:T(8,128)} custom-call(s32[2]{0:T(128)S(1)} %pad_add_fusion.place, f32[1,128,1024]{2,1,0:T(8,128)S(1)} %get-tuple-element.25.residual, f32[1,128,1024]{2,1,0:T(8,128)S(1)} %collective-permute-done.4.ahead, f32[8,1024]{1,0:T(8,128)S(1)} %get-tuple-element.20.edges, ...), custom_call_target="tpu_custom_call", output_to_operand_aliasing={{}: (6, {})} | custom-call | flops 16777216 | bytes 2723848 | tf_op jit(solution)/shard_map/pallas_call | solution.py:47
  109.0 3.5 %all-to-all-start.2 = ((f32[8,136,128]{2,1,0:T(8,128)}), f32[8,136,128]{2,1,0:T(8,128)S(1)}, u32[]{:S(2)}, u32[]{:S(2)}) async-start(f32[8,136,128]{2,1,0:T(8,128)} %shard_map.55), calls=%async_computation.2 | async-start | bytes 1114112 | tf_op jit(solution)/shard_map/all_to_all | solution.py:511
  112.5 1.9 %collective-permute-start.5 = (f32[1,128,1024]{2,1,0:T(8,128)S(1)}, f32[1,128,1024]{2,1,0:T(8,128)S(1)}, u32[]{:S(2)}, u32[]{:S(2)}) collective-permute-start(f32[1,128,1024]{2,1,0:T(8,128)S(1)} %get-tuple-element.25.residual), channel_id=1, source_target_pairs={{0,8},{8,16},{16,24},{24,32},{32,40},{40,48},{48,56},{56,64},{64,7... | collective-permute-start | bytes 1572872 | tf_op jit(solution)/shard_map/ppermute | solution.py:593
  114.5 6.8 %all-to-all-done.2.got = f32[8,136,128]{2,1,0:T(8,128)S(1)} async-done(((f32[8,136,128]{2,1,0:T(8,128)}), f32[8,136,128]{2,1,0:T(8,128)S(1)}, u32[]{:S(2)}, u32[]{:S(2)}) %all-to-all-start.2) | async-done | bytes 557088 | tf_op jit(solution)/shard_map/all_to_all | solution.py:511
  121.2 0.6 broadcast_in_dim.2
  121.9 7.0 %all-to-all-start.3 = ((f32[16,8,128]{2,1,0:T(8,128)}), f32[16,8,128]{2,1,0:T(8,128)S(1)}, u32[]{:S(2)}, u32[]{:S(2)}) async-start(f32[16,8,128]{2,1,0:T(8,128)} %broadcast_in_dim.2), calls=%async_computation.3 | async-start | bytes 131072 | tf_op jit(solution)/shard_map/all_to_all | solution.py:511
  128.9 0.0 collective-permute-done.5.behind
  128.9 0.0 copy-done.1
  128.9 1.5 %shard_map.56.reg = f32[128,1024]{1,0:T(8,128)S(1)} custom-call(s32[2]{0:T(128)S(1)} %pad_add_fusion.place, f32[1,128,1024]{2,1,0:T(8,128)S(1)} %get-tuple-element.25.residual, f32[1,128,1024]{2,1,0:T(8,128)S(1)} %collective-permute-done.5.behind, f32[1,128,1024]{2,1,0:T(8,128)S(1)} %collective-permute-done.4.ahead, f32[8,1024]{1,0:T(8,128)S(1)} %get-tuple-element.20.edges, ...), custom_call_target="tpu_custom_call" | custom-call | flops 16777216 | bytes 3182600 | tf_op jit(solution)/shard_map/pallas_call | solution.py:47
  130.4 0.0 copy-start.2
  130.5 0.8 copy-done.2
  131.2 3.5 %all-to-all-done.3.sums = f32[16,8,128]{2,1,0:T(8,128)S(1)} async-done(((f32[16,8,128]{2,1,0:T(8,128)}), f32[16,8,128]{2,1,0:T(8,128)S(1)}, u32[]{:S(2)}, u32[]{:S(2)}) %all-to-all-start.3) | async-done | bytes 65568 | tf_op jit(solution)/shard_map/all_to_all | solution.py:511
  134.7 1.0 copy-done.3
  135.8 1.0 copy-done.5
  136.8 2.9 %shard_map.57 = (f32[1,128,1024]{2,1,0:T(8,128)}, f32[1,128,1024]{2,1,0:T(8,128)}) custom-call(f32[16,8,128]{2,1,0:T(8,128)S(1)} %all-to-all-done.3.sums, f32[8,136,128]{2,1,0:T(8,128)S(1)} %all-to-all-done.2.got, f32[128,1024]{1,0:T(8,128)S(1)} %copy-done.3, f32[1,128,1024]{2,1,0:T(8,128)S(1)} %copy-done.5, f32[1,128,1024]{2,1,0:T(8,128)S(1)} %get-tuple-element.25.residual), custom_call_target="tpu_custom_call" | custom-call | flops 805306368 | bytes 3244032 | tf_op jit(solution)/shard_map/pallas_call | solution.py:47
  (11 shorter events, 0.1 us)
Async XLA Ops:
  4.9 8.5 %copy-start.4 = (f32[1,128,1024]{2,1,0:T(8,128)S(1)}, f32[1,128,1024]{2,1,0:T(8,128)}, u32[]{:S(2)}) copy-start(f32[1,128,1024]{2,1,0:T(8,128)} %estimate.5) | copy-start | bytes 1572868
  4.9 53.8 %all-to-all-start = ((f32[8,3,128,128]{3,2,1,0:T(8,128)}), f32[8,3,128,128]{3,2,1,0:T(8,128)S(1)}, u32[]{:S(2)}, u32[]{:S(2)}) async-start(f32[8,3,128,128]{3,2,1,0:T(8,128)} %shard_map.50), calls=%async_computation | async-start | bytes 3145728 | tf_op jit(solution)/shard_map/all_to_all | solution.py:511
  13.4 29.6 %collective-permute-start.1 = (f32[1,128,1024]{2,1,0:T(8,128)S(1)}, f32[1,128,1024]{2,1,0:T(8,128)S(1)}, u32[]{:S(2)}, u32[]{:S(2)}) collective-permute-start(f32[1,128,1024]{2,1,0:T(8,128)S(1)} %copy-done.4), channel_id=1, source_target_pairs={{8,0},{16,8},{24,16},{32,24},{40,32},{48,40},{56,48},{64,56},{72,6... | collective-permute-start | bytes 1572872 | tf_op jit(solution)/shard_map/ppermute | solution.py:529
  16.3 30.1 %collective-permute-start = (f32[1,128,1024]{2,1,0:T(8,128)S(1)}, f32[1,128,1024]{2,1,0:T(8,128)S(1)}, u32[]{:S(2)}, u32[]{:S(2)}) collective-permute-start(f32[1,128,1024]{2,1,0:T(8,128)S(1)} %copy-done.4), channel_id=1, source_target_pairs={{0,8},{8,16},{16,24},{24,32},{32,40},{40,48},{48,56},{56,64},{64,7... | collective-permute-start | bytes 1572872 | tf_op jit(solution)/shard_map/ppermute | solution.py:528
  43.0 5.6 %collective-permute-start.2 = (f32[2,1,1024]{2,1,0:T(1,128)S(1)}, f32[2,1,1024]{2,1,0:T(1,128)S(1)}, u32[]{:S(2)}, u32[]{:S(2)}) collective-permute-start(f32[2,1,1024]{2,1,0:T(1,128)S(1)} %pad_maximum_fusion), channel_id=1, source_target_pairs={{0,1},{1,2},{2,3},{3,4},{4,5},{5,6},{6,7},{8,9},{9,10},{10,11},{11... | collective-permute-start | bytes 24584 | tf_op jit(solution)/shard_map/ppermute | solution.py:542
  46.4 0.8 copy-start.6
  47.2 4.4 %collective-permute-start.3 = (f32[2,1,1024]{2,1,0:T(1,128)S(1)}, f32[2,1,1024]{2,1,0:T(1,128)S(1)}, u32[]{:S(2)}, u32[]{:S(2)}) collective-permute-start(f32[2,1,1024]{2,1,0:T(1,128)S(1)} %pad_maximum_fusion.1), channel_id=1, source_target_pairs={{1,0},{2,1},{3,2},{4,3},{5,4},{6,5},{7,6},{9,8},{10,9},{11,10},{12... | collective-permute-start | bytes 24584 | tf_op jit(solution)/shard_map/ppermute | solution.py:543
  51.6 1.0 copy-start.7
  56.4 0.8 copy-start
  57.2 0.8 copy-start.8
  58.0 0.8 copy-start.10
  58.8 1.0 copy-start.11
  66.5 21.7 %copy-start.9 = (f32[128,1024]{1,0:T(8,128)S(1)}, f32[128,1024]{1,0:T(8,128)}, u32[]{:S(2)}) copy-start(f32[128,1024]{1,0:T(8,128)} %copy-done.8) | copy-start | bytes 1572868
  90.6 16.6 %collective-permute-start.4 = (f32[1,128,1024]{2,1,0:T(8,128)S(1)}, f32[1,128,1024]{2,1,0:T(8,128)S(1)}, u32[]{:S(2)}, u32[]{:S(2)}) collective-permute-start(f32[1,128,1024]{2,1,0:T(8,128)S(1)} %get-tuple-element.25.residual), channel_id=1, source_target_pairs={{8,0},{16,8},{24,16},{32,24},{40,32},{48,40},{56,48},{64,56},{72,6... | collective-permute-start | bytes 1572872 | tf_op jit(solution)/shard_map/ppermute | solution.py:571
  107.2 21.7 %copy-start.1 = (f32[128,1024]{1,0:T(8,128)S(1)}, f32[128,1024]{1,0:T(8,128)}, u32[]{:S(2)}) copy-start(f32[128,1024]{1,0:T(8,128)} %copy-done) | copy-start | bytes 1572868
  109.0 12.3 %all-to-all-start.2 = ((f32[8,136,128]{2,1,0:T(8,128)}), f32[8,136,128]{2,1,0:T(8,128)S(1)}, u32[]{:S(2)}, u32[]{:S(2)}) async-start(f32[8,136,128]{2,1,0:T(8,128)} %shard_map.55), calls=%async_computation.2 | async-start | bytes 1114112 | tf_op jit(solution)/shard_map/all_to_all | solution.py:511
  112.5 16.4 %collective-permute-start.5 = (f32[1,128,1024]{2,1,0:T(8,128)S(1)}, f32[1,128,1024]{2,1,0:T(8,128)S(1)}, u32[]{:S(2)}, u32[]{:S(2)}) collective-permute-start(f32[1,128,1024]{2,1,0:T(8,128)S(1)} %get-tuple-element.25.residual), channel_id=1, source_target_pairs={{0,8},{8,16},{16,24},{24,32},{32,40},{40,48},{48,56},{56,64},{64,7... | collective-permute-start | bytes 1572872 | tf_op jit(solution)/shard_map/ppermute | solution.py:593
  121.9 12.8 %all-to-all-start.3 = ((f32[16,8,128]{2,1,0:T(8,128)}), f32[16,8,128]{2,1,0:T(8,128)S(1)}, u32[]{:S(2)}, u32[]{:S(2)}) async-start(f32[16,8,128]{2,1,0:T(8,128)} %broadcast_in_dim.2), calls=%async_computation.3 | async-start | bytes 131072 | tf_op jit(solution)/shard_map/all_to_all | solution.py:511
  130.4 0.8 copy-start.2
  134.7 1.0 copy-start.3
  135.8 1.0 copy-start.5

commit v2 on v1

v2 whole, which is shorter than its diff:
```python
import math

import jax
import jax.numpy as jnp
from jax import lax
from jax.experimental import pallas as pl
from jax.experimental.pallas import tpu as pltpu
from jax.sharding import Mesh
from jax.sharding import PartitionSpec as P


PLANES = ("planes_0", "planes_1", "planes_2")
ROWS = ("rows_0", "rows_1")
ALL = PLANES + ROWS
N = 1024
R = 128
G = 8
SECOND = R + 8
BOTH = 2 * R + 8
HUBER_EDGE = 0.5
SMOOTHING = 0.3
F32 = jnp.float32
BF16 = jnp.bfloat16
VMEM = pl.BlockSpec(memory_space=pltpu.VMEM)
SMEM = pl.BlockSpec(memory_space=pltpu.SMEM)
ANY = pl.BlockSpec(memory_space=pl.ANY)
HBM = pl.BlockSpec(memory_space=pltpu.HBM)
DMA = pltpu.SemaphoreType.DMA
TABLE = pltpu.VMEM((4, 32, N), F32)
MATRIX = pltpu.VMEM((N, N), BF16)
CHUNK = 16


def shape(*dims, dtype=F32):
    return jax.ShapeDtypeStruct(dims, dtype)


def call(body, outs, flops, scratch=(), out_specs=None, aliases=None, limit=32, direct=0):
    def place_of(i, a):
        if a.dtype == jnp.int32:
            return SMEM
        return VMEM if i < direct else ANY

    def launch(*args):
        size = sum(math.prod(a.shape) * a.dtype.itemsize for a in args)
        size += sum(math.prod(o.shape) * o.dtype.itemsize for o in outs)
        return pl.pallas_call(
            body,
            out_shape=tuple(outs),
            in_specs=[place_of(i, a) for i, a in enumerate(args)],
            out_specs=out_specs or tuple(VMEM for _ in outs),
            scratch_shapes=list(scratch),
            input_output_aliases=aliases or {},
            compiler_params=pltpu.CompilerParams(vmem_limit_bytes=limit << 20),
            cost_estimate=pl.CostEstimate(flops=flops, bytes_accessed=size, transcendentals=0),
        )(*args)

    return launch


def cos_sin(units):
    quarter = (units + 512) >> 10
    angle = (units - (quarter << 10)).astype(F32) * (math.pi / (2.0 * N))
    square = angle * angle
    sine = angle * (
        1.0 + square * (-1.0 / 6.0 + square * (1.0 / 120.0 + square * (-1.0 / 5040.0)))
    )
    cosine = 1.0 + square * (
        -0.5 + square * (1.0 / 24.0 + square * (-1.0 / 720.0 + square * (1.0 / 40320.0)))
    )
    odd = (quarter & 1) == 1
    cos_value = jnp.where(odd, sine, cosine)
    sin_value = jnp.where(odd, cosine, sine)
    cos_value = jnp.where(((quarter + 1) & 2) == 2, -cos_value, cos_value)
    sin_value = jnp.where((quarter & 2) == 2, -sin_value, sin_value)
    return cos_value, sin_value


def fill_table(table, samples):
    row = lax.broadcasted_iota(jnp.int32, (16, N), 0)
    lane = lax.broadcasted_iota(jnp.int32, (16, N), 1)
    if samples:
        shift = jnp.where(row < 5, row + 6, jnp.where(row < 10, row - 4, 0))
        value = lane
    else:
        shift = jnp.where(row < 5, row + 5, jnp.where(row < 10, row - 5, 0))
        value = 2 * lane + 1
    cos_bits, sin_bits = cos_sin((value << shift) & (4 * N - 1))
    norm = math.sqrt(2.0 / N)
    if samples:
        first = jnp.where(lane[:1] == 0, math.sqrt(1.0 / N), norm)
        fine = (cos_bits[10:11] * first, sin_bits[10:11] * first)
    else:
        fine = (jnp.full((1, N), norm, F32), jnp.zeros((1, N), F32))
    table[0, 0:1], table[1, 0:1] = jnp.ones((1, N), F32), jnp.zeros((1, N), F32)
    table[2, 0:1], table[3, 0:1] = fine
    for part in range(2):
        for bit in range(5):
            at = 5 * part + bit
            size = 1 << bit
            c, s = table[2 * part, 0:size], table[2 * part + 1, 0:size]
            cb, sb = cos_bits[at : at + 1], sin_bits[at : at + 1]
            table[2 * part, size : 2 * size] = c * cb - s * sb
            table[2 * part + 1, size : 2 * size] = s * cb + c * sb


def split(x):
    high = x.astype(BF16)
    low = (x - high.astype(F32)).astype(BF16)
    return high, low


def build(table, high, low, rows, lanes, first_row=None):
    for a in range(rows.start // 32, rows.stop // 32):
        value = table[0, a : a + 1, lanes] * table[2, :, lanes]
        value -= table[1, a : a + 1, lanes] * table[3, :, lanes]
        if first_row is not None and a == 0:
            row = lax.broadcasted_iota(jnp.int32, value.shape, 0)
            value = jnp.where(row == 0, first_row, value)
        block = slice(32 * a, 32 * a + 32)
        high[block, lanes], low[block, lanes] = split(value)


WHOLE = slice(0, N)


def build_samples(table, high, low, rows=WHOLE, lanes=WHOLE):
    build(table, high, low, rows, lanes)


def build_freqs(table, high, low, rows=WHOLE, lanes=WHOLE):
    build(table, high, low, rows, lanes, math.sqrt(1.0 / N))


def start(source, target, sem):
    copy = pltpu.make_async_copy(source, target, sem)
    copy.start()
    return copy


def dot(a, b):
    return jnp.dot(a, b, preferred_element_type=F32)


def stacked_times(stack, rows, high, low, columns):
    both = dot(stack[0 : 2 * rows, :], high[:, columns])
    return both[:rows] + both[rows:] + dot(stack[0:rows, :], low[:, columns])


def matrix_times(high, low, rows, pair, width, offset=0):
    both = dot(high[rows, :], pair[:, offset : offset + 2 * width])
    return both[:, :width] + both[:, width:] + dot(low[rows, :], pair[:, offset : offset + width])


def first_kernel(
    observed, estimate, sent,
    table_v, observed_v, estimate_v, sent_v, high, low, stack, sems,
):
    copies = [
        start(observed.at[0], observed_v, sems.at[1]),
        start(estimate.at[0], estimate_v, sems.at[2]),
    ]
    fill_table(table_v, True)
    copies[0].wait()
    stack[0:R, :], stack[2 * R : 3 * R, :] = split(observed_v[...])
    copies[1].wait()
    stack[R : 2 * R, :], stack[3 * R : 4 * R, :] = split(estimate_v[...])
    out_copies = []
    for d in range(G // 2):
        columns = slice(256 * d, 256 * d + 256)
        build_samples(table_v, high, low, WHOLE, columns)
        out = stacked_times(stack, 2 * R, high, low, columns)
        for h in range(2):
            lanes = slice(128 * h, 128 * h + 128)
            e = 2 * d + h
            sent_v[e, 0] = out[:R, lanes]
            sent_v[e, 1] = out[R:, lanes]
        out_copies.append(
            start(sent_v.at[2 * d : 2 * d + 2], sent.at[2 * d : 2 * d + 2], sems.at[4 + d])
        )
    for copy in out_copies:
        copy.wait()


def left(x):
    return pltpu.roll(x, N - 1, 1)


def weight_of(plane, row, value, last):
    column = jnp.where(last, 0.0, left(value) - value)
    square = plane * plane + row * row + column * column
    return 1.0 / jnp.maximum(jnp.sqrt(square), HUBER_EDGE)


def divergence(value, ahead_plane, behind_plane, ahead_row, behind_row, w_plane, w_back, w_row, w_row_back, w_col):
    flux_col = w_col * (left(value) - value)
    total = w_back * (value - behind_plane) - w_plane * (ahead_plane - value)
    total += w_row_back * (value - behind_row) - w_row * (ahead_row - value)
    total += pltpu.roll(flux_col, 1, 1) - flux_col
    return SMOOTHING * total


def as_tile(row):
    return jnp.concatenate([row[:, 128 * i : 128 * i + 128] for i in range(8)], axis=0)


def weights_kernel(
    place, estimate, behind, ahead, from_above, from_below, spectrum,
    sent, w_all, w_back_all, w_top,
    table_v, ext, ext_back, spectrum_v, sent_v, ext_w,
    high, low, stack, sems,
):
    spectrum_copy = start(spectrum.at[0], spectrum_v, sems.at[0])
    fill_table(table_v, True)
    plane, row = place[0], place[1]
    ok_plane = jnp.where(plane < 15, 1.0, 0.0)
    ok_back = jnp.where(plane > 0, 1.0, 0.0)
    ok_top = jnp.where(row > 0, 1.0, 0.0)
    ext[8 : 8 + R, :] = estimate[0]
    ext_back[0:R, :] = behind[0]
    ext[7:8, :] = from_above[0]
    ext[8 + R : 9 + R, :] = jnp.where(row < G - 1, from_below[0], estimate[0, R - 1 : R, :])
    ext_back[R : R + 1, :] = jnp.where(row < G - 1, from_below[1], behind[0, R - 1 : R, :])
    last1 = lax.broadcasted_iota(jnp.int32, (1, N), 1) == N - 1
    edge = ext[7:8, :]
    w_edge = weight_of(
        (from_above[1] - edge) * ok_plane, (ext[8:9, :] - edge) * ok_top, edge, last1
    ) * ok_top
    w_top[...] = w_edge
    ext_w[7:8, :] = w_edge
    last = lax.broadcasted_iota(jnp.int32, (CHUNK, N), 1) == N - 1
    for c in range(0, R, CHUNK):
        value = ext[8 + c : 8 + c + CHUNK, :]
        back = ext_back[c : c + CHUNK, :]
        w = weight_of(
            (ahead[0, c : c + CHUNK, :] - value) * ok_plane,
            ext[9 + c : 9 + c + CHUNK, :] - value,
            value,
            last,
        )
        ext_w[8 + c : 8 + c + CHUNK, :] = w
        w_all[c : c + CHUNK, :] = w
        w_back_all[c : c + CHUNK, :] = weight_of(
            (value - back) * ok_back, ext_back[1 + c : 1 + c + CHUNK, :] - back, back, last
        ) * ok_back
    for c in range(0, R, CHUNK):
        w = ext_w[8 + c : 8 + c + CHUNK, :]
        out = divergence(
            ext[8 + c : 8 + c + CHUNK, :],
            ahead[0, c : c + CHUNK, :],
            ext_back[c : c + CHUNK, :],
            ext[9 + c : 9 + c + CHUNK, :],
            ext[7 + c : 7 + c + CHUNK, :],
            w * ok_plane,
            w_back_all[c : c + CHUNK, :],
            w,
            ext_w[7 + c : 7 + c + CHUNK, :],
            jnp.where(last, 0.0, w),
        )
        stack[c : c + CHUNK, :], stack[R + c : R + c + CHUNK, :] = split(out)
    spectrum_copy.wait()
    out_copies = []
    for d in range(G // 2):
        columns = slice(256 * d, 256 * d + 256)
        build_samples(table_v, high, low, WHOLE, columns)
        out = stacked_times(stack, R, high, low, columns)
        for h in range(2):
            e = 2 * d + h
            sent_v[e, 0] = spectrum_v[:, 128 * e : 128 * e + 128]
            sent_v[e, 1] = out[:, 128 * h : 128 * h + 128]
        out_copies.append(
            start(sent_v.at[2 * d : 2 * d + 2], sent.at[2 * d : 2 * d + 2], sems.at[1 + d])
        )
    for copy in out_copies:
        copy.wait()


def forward_kernel(got, spectral, table_v, high, low, pair):
    fill_table(table_v, False)
    for d in range(G):
        rows = slice(R * d, R * d + R)
        pair[rows, 0:128], pair[rows, 256:384] = split(got[d, 0])
        pair[rows, 128:256], pair[rows, 384:512] = split(got[d, 1])
    for m in range(4):
        rows = slice(256 * m, 256 * m + 256)
        build_freqs(table_v, high, low, rows)
        spectral[rows, :] = matrix_times(high, low, rows, pair, 256)


def middle_kernel(
    got, spectral, sent, freq_v, sample_v, f_high, f_low, s_high, s_low, pair,
):
    fill_table(freq_v, False)
    fill_table(sample_v, True)
    for d in range(G):
        rows = slice(R * d, R * d + R)
        pair[rows, 0:128], pair[rows, 128:256] = split(got[d, 1])
    for m in range(4):
        rows = slice(256 * m, 256 * m + 256)
        build_freqs(freq_v, f_high, f_low, rows)
        reg = matrix_times(f_high, f_low, rows, pair, 128)
        gain = jnp.concatenate([got[2 * m, 0], got[2 * m + 1, 0]], axis=0)
        value = gain * (spectral[rows, :128] - gain * spectral[rows, 128:]) - reg
        pair[rows, 256:384], pair[rows, 512:640] = split(value)
        pair[rows, 384:512], pair[rows, 640:768] = split(gain * gain * value)
    for d in range(G):
        sent[d, R:SECOND] = jnp.zeros((8, 128), F32)
    for m in range(4):
        rows = slice(256 * m, 256 * m + 256)
        build_samples(sample_v, s_high, s_low, rows)
        out = matrix_times(s_high, s_low, rows, pair, 256, 256)
        for h in range(2):
            d = 2 * m + h
            block = out[R * h : R * h + R]
            sent[d, 0:R] = block[:, :128]
            sent[d, SECOND:] = block[:, 128:]
            if d + 1 < G:
                sent[d + 1, R : R + 1] = block[R - 1 : R, :128]
            if d > 0:
                sent[d - 1, R + 1 : R + 2] = block[0:1, :128]


def residual_kernel(got, residual, image, edges, table_v, f_high, f_low, stack):
    fill_table(table_v, False)
    rows = BOTH + 8
    pad = jnp.zeros((8, 128), BF16)
    for d in range(G):
        lanes = slice(128 * d, 128 * d + 128)
        high, low = split(got[d])
        stack[0:rows, lanes] = jnp.concatenate([high, pad], axis=0)
        stack[rows : 2 * rows, lanes] = jnp.concatenate([low, pad], axis=0)
    for d in range(G // 2):
        lanes = slice(256 * d, 256 * d + 256)
        build_freqs(table_v, f_high, f_low, WHOLE, lanes)
        out = stacked_times(stack, rows, f_high, f_low, lanes)
        residual[0, :, lanes] = out[:R]
        edges[0:2, lanes] = out[R : R + 2]
        image[:, lanes] = out[SECOND:BOTH]


def extend(place, residual, edges, ext):
    ext[7:8, :] = edges[0:1, :]
    ext[8 : 8 + R, :] = residual[0]
    ext[8 + R : 9 + R, :] = jnp.where(place[1] < G - 1, edges[1:2, :], residual[0, R - 1 : R, :])


def partial_kernel(place, residual, edges, w_all, image, parts, ext):
    extend(place, residual, edges, ext)
    last = lax.broadcasted_iota(jnp.int32, (CHUNK, N), 1) == N - 1
    norm = jnp.zeros((8, N), F32)
    product = jnp.zeros((8, N), F32)
    for c in range(0, R, CHUNK):
        value = ext[8 + c : 8 + c + CHUNK, :]
        row = ext[9 + c : 9 + c + CHUNK, :] - value
        column = jnp.where(last, 0.0, left(value) - value)
        cross = (SMOOTHING * w_all[c : c + CHUNK, :]) * (row * row + column * column)
        cross += value * image[c : c + CHUNK, :]
        square = value * value
        norm += square[:8] + square[8:]
        product += cross[:8] + cross[8:]
    parts[0] = norm
    parts[1] = product


def product_kernel(place, residual, ahead, w_all, parts, sent):
    total = jnp.zeros((8, N), F32)
    for c in range(0, R, CHUNK):
        plane = ahead[0, c : c + CHUNK, :] - residual[0, c : c + CHUNK, :]
        cross = w_all[c : c + CHUNK, :] * (plane * plane)
        total += cross[:8] + cross[8:]
    product = parts[1] + jnp.where(place[0] < 15, SMOOTHING, 0.0) * total
    norm = jnp.sum(as_tile(jnp.sum(parts[0], axis=0, keepdims=True)), axis=0, keepdims=True)
    product = jnp.sum(as_tile(jnp.sum(product, axis=0, keepdims=True)), axis=0, keepdims=True)
    lane = lax.broadcasted_iota(jnp.int32, (1, 128), 1)
    both = jnp.where(
        lane < 64, norm + pltpu.roll(norm, 64, 1), product + pltpu.roll(product, 64, 1)
    )
    sent[...] = jnp.broadcast_to(both[None], (128, 1, 128))


def inner_kernel(
    place, residual, behind, ahead, edges, w_all, w_back_all, w_top, blurred, image, ext, ext_w,
):
    ok_plane = jnp.where(place[0] < 15, 1.0, 0.0)
    extend(place, residual, edges, ext)
    ext_w[7:8, :] = w_top[...]
    ext_w[8 : 8 + R, :] = w_all[...]
    last = lax.broadcasted_iota(jnp.int32, (CHUNK, N), 1) == N - 1
    for c in range(0, R, CHUNK):
        w = ext_w[8 + c : 8 + c + CHUNK, :]
        image[c : c + CHUNK, :] = blurred[c : c + CHUNK, :] + divergence(
            ext[8 + c : 8 + c + CHUNK, :],
            ahead[0, c : c + CHUNK, :],
            behind[0, c : c + CHUNK, :],
            ext[9 + c : 9 + c + CHUNK, :],
            ext[7 + c : 7 + c + CHUNK, :],
            w * ok_plane,
            w_back_all[c : c + CHUNK, :],
            w,
            ext_w[7 + c : 7 + c + CHUNK, :],
            jnp.where(last, 0.0, w),
        )


def last_kernel(
    sums, estimate, residual, image, restored, final, restored_v, final_v, sems,
):
    both = jnp.sum(sums[...], axis=0)
    lane = lax.broadcasted_iota(jnp.int32, (1, 128), 1)
    norm = jnp.sum(jnp.where(lane < 64, both, 0.0), axis=1, keepdims=True)
    product = jnp.sum(jnp.where(lane < 64, 0.0, both), axis=1, keepdims=True)
    step = norm / product
    out_copies = []
    for c in range(4):
        rows = slice(32 * c, 32 * c + 32)
        restored_v[rows] = estimate[0, rows] + step * residual[0, rows]
        out_copies.append(start(restored_v.at[rows], restored.at[0, rows], sems.at[2 * c]))
        final_v[rows] = residual[0, rows] - step * image[rows]
        out_copies.append(start(final_v.at[rows], final.at[0, rows], sems.at[2 * c + 1]))
    for copy in out_copies:
        copy.wait()


def across(x, axes):
    return lax.all_to_all(x, axes, split_axis=0, concat_axis=0, tiled=True)


def field(rows=R):
    return pltpu.VMEM((rows, N), F32)


def step(observed, estimate, spectrum):
    planes, groups = 16, G
    place = jnp.stack([lax.axis_index(PLANES), lax.axis_index(ROWS)]).astype(jnp.int32)
    up = [(i, i + 1) for i in range(planes - 1)]
    down = [(i + 1, i) for i in range(planes - 1)]
    row_up = [(i, i + 1) for i in range(groups - 1)]
    row_down = [(i + 1, i) for i in range(groups - 1)]
    big = 2 * N * N * R
    block = shape(R, N)

    behind = lax.ppermute(estimate, PLANES, up)
    ahead = lax.ppermute(estimate, PLANES, down)
    sent = call(
        first_kernel,
        (shape(G, 2, R, 128),),
        6 * big,
        (TABLE, field(), field(), pltpu.VMEM((G, 2, R, 128), F32), MATRIX, MATRIX,
         pltpu.VMEM((4 * R, N), BF16), DMA((8,))),
        (ANY,), limit=60,
    )(observed, estimate)[0]
    first = across(sent, ROWS)

    tails = jnp.concatenate([estimate[:, R - 1 :], ahead[:, R - 1 :]], axis=0)
    heads = jnp.concatenate([estimate[:, :1], behind[:, :1]], axis=0)
    from_above = lax.ppermute(tails, ROWS, row_up)
    from_below = lax.ppermute(heads, ROWS, row_down)
    sent, w_all, w_back, w_top = call(
        weights_kernel,
        (shape(G, 2, R, 128), block, block, shape(1, N)),
        3 * big,
        (TABLE, field(R + 16), field(R + 8), field(), pltpu.VMEM((G, 2, R, 128), F32),
         field(R + 16), MATRIX, MATRIX, pltpu.VMEM((2 * R, N), BF16), DMA((5,))),
        (ANY, VMEM, VMEM, VMEM), direct=6,
    )(place, estimate, behind, ahead, from_above, from_below, spectrum)
    second = across(sent, ROWS)
    spectral = call(
        forward_kernel,
        (shape(N, 256),),
        6 * big,
        (TABLE, MATRIX, MATRIX, pltpu.VMEM((N, 512), BF16)),
        direct=9,
    )(first)[0]
    sent = call(
        middle_kernel,
        (shape(G, BOTH, 128),),
        9 * big,
        (TABLE, TABLE, MATRIX, MATRIX, MATRIX, MATRIX, pltpu.VMEM((N, 768), BF16)),
        direct=9,
    )(second, spectral)[0]
    third = across(sent, ROWS)

    residual, blurred, edges = call(
        residual_kernel,
        (shape(1, R, N), block, shape(8, N)),
        6 * big,
        (TABLE, MATRIX, MATRIX, pltpu.VMEM((2 * BOTH + 16, N), BF16)),
        direct=9,
    )(third)
    ahead = lax.ppermute(residual, PLANES, down)
    parts = call(
        partial_kernel, (shape(2, 8, N),), big // 16, (field(R + 16),), direct=9
    )(place, residual, edges, w_all, blurred)[0]
    late, _ = lax.optimization_barrier((residual, parts))
    behind = lax.ppermute(late, PLANES, up)
    sent = call(
        product_kernel, (shape(128, 1, 128),), big // 64, direct=9
    )(place, residual, ahead, w_all, parts)[0]
    sums = across(sent, ALL)
    image = call(
        inner_kernel, (block,), big // 16, (field(R + 16), field(R + 16)), direct=9
    )(place, residual, behind, ahead, edges, w_all, w_back, w_top, blurred)[0]
    return call(
        last_kernel,
        (shape(1, R, N), shape(1, R, N)),
        R * N * 4,
        (field(), field(), DMA((8,))),
        (ANY, ANY),
        direct=9,
    )(sums, estimate, residual, image)


def solution(mesh):
    finer = Mesh(
        mesh.devices.reshape(4, 2, 2, 2, 4),
        ("planes_0", "planes_1", "planes_2", "rows_0", "rows_1"),
    )
    spec = P(PLANES, ROWS, None)
    return jax.shard_map(
        step,
        mesh=finer,
        in_specs=(spec, spec, spec),
        out_specs=(spec, spec),
        check_vma=False,
    )
```

time: 141 us -> 129 us (0.915)
  starting transfers between devices: 33.1 us -> 50.9 us
  waiting for transfers between devices: 47.8 us -> 31.8 us
  blocking collectives: 21.7 us -> 15.6 us
  Pallas kernels: 27.4 us -> 22.1 us
  local copies, waits for them, and re-layouts: 8.79 us -> 6.91 us
    ppermute x1, waiting for transfers between devices: 23.9 us -> 0.01 us  [step(): ahead = lax.ppermute(estimate, PLANES, down)]
    ppermute x1, starting transfers between devices: 1.92 us -> 13.3 us  [step(): behind = lax.ppermute(late, PLANES, up)]
    ppermute x1, waiting for transfers between devices: 0.01 us -> 11.1 us  [step(): behind = lax.ppermute(estimate, PLANES, up)]
    ppermute x1, waiting for transfers between devices: 10.5 us -> 4.42 us  [step(): ahead = lax.ppermute(residual, PLANES, down)]
    all_to_all x1, blocking collectives: 21.7 us -> 15.6 us  [across(): return lax.all_to_all(x, axes, split_axis=0, concat_axis=0, tiled=True)]
    all_to_all x3, starting transfers between devices: 19 us -> 24.8 us  [across(): return lax.all_to_all(x, axes, split_axis=0, concat_axis=0, tiled=True)]
    pallas_call x8 -> x9, Pallas kernels: 27.4 us -> 22.1 us  [launch(): pl.pallas_call(body, out_shape=tuple(outs), in_specs=[place_of(i, a) for...]
    all_to_all x3, waiting for transfers between devices: 10.3 us -> 13.1 us  [across(): return lax.all_to_all(x, axes, split_axis=0, concat_axis=0, tiled=True)]
  transfers between devices with their start and end apart: 9 -> 9, of which waited for: 5 -> 5; matrix products, arithmetic and copies ran while one was open for 1% -> 0% of each run, Pallas kernels for 7% -> 11%
where the time goes in v2:
time: 129 us; the launch traced here: 128 us
  starting transfers between devices  50.9 us (39%)
  waiting for transfers between devices  31.8 us (25%)
  Pallas kernels  22.1 us (17%)
  blocking collectives  15.6 us (12%)
  local copies, waits for them, and re-layouts  6.91 us (5%)
    all_to_all x3, starting transfers between devices, across(): return lax.all_to_all(x, axes, split_axis=0, concat_axis=0, tiled=True)  24.8 us
    pallas_call x9, Pallas kernels, launch(): pl.pallas_call(body, out_shape=tuple(outs), in_specs=[place_of(i, a) for...  22.1 us
    all_to_all x1, blocking collectives, across(): return lax.all_to_all(x, axes, split_axis=0, concat_axis=0, tiled=True)  15.6 us
    ppermute x1, starting transfers between devices, step(): behind = lax.ppermute(late, PLANES, up)  13.3 us
    all_to_all x3, waiting for transfers between devices, across(): return lax.all_to_all(x, axes, split_axis=0, concat_axis=0, tiled=True)  13.1 us
    ppermute x1, waiting for transfers between devices, step(): behind = lax.ppermute(estimate, PLANES, up)  11.1 us
    unnamed x18, local copies, waits for them, and re-layouts  6.89 us
    ppermute x1, waiting for transfers between devices, step(): ahead = lax.ppermute(residual, PLANES, down)  4.42 us
  transfers between devices with their start and end apart: 9, of which 5 were waited for; matrix products, arithmetic and copies ran while one was open for 0% of the time, Pallas kernels for 11%

profile of v2, /device:TPU:1, one launch (start us, length us, event | category | flops | bytes accessed | tf_op | source)
XLA Modules:
  0.0 128.3 jit_solution(6558765777344168007)
XLA Ops:
  0.6 3.3 %collective-permute-start.1 = (f32[1,128,1024]{2,1,0:T(8,128)}, f32[1,128,1024]{2,1,0:T(8,128)S(1)}, u32[]{:S(2)}, u32[]{:S(2)}) collective-permute-start(f32[1,128,1024]{2,1,0:T(8,128)} %estimate.5), channel_id=1, source_target_pairs={{8,0},{16,8},{24,16},{32,24},{40,32},{48,40},{56,48},{64,56},{72,6... | collective-permute-start | bytes 1572872 | tf_op jit(solution)/shard_map/ppermute | solution.py:443
  3.9 4.0 %shard_map.51 = f32[8,2,128,128]{3,2,1,0:T(8,128)} custom-call(f32[1,128,1024]{2,1,0:T(8,128)} %observed.1, f32[1,128,1024]{2,1,0:T(8,128)} %estimate.5), custom_call_target="tpu_custom_call" | custom-call | flops 1610612736 | bytes 2097152 | tf_op jit(solution)/shard_map/pallas_call | solution.py:47
  7.9 0.0 copy-start
  8.0 7.7 %all-to-all-start.1 = ((f32[8,2,128,128]{3,2,1,0:T(8,128)}), f32[8,2,128,128]{3,2,1,0:T(8,128)S(1)}, u32[]{:S(2)}, u32[]{:S(2)}) async-start(f32[8,2,128,128]{3,2,1,0:T(8,128)} %shard_map.51), calls=%async_computation.1 | async-start | bytes 2097152 | tf_op jit(solution)/shard_map/all_to_all | solution.py:425
  15.7 0.0 copy-done
  15.7 2.7 %collective-permute-start = (f32[1,128,1024]{2,1,0:T(8,128)S(1)}, f32[1,128,1024]{2,1,0:T(8,128)S(1)}, u32[]{:S(2)}, u32[]{:S(2)}) collective-permute-start(f32[1,128,1024]{2,1,0:T(8,128)S(1)} %copy-done), channel_id=1, source_target_pairs={{0,8},{8,16},{16,24},{24,32},{32,40},{40,48},{48,56},{56,64},{64,7... | collective-permute-start | bytes 1572872 | tf_op jit(solution)/shard_map/ppermute | solution.py:442
  18.4 0.0 collective-permute-done.1.ahead
  18.4 3.6 %collective-permute-start.2 = (f32[2,1,1024]{2,1,0:T(1,128)S(1)}, f32[2,1,1024]{2,1,0:T(1,128)S(1)}, u32[]{:S(2)}, u32[]{:S(2)}) collective-permute-start(f32[2,1,1024]{2,1,0:T(1,128)S(1)} %pad_maximum_fusion), channel_id=1, source_target_pairs={{0,1},{1,2},{2,3},{3,4},{4,5},{5,6},{6,7},{8,9},{9,10},{10,11},{11... | collective-permute-start | bytes 24584 | tf_op jit(solution)/shard_map/ppermute | solution.py:456
  22.1 11.1 %collective-permute-done.behind = f32[1,128,1024]{2,1,0:T(8,128)S(1)} collective-permute-done((f32[1,128,1024]{2,1,0:T(8,128)S(1)}, f32[1,128,1024]{2,1,0:T(8,128)S(1)}, u32[]{:S(2)}, u32[]{:S(2)}) %collective-permute-start) | collective-permute-done | bytes 524320 | tf_op jit(solution)/shard_map/ppermute | solution.py:442
  33.2 1.3 %collective-permute-start.3 = (f32[2,1,1024]{2,1,0:T(1,128)S(1)}, f32[2,1,1024]{2,1,0:T(1,128)S(1)}, u32[]{:S(2)}, u32[]{:S(2)}) collective-permute-start(f32[2,1,1024]{2,1,0:T(1,128)S(1)} %pad_maximum_fusion.1), channel_id=1, source_target_pairs={{1,0},{2,1},{3,2},{4,3},{5,4},{6,5},{7,6},{9,8},{10,9},{11,10},{12... | collective-permute-start | bytes 24584 | tf_op jit(solution)/shard_map/ppermute | solution.py:457
  34.5 0.1 pad_add_fusion.place
  34.5 0.0 collective-permute-done.2.from_above
  34.5 3.2 %collective-permute-done.3.from_below = f32[2,1,1024]{2,1,0:T(1,128)S(1)} collective-permute-done((f32[2,1,1024]{2,1,0:T(1,128)S(1)}, f32[2,1,1024]{2,1,0:T(1,128)S(1)}, u32[]{:S(2)}, u32[]{:S(2)}) %collective-permute-start.3) | collective-permute-done | bytes 8224 | tf_op jit(solution)/shard_map/ppermute | solution.py:457
  37.7 0.0 copy-start.6
  37.7 1.0 copy-done.6
  38.8 4.6 %shard_map.50 = (f32[8,2,128,128]{3,2,1,0:T(8,128)}, f32[128,1024]{1,0:T(8,128)S(1)}, f32[128,1024]{1,0:T(8,128)S(1)}, f32[1,1024]{1,0:T(1,128)S(1)}) custom-call(s32[2]{0:T(128)S(1)} %pad_add_fusion.place, f32[1,128,1024]{2,1,0:T(8,128)S(1)} %copy-done, f32[1,128,1024]{2,1,0:T(8,128)S(1)} %collective-permute-done.behind, ...), custom_call_target="tpu_custom_call" | custom-call | flops 805306368 | bytes 4214792 | tf_op jit(solution)/shard_map/pallas_call | solution.py:47
  43.4 0.0 copy-start.2
  43.4 0.8 copy-done.2
  44.2 0.0 all-to-all-done.1.got
  44.2 7.9 %all-to-all-start = ((f32[8,2,128,128]{3,2,1,0:T(8,128)}), f32[8,2,128,128]{3,2,1,0:T(8,128)S(1)}, u32[]{:S(2)}, u32[]{:S(2)}) async-start(f32[8,2,128,128]{3,2,1,0:T(8,128)} %get-tuple-element.10), calls=%async_computation | async-start | bytes 2097152 | tf_op jit(solution)/shard_map/all_to_all | solution.py:425
  52.1 2.3 %shard_map.52.spectral = f32[1024,256]{1,0:T(8,128)S(1)} custom-call(f32[8,2,128,128]{3,2,1,0:T(8,128)S(1)} %all-to-all-done.1.got), custom_call_target="tpu_custom_call" | custom-call | flops 1610612736 | bytes 2097152 | tf_op jit(solution)/shard_map/pallas_call | solution.py:47
  54.4 0.0 copy-start.7
  54.4 1.0 copy-done.7
  55.4 7.4 %all-to-all-done.got = f32[8,2,128,128]{3,2,1,0:T(8,128)S(1)} async-done(((f32[8,2,128,128]{3,2,1,0:T(8,128)}), f32[8,2,128,128]{3,2,1,0:T(8,128)S(1)}, u32[]{:S(2)}, u32[]{:S(2)}) %all-to-all-start) | async-done | bytes 1048608 | tf_op jit(solution)/shard_map/all_to_all | solution.py:425
  62.8 0.0 copy-start.8
  62.8 1.2 copy-done.8
  64.1 4.1 %shard_map.53 = f32[8,264,128]{2,1,0:T(8,128)S(1)} custom-call(f32[8,2,128,128]{3,2,1,0:T(8,128)S(1)} %all-to-all-done.got, f32[1024,256]{1,0:T(8,128)S(1)} %copy-done.8), custom_call_target="tpu_custom_call" | custom-call | flops 2415919104 | bytes 3178496 | tf_op jit(solution)/shard_map/pallas_call | solution.py:47
  68.2 15.6 %all_to_all.20.got = f32[8,264,128]{2,1,0:T(8,128)S(1)} all-to-all(f32[8,264,128]{2,1,0:T(8,128)S(1)} %shard_map.53), channel_id=1, replica_groups=mesh['planes_0'=4,'planes_1'=2,'planes_2'=2,'rows_0'=2,'rows_1'=4] {'row..., dimensions={0} | all-to-all | bytes 2162688 | tf_op jit(solution)/shard_map/all_to_all | solution.py:425
  83.8 2.3 %shard_map.54 = (f32[1,128,1024]{2,1,0:T(8,128)S(1)}, f32[128,1024]{1,0:T(8,128)S(1)}, f32[8,1024]{1,0:T(8,128)S(1)}) custom-call(f32[8,264,128]{2,1,0:T(8,128)S(1)} %all_to_all.20.got), custom_call_target="tpu_custom_call" | custom-call | flops 1610612736 | bytes 2162688 | tf_op jit(solution)/shard_map/pallas_call | solution.py:47
  86.0 1.9 %collective-permute-start.4 = (f32[1,128,1024]{2,1,0:T(8,128)S(1)}, f32[1,128,1024]{2,1,0:T(8,128)S(1)}, u32[]{:S(2)}, u32[]{:S(2)}) collective-permute-start(f32[1,128,1024]{2,1,0:T(8,128)S(1)} %get-tuple-element.15.residual), channel_id=1, source_target_pairs={{8,0},{16,8},{24,16},{32,24},{40,32},{48,40},{56,48},{64,56},{72,6... | collective-permute-start | bytes 1572872 | tf_op jit(solution)/shard_map/ppermute | solution.py:490
  88.0 0.9 shard_map.55.parts
  88.9 13.3 %collective-permute-start.5 = (f32[1,128,1024]{2,1,0:T(8,128)S(1)}, f32[1,128,1024]{2,1,0:T(8,128)S(1)}, u32[]{:S(2)}, u32[]{:S(2)}) collective-permute-start(f32[1,128,1024]{2,1,0:T(8,128)S(1)} %get-tuple-element.15.residual), channel_id=1, source_target_pairs={{0,8},{8,16},{16,24},{24,32},{32,40},{40,48},{48,56},{56,64},{64,7... | collective-permute-start | bytes 1572872 | tf_op jit(solution)/shard_map/ppermute | solution.py:495
  102.2 4.4 %collective-permute-done.4.ahead = f32[1,128,1024]{2,1,0:T(8,128)S(1)} collective-permute-done((f32[1,128,1024]{2,1,0:T(8,128)S(1)}, f32[1,128,1024]{2,1,0:T(8,128)S(1)}, u32[]{:S(2)}, u32[]{:S(2)}) %collective-permute-start.4) | collective-permute-done | bytes 524320 | tf_op jit(solution)/shard_map/ppermute | solution.py:490
  106.6 1.4 %shard_map.56 = f32[128,1,128]{2,1,0:T(1,128)} custom-call(s32[2]{0:T(128)S(1)} %pad_add_fusion.place, f32[1,128,1024]{2,1,0:T(8,128)S(1)} %get-tuple-element.15.residual, f32[1,128,1024]{2,1,0:T(8,128)S(1)} %collective-permute-done.4.ahead, f32[128,1024]{1,0:T(8,128)S(1)} %get-tuple-element.12.w_all, f32[2,8,1024]{2,1,0:T(8,128)S(1)} %shard_map.55.parts), custom_call_target="tpu_custom_call" | custom-call | flops 4194304 | bytes 1703944 | tf_op jit(solution)/shard_map/pallas_call | solution.py:47
  108.0 9.1 %all-to-all-start.3 = ((f32[128,1,128]{2,1,0:T(1,128)}), f32[128,1,128]{2,1,0:T(1,128)S(1)}, u32[]{:S(2)}, u32[]{:S(2)}) async-start(f32[128,1,128]{2,1,0:T(1,128)} %shard_map.56), calls=%async_computation.3 | async-start | bytes 131072 | tf_op jit(solution)/shard_map/all_to_all | solution.py:425
  117.1 0.0 collective-permute-done.5.behind
  117.1 0.0 copy-start.4
  117.1 0.8 copy-done.4
  117.9 0.0 copy-start.3
  117.9 1.0 copy-done.3
  118.9 0.0 copy-start.5
  118.9 1.0 copy-done.5
  120.0 0.0 copy-start.1
  120.0 1.3 shard_map.57.image
  121.2 5.7 %all-to-all-done.3.sums = f32[128,1,128]{2,1,0:T(1,128)S(1)} async-done(((f32[128,1,128]{2,1,0:T(1,128)}), f32[128,1,128]{2,1,0:T(1,128)S(1)}, u32[]{:S(2)}, u32[]{:S(2)}) %all-to-all-start.3) | async-done | bytes 65568 | tf_op jit(solution)/shard_map/all_to_all | solution.py:425
  126.9 0.0 copy-done.1
  126.9 1.3 shard_map.58
  (5 shorter events, 0.0 us)
Async XLA Ops:
  0.6 17.8 %collective-permute-start.1 = (f32[1,128,1024]{2,1,0:T(8,128)}, f32[1,128,1024]{2,1,0:T(8,128)S(1)}, u32[]{:S(2)}, u32[]{:S(2)}) collective-permute-start(f32[1,128,1024]{2,1,0:T(8,128)} %estimate.5), channel_id=1, source_target_pairs={{8,0},{16,8},{24,16},{32,24},{40,32},{48,40},{56,48},{64,56},{72,6... | collective-permute-start | bytes 1572872 | tf_op jit(solution)/shard_map/ppermute | solution.py:443
  7.9 7.8 %copy-start = (f32[1,128,1024]{2,1,0:T(8,128)S(1)}, f32[1,128,1024]{2,1,0:T(8,128)}, u32[]{:S(2)}) copy-start(f32[1,128,1024]{2,1,0:T(8,128)} %estimate.5) | copy-start | bytes 1572868
  8.0 36.2 %all-to-all-start.1 = ((f32[8,2,128,128]{3,2,1,0:T(8,128)}), f32[8,2,128,128]{3,2,1,0:T(8,128)S(1)}, u32[]{:S(2)}, u32[]{:S(2)}) async-start(f32[8,2,128,128]{3,2,1,0:T(8,128)} %shard_map.51), calls=%async_computation.1 | async-start | bytes 2097152 | tf_op jit(solution)/shard_map/all_to_all | solution.py:425
  15.7 17.4 %collective-permute-start = (f32[1,128,1024]{2,1,0:T(8,128)S(1)}, f32[1,128,1024]{2,1,0:T(8,128)S(1)}, u32[]{:S(2)}, u32[]{:S(2)}) collective-permute-start(f32[1,128,1024]{2,1,0:T(8,128)S(1)} %copy-done), channel_id=1, source_target_pairs={{0,8},{8,16},{16,24},{24,32},{32,40},{40,48},{48,56},{56,64},{64,7... | collective-permute-start | bytes 1572872 | tf_op jit(solution)/shard_map/ppermute | solution.py:442
  18.4 16.1 %collective-permute-start.2 = (f32[2,1,1024]{2,1,0:T(1,128)S(1)}, f32[2,1,1024]{2,1,0:T(1,128)S(1)}, u32[]{:S(2)}, u32[]{:S(2)}) collective-permute-start(f32[2,1,1024]{2,1,0:T(1,128)S(1)} %pad_maximum_fusion), channel_id=1, source_target_pairs={{0,1},{1,2},{2,3},{3,4},{4,5},{5,6},{6,7},{8,9},{9,10},{10,11},{11... | collective-permute-start | bytes 24584 | tf_op jit(solution)/shard_map/ppermute | solution.py:456
  33.2 4.6 %collective-permute-start.3 = (f32[2,1,1024]{2,1,0:T(1,128)S(1)}, f32[2,1,1024]{2,1,0:T(1,128)S(1)}, u32[]{:S(2)}, u32[]{:S(2)}) collective-permute-start(f32[2,1,1024]{2,1,0:T(1,128)S(1)} %pad_maximum_fusion.1), channel_id=1, source_target_pairs={{1,0},{2,1},{3,2},{4,3},{5,4},{6,5},{7,6},{9,8},{10,9},{11,10},{12... | collective-permute-start | bytes 24584 | tf_op jit(solution)/shard_map/ppermute | solution.py:457
  37.7 1.0 copy-start.6
  43.4 0.8 copy-start.2
  44.2 18.7 %all-to-all-start = ((f32[8,2,128,128]{3,2,1,0:T(8,128)}), f32[8,2,128,128]{3,2,1,0:T(8,128)S(1)}, u32[]{:S(2)}, u32[]{:S(2)}) async-start(f32[8,2,128,128]{3,2,1,0:T(8,128)} %get-tuple-element.10), calls=%async_computation | async-start | bytes 2097152 | tf_op jit(solution)/shard_map/all_to_all | solution.py:425
  54.4 1.0 copy-start.7
  62.8 1.2 copy-start.8
  86.0 20.6 %collective-permute-start.4 = (f32[1,128,1024]{2,1,0:T(8,128)S(1)}, f32[1,128,1024]{2,1,0:T(8,128)S(1)}, u32[]{:S(2)}, u32[]{:S(2)}) collective-permute-start(f32[1,128,1024]{2,1,0:T(8,128)S(1)} %get-tuple-element.15.residual), channel_id=1, source_target_pairs={{8,0},{16,8},{24,16},{32,24},{40,32},{48,40},{56,48},{64,56},{72,6... | collective-permute-start | bytes 1572872 | tf_op jit(solution)/shard_map/ppermute | solution.py:490
  88.9 28.2 %collective-permute-start.5 = (f32[1,128,1024]{2,1,0:T(8,128)S(1)}, f32[1,128,1024]{2,1,0:T(8,128)S(1)}, u32[]{:S(2)}, u32[]{:S(2)}) collective-permute-start(f32[1,128,1024]{2,1,0:T(8,128)S(1)} %get-tuple-element.15.residual), channel_id=1, source_target_pairs={{0,8},{8,16},{16,24},{24,32},{32,40},{40,48},{48,56},{56,64},{64,7... | collective-permute-start | bytes 1572872 | tf_op jit(solution)/shard_map/ppermute | solution.py:495
  108.0 18.9 %all-to-all-start.3 = ((f32[128,1,128]{2,1,0:T(1,128)}), f32[128,1,128]{2,1,0:T(1,128)S(1)}, u32[]{:S(2)}, u32[]{:S(2)}) async-start(f32[128,1,128]{2,1,0:T(1,128)} %shard_map.56), calls=%async_computation.3 | async-start | bytes 131072 | tf_op jit(solution)/shard_map/all_to_all | solution.py:425
  117.1 0.8 copy-start.4
  117.9 1.0 copy-start.3
  118.9 1.0 copy-start.5
  120.0 6.9 %copy-start.1 = (f32[1,128,1024]{2,1,0:T(8,128)S(1)}, f32[1,128,1024]{2,1,0:T(8,128)}, u32[]{:S(2)}) copy-start(f32[1,128,1024]{2,1,0:T(8,128)} %estimate.5) | copy-start | bytes 1572868

commit v3 on v2

--- a/solution.py
+++ b/solution.py
@@ -205,29 +205,21 @@
 
 
 def weights_kernel(
-    place, estimate, behind, ahead, from_above, from_below, spectrum,
-    sent, w_all, w_back_all, w_top,
+    place, estimate, behind, ahead, spectrum,
+    sent, w_all, w_back_all, strip,
     table_v, ext, ext_back, spectrum_v, sent_v, ext_w,
     high, low, stack, sems,
 ):
     spectrum_copy = start(spectrum.at[0], spectrum_v, sems.at[0])
     fill_table(table_v, True)
-    plane, row = place[0], place[1]
-    ok_plane = jnp.where(plane < 15, 1.0, 0.0)
-    ok_back = jnp.where(plane > 0, 1.0, 0.0)
-    ok_top = jnp.where(row > 0, 1.0, 0.0)
+    ok_plane = jnp.where(place[0] < 15, 1.0, 0.0)
+    ok_back = jnp.where(place[0] > 0, 1.0, 0.0)
     ext[8 : 8 + R, :] = estimate[0]
     ext_back[0:R, :] = behind[0]
-    ext[7:8, :] = from_above[0]
-    ext[8 + R : 9 + R, :] = jnp.where(row < G - 1, from_below[0], estimate[0, R - 1 : R, :])
-    ext_back[R : R + 1, :] = jnp.where(row < G - 1, from_below[1], behind[0, R - 1 : R, :])
-    last1 = lax.broadcasted_iota(jnp.int32, (1, N), 1) == N - 1
-    edge = ext[7:8, :]
-    w_edge = weight_of(
-        (from_above[1] - edge) * ok_plane, (ext[8:9, :] - edge) * ok_top, edge, last1
-    ) * ok_top
-    w_top[...] = w_edge
-    ext_w[7:8, :] = w_edge
+    ext[7:8, :] = estimate[0, 0:1, :]
+    ext[8 + R : 9 + R, :] = estimate[0, R - 1 : R, :]
+    ext_back[R : R + 1, :] = behind[0, R - 1 : R, :]
+    ext_w[7:8, :] = jnp.zeros((1, N), F32)
     last = lax.broadcasted_iota(jnp.int32, (CHUNK, N), 1) == N - 1
     for c in range(0, R, CHUNK):
         value = ext[8 + c : 8 + c + CHUNK, :]
@@ -258,6 +250,13 @@
             jnp.where(last, 0.0, w),
         )
         stack[c : c + CHUNK, :], stack[R + c : R + c + CHUNK, :] = split(out)
+    for i, rows in enumerate((
+        estimate[0, 0:2, :], estimate[0, R - 2 : R, :], ahead[0, 0:1, :], ahead[0, R - 1 : R, :],
+        behind[0, 0:1, :], behind[0, R - 1 : R, :], w_all[0:1, :], w_all[R - 2 : R - 1, :],
+        w_back_all[0:1, :],
+    )):
+        at = 2 * i if i < 2 else i + 2
+        strip[at : at + rows.shape[0], :] = rows
     spectrum_copy.wait()
     out_copies = []
     for d in range(G // 2):
@@ -271,6 +270,60 @@
         out_copies.append(
             start(sent_v.at[2 * d : 2 * d + 2], sent.at[2 * d : 2 * d + 2], sems.at[1 + d])
         )
+    for copy in out_copies:
+        copy.wait()
+
+
+def edge_kernel(
+    place, from_above, from_below, strip, half_sent, sent, w_edge,
+    table_v, high, low, stack, rows_v, sems,
+):
+    fill_table(table_v, True)
+    plane, row = place[0], place[1]
+    ok_plane = jnp.where(plane < 15, 1.0, 0.0)
+    ok_back = jnp.where(plane > 0, 1.0, 0.0)
+    ok_top = jnp.where(row > 0, 1.0, 0.0)
+    inside = row < G - 1
+    last = lax.broadcasted_iota(jnp.int32, (1, N), 1) == N - 1
+
+    def line(i):
+        return strip[i : i + 1, :]
+
+    head, second, before, tail = line(0), line(1), line(2), line(3)
+    top = from_above[0]
+    bottom = jnp.where(inside, from_below[0], tail)
+    behind_bottom = jnp.where(inside, from_below[1], line(7))
+    w_top = ok_top * weight_of(
+        (from_above[1] - top) * ok_plane, (head - top) * ok_top, top, last
+    )
+    w_tail = weight_of((line(5) - tail) * ok_plane, bottom - tail, tail, last)
+    w_back_tail = ok_back * weight_of(
+        (tail - line(7)) * ok_back, behind_bottom - line(7), line(7), last
+    )
+    w_edge[0:1, :], w_edge[1:2, :], w_edge[2:3, :] = w_top, w_tail, w_back_tail
+    w_head = line(8)
+    first_row = divergence(
+        head, line(4), line(6), second, top,
+        w_head * ok_plane, line(10), w_head, w_top, jnp.where(last, 0.0, w_head),
+    )
+    last_row = divergence(
+        tail, line(5), line(7), bottom, before,
+        w_tail * ok_plane, w_back_tail, w_tail, line(9), jnp.where(last, 0.0, w_tail),
+    )
+    pair = jnp.concatenate([first_row, last_row, jnp.zeros((14, N), F32)], axis=0)
+    stack[0:16, :], stack[16:32, :] = split(pair)
+    out_copies = []
+    for d in range(G // 2):
+        columns = slice(256 * d, 256 * d + 256)
+        build_samples(table_v, high, low, WHOLE, columns)
+        out = stacked_times(stack, 16, high, low, columns)
+        for h in range(2):
+            e = 2 * d + h
+            rows_v[e] = out[0:8, 128 * h : 128 * h + 128]
+            for i, at in enumerate((0, R - 1)):
+                out_copies.append(
+                    start(rows_v.at[e, i : i + 1], sent.at[e, 1, at : at + 1], sems.at[2 * e + i])
+                )
     for copy in out_copies:
         copy.wait()
 
@@ -338,13 +391,21 @@
         image[:, lanes] = out[SECOND:BOTH]
 
 
+def patched(weights, w_edge, c, line):
+    w = weights[c : c + CHUNK, :]
+    if c + CHUNK < R:
+        return w
+    row = lax.broadcasted_iota(jnp.int32, (CHUNK, N), 0)
+    return jnp.where(row == CHUNK - 1, w_edge[line : line + 1, :], w)
+
+
 def extend(place, residual, edges, ext):
     ext[7:8, :] = edges[0:1, :]
     ext[8 : 8 + R, :] = residual[0]
     ext[8 + R : 9 + R, :] = jnp.where(place[1] < G - 1, edges[1:2, :], residual[0, R - 1 : R, :])
 
 
-def partial_kernel(place, residual, edges, w_all, image, parts, ext):
+def partial_kernel(place, residual, edges, w_all, w_edge, image, parts, ext):
     extend(place, residual, edges, ext)
     last = lax.broadcasted_iota(jnp.int32, (CHUNK, N), 1) == N - 1
     norm = jnp.zeros((8, N), F32)
@@ -353,7 +414,7 @@
         value = ext[8 + c : 8 + c + CHUNK, :]
         row = ext[9 + c : 9 + c + CHUNK, :] - value
         column = jnp.where(last, 0.0, left(value) - value)
-        cross = (SMOOTHING * w_all[c : c + CHUNK, :]) * (row * row + column * column)
+        cross = (SMOOTHING * patched(w_all, w_edge, c, 1)) * (row * row + column * column)
         cross += value * image[c : c + CHUNK, :]
         square = value * value
         norm += square[:8] + square[8:]
@@ -362,11 +423,11 @@
     parts[1] = product
 
 
-def product_kernel(place, residual, ahead, w_all, parts, sent):
+def product_kernel(place, residual, ahead, w_all, w_edge, parts, sent):
     total = jnp.zeros((8, N), F32)
     for c in range(0, R, CHUNK):
         plane = ahead[0, c : c + CHUNK, :] - residual[0, c : c + CHUNK, :]
-        cross = w_all[c : c + CHUNK, :] * (plane * plane)
+        cross = patched(w_all, w_edge, c, 1) * (plane * plane)
         total += cross[:8] + cross[8:]
     product = parts[1] + jnp.where(place[0] < 15, SMOOTHING, 0.0) * total
     norm = jnp.sum(as_tile(jnp.sum(parts[0], axis=0, keepdims=True)), axis=0, keepdims=True)
@@ -379,12 +440,13 @@
 
 
 def inner_kernel(
-    place, residual, behind, ahead, edges, w_all, w_back_all, w_top, blurred, image, ext, ext_w,
+    place, residual, behind, ahead, edges, w_all, w_back_all, w_edge, blurred, image, ext, ext_w,
 ):
     ok_plane = jnp.where(place[0] < 15, 1.0, 0.0)
     extend(place, residual, edges, ext)
-    ext_w[7:8, :] = w_top[...]
+    ext_w[7:8, :] = w_edge[0:1, :]
     ext_w[8 : 8 + R, :] = w_all[...]
+    ext_w[7 + R : 8 + R, :] = w_edge[1:2, :]
     last = lax.broadcasted_iota(jnp.int32, (CHUNK, N), 1) == N - 1
     for c in range(0, R, CHUNK):
         w = ext_w[8 + c : 8 + c + CHUNK, :]
@@ -395,7 +457,7 @@
             ext[9 + c : 9 + c + CHUNK, :],
             ext[7 + c : 7 + c + CHUNK, :],
             w * ok_plane,
-            w_back_all[c : c + CHUNK, :],
+            patched(w_back_all, w_edge, c, 2),
             w,
             ext_w[7 + c : 7 + c + CHUNK, :],
             jnp.where(last, 0.0, w),
@@ -455,14 +517,22 @@
     heads = jnp.concatenate([estimate[:, :1], behind[:, :1]], axis=0)
     from_above = lax.ppermute(tails, ROWS, row_up)
     from_below = lax.ppermute(heads, ROWS, row_down)
-    sent, w_all, w_back, w_top = call(
+    half_sent, w_all, w_back, strip = call(
         weights_kernel,
-        (shape(G, 2, R, 128), block, block, shape(1, N)),
+        (shape(G, 2, R, 128), block, block, shape(16, N)),
         3 * big,
         (TABLE, field(R + 16), field(R + 8), field(), pltpu.VMEM((G, 2, R, 128), F32),
          field(R + 16), MATRIX, MATRIX, pltpu.VMEM((2 * R, N), BF16), DMA((5,))),
-        (ANY, VMEM, VMEM, VMEM), direct=6,
-    )(place, estimate, behind, ahead, from_above, from_below, spectrum)
+        (ANY, VMEM, VMEM, VMEM), direct=4,
+    )(place, estimate, behind, ahead, spectrum)
+    sent, w_edge = call(
+        edge_kernel,
+        (shape(G, 2, R, 128), shape(8, N)),
+        big,
+        (TABLE, MATRIX, MATRIX, pltpu.VMEM((32, N), BF16), pltpu.VMEM((G, 8, 128), F32),
+         DMA((16,))),
+        (ANY, VMEM), {4: 0}, direct=4,
+    )(place, from_above, from_below, strip, half_sent)
     second = across(sent, ROWS)
     spectral = call(
         forward_kernel,
@@ -490,16 +560,16 @@
     ahead = lax.ppermute(residual, PLANES, down)
     parts = call(
         partial_kernel, (shape(2, 8, N),), big // 16, (field(R + 16),), direct=9
-    )(place, residual, edges, w_all, blurred)[0]
-    late, _ = lax.optimization_barrier((residual, parts))
+    )(place, residual, edges, w_all, w_edge, blurred)[0]
+    late, _ = lax.optimization_barrier((residual, ahead))
     behind = lax.ppermute(late, PLANES, up)
     sent = call(
         product_kernel, (shape(128, 1, 128),), big // 64, direct=9
-    )(place, residual, ahead, w_all, parts)[0]
+    )(place, residual, ahead, w_all, w_edge, parts)[0]
     sums = across(sent, ALL)
     image = call(
         inner_kernel, (block,), big // 16, (field(R + 16), field(R + 16)), direct=9
-    )(place, residual, behind, ahead, edges, w_all, w_back, w_top, blurred)[0]
+    )(place, residual, behind, ahead, edges, w_all, w_back, w_edge, blurred)[0]
     return call(
         last_kernel,
         (shape(1, R, N), shape(1, R, N)),

time: 129 us -> 143 us (1.11)
  waiting for transfers between devices: 31.8 us -> 47.2 us
  starting transfers between devices: 50.9 us -> 42.9 us
  blocking collectives: 15.6 us -> 19.5 us
  Pallas kernels: 22.1 us -> 24.8 us
    ppermute x1, waiting for transfers between devices: 0.01 us -> 18.3 us  [step(): ahead = lax.ppermute(estimate, PLANES, down)]
    ppermute x1, starting transfers between devices: 13.3 us -> 1.91 us  [step(): behind = lax.ppermute(late, PLANES, up)]
    ppermute x1, waiting for transfers between devices: 11.1 us -> 0.01 us  [step(): behind = lax.ppermute(estimate, PLANES, up)]
    ppermute x1, waiting for transfers between devices: 4.42 us -> 14.3 us  [step(): ahead = lax.ppermute(residual, PLANES, down)]
    all_to_all x3, starting transfers between devices: 24.8 us -> 28.9 us  [across(): return lax.all_to_all(x, axes, split_axis=0, concat_axis=0, tiled=True)]
    all_to_all x1, blocking collectives: 15.6 us -> 19.5 us  [across(): return lax.all_to_all(x, axes, split_axis=0, concat_axis=0, tiled=True)]
    ppermute x1, waiting for transfers between devices: 3.18 us -> 0.01 us  [step(): from_below = lax.ppermute(heads, ROWS, row_down)]
    pallas_call x9 -> x10, Pallas kernels: 22.1 us -> 24.8 us  [launch(): pl.pallas_call(body, out_shape=tuple(outs), in_specs=[place_of(i, a) for...]
  transfers between devices with their start and end apart: 9 -> 9, of which waited for: 5 -> 4; matrix products, arithmetic and copies ran while one was open for 0% -> 0% of each run, Pallas kernels for 11% -> 9%
where the time goes in v3:
time: 143 us; the launch traced here: 142 us
  waiting for transfers between devices  47.2 us (33%)
  starting transfers between devices  42.9 us (30%)
  Pallas kernels  24.8 us (17%)
  blocking collectives  19.5 us (14%)
  local copies, waits for them, and re-layouts  6.93 us (5%)
    all_to_all x3, starting transfers between devices, across(): return lax.all_to_all(x, axes, split_axis=0, concat_axis=0, tiled=True)  28.9 us
    pallas_call x10, Pallas kernels, launch(): pl.pallas_call(body, out_shape=tuple(outs), in_specs=[place_of(i, a) for...  24.8 us
    all_to_all x1, blocking collectives, across(): return lax.all_to_all(x, axes, split_axis=0, concat_axis=0, tiled=True)  19.5 us
    ppermute x1, waiting for transfers between devices, step(): ahead = lax.ppermute(estimate, PLANES, down)  18.3 us
    all_to_all x3, waiting for transfers between devices, across(): return lax.all_to_all(x, axes, split_axis=0, concat_axis=0, tiled=True)  14.6 us
    ppermute x1, waiting for transfers between devices, step(): ahead = lax.ppermute(residual, PLANES, down)  14.3 us
    unnamed x18, local copies, waits for them, and re-layouts  6.91 us
    ppermute x1, starting transfers between devices, step(): from_above = lax.ppermute(tails, ROWS, row_up)  3.37 us
  transfers between devices with their start and end apart: 9, of which 4 were waited for; matrix products, arithmetic and copies ran while one was open for 0% of the time, Pallas kernels for 9%

profile of v3, /device:TPU:1, one launch (start us, length us, event | category | flops | bytes accessed | tf_op | source)
XLA Modules:
  0.0 142.5 jit_solution(8940240525542422556)
XLA Ops:
  0.6 4.0 %shard_map.52 = f32[8,2,128,128]{3,2,1,0:T(8,128)} custom-call(f32[1,128,1024]{2,1,0:T(8,128)} %observed.1, f32[1,128,1024]{2,1,0:T(8,128)} %estimate.5), custom_call_target="tpu_custom_call" | custom-call | flops 1610612736 | bytes 2097152 | tf_op jit(solution)/shard_map/pallas_call | solution.py:47
  4.6 0.0 copy-start
  4.7 8.5 %all-to-all-start.1 = ((f32[8,2,128,128]{3,2,1,0:T(8,128)}), f32[8,2,128,128]{3,2,1,0:T(8,128)S(1)}, u32[]{:S(2)}, u32[]{:S(2)}) async-start(f32[8,2,128,128]{3,2,1,0:T(8,128)} %shard_map.52), calls=%async_computation.1 | async-start | bytes 2097152 | tf_op jit(solution)/shard_map/all_to_all | solution.py:487
  13.1 0.0 copy-done
  13.1 2.9 %collective-permute-start = (f32[1,128,1024]{2,1,0:T(8,128)S(1)}, f32[1,128,1024]{2,1,0:T(8,128)S(1)}, u32[]{:S(2)}, u32[]{:S(2)}) collective-permute-start(f32[1,128,1024]{2,1,0:T(8,128)S(1)} %copy-done), channel_id=1, source_target_pairs={{8,0},{16,8},{24,16},{32,24},{40,32},{48,40},{56,48},{64,56},{72,6... | collective-permute-start | bytes 1572872 | tf_op jit(solution)/shard_map/ppermute | solution.py:505
  16.0 2.7 %collective-permute-start.2 = (f32[1,128,1024]{2,1,0:T(8,128)S(1)}, f32[1,128,1024]{2,1,0:T(8,128)S(1)}, u32[]{:S(2)}, u32[]{:S(2)}) collective-permute-start(f32[1,128,1024]{2,1,0:T(8,128)S(1)} %copy-done), channel_id=1, source_target_pairs={{0,8},{8,16},{16,24},{24,32},{32,40},{40,48},{48,56},{56,64},{64,7... | collective-permute-start | bytes 1572872 | tf_op jit(solution)/shard_map/ppermute | solution.py:504
  18.7 0.1 pad_add_fusion.place
  18.8 18.3 %collective-permute-done.ahead = f32[1,128,1024]{2,1,0:T(8,128)S(1)} collective-permute-done((f32[1,128,1024]{2,1,0:T(8,128)S(1)}, f32[1,128,1024]{2,1,0:T(8,128)S(1)}, u32[]{:S(2)}, u32[]{:S(2)}) %collective-permute-start) | collective-permute-done | bytes 524320 | tf_op jit(solution)/shard_map/ppermute | solution.py:505
  37.1 3.4 %collective-permute-start.1 = (f32[2,1,1024]{2,1,0:T(1,128)S(1)}, f32[2,1,1024]{2,1,0:T(1,128)S(1)}, u32[]{:S(2)}, u32[]{:S(2)}) collective-permute-start(f32[2,1,1024]{2,1,0:T(1,128)S(1)} %pad_maximum_fusion), channel_id=1, source_target_pairs={{0,1},{1,2},{2,3},{3,4},{4,5},{5,6},{6,7},{8,9},{9,10},{10,11},{11... | collective-permute-start | bytes 24584 | tf_op jit(solution)/shard_map/ppermute | solution.py:518
  40.4 0.0 collective-permute-done.2.behind
  40.5 1.3 collective-permute-start.3
  41.8 0.0 copy-start.6
  41.8 1.0 copy-done.6
  42.8 4.6 %shard_map.50 = (f32[8,2,128,128]{3,2,1,0:T(8,128)}, f32[128,1024]{1,0:T(8,128)S(1)}, f32[128,1024]{1,0:T(8,128)S(1)}, f32[16,1024]{1,0:T(8,128)S(1)}) custom-call(s32[2]{0:T(128)S(1)} %pad_add_fusion.place, f32[1,128,1024]{2,1,0:T(8,128)S(1)} %copy-done, f32[1,128,1024]{2,1,0:T(8,128)S(1)} %collective-permute-done.2.behind, ...), custom_call_target="tpu_custom_call" | custom-call | flops 805306368 | bytes 4259848 | tf_op jit(solution)/shard_map/pallas_call | solution.py:47
  47.4 0.0 copy-start.2
  47.4 0.8 copy-done.2
  48.2 0.0 collective-permute-done.1.from_above
  48.2 0.0 collective-permute-done.3.from_below
  48.2 2.7 %shard_map.51 = (f32[8,2,128,128]{3,2,1,0:T(8,128)}, f32[8,1024]{1,0:T(8,128)S(1)}) custom-call(s32[2]{0:T(128)S(1)} %pad_add_fusion.place, f32[2,1,1024]{2,1,0:T(1,128)S(1)} %collective-permute-done.1.from_above, f32[2,1,1024]{2,1,0:T(1,128)S(1)} %collective-permute-done.3.from_below, ...), custom_call_target="tpu_custom_call", output_to_operand_aliasing={{0}: (4, {})} | custom-call | flops 268435456 | bytes 2211848 | tf_op jit(solution)/shard_map/pallas_call | solution.py:47
  50.9 0.0 all-to-all-done.1.got
  50.9 9.3 %all-to-all-start = ((f32[8,2,128,128]{3,2,1,0:T(8,128)}), f32[8,2,128,128]{3,2,1,0:T(8,128)S(1)}, u32[]{:S(2)}, u32[]{:S(2)}) async-start(f32[8,2,128,128]{3,2,1,0:T(8,128)} %get-tuple-element.14), calls=%async_computation | async-start | bytes 2097152 | tf_op jit(solution)/shard_map/all_to_all | solution.py:487
  60.2 2.3 %shard_map.53.spectral = f32[1024,256]{1,0:T(8,128)S(1)} custom-call(f32[8,2,128,128]{3,2,1,0:T(8,128)S(1)} %all-to-all-done.1.got), custom_call_target="tpu_custom_call" | custom-call | flops 1610612736 | bytes 2097152 | tf_op jit(solution)/shard_map/pallas_call | solution.py:47
  62.5 0.0 copy-start.7
  62.5 1.0 copy-done.7
  63.5 8.9 %all-to-all-done.got = f32[8,2,128,128]{3,2,1,0:T(8,128)S(1)} async-done(((f32[8,2,128,128]{3,2,1,0:T(8,128)}), f32[8,2,128,128]{3,2,1,0:T(8,128)S(1)}, u32[]{:S(2)}, u32[]{:S(2)}) %all-to-all-start) | async-done | bytes 1048608 | tf_op jit(solution)/shard_map/all_to_all | solution.py:487
  72.5 0.0 copy-start.8
  72.5 1.2 copy-done.8
  73.7 4.1 %shard_map.54 = f32[8,264,128]{2,1,0:T(8,128)S(1)} custom-call(f32[8,2,128,128]{3,2,1,0:T(8,128)S(1)} %all-to-all-done.got, f32[1024,256]{1,0:T(8,128)S(1)} %copy-done.8), custom_call_target="tpu_custom_call" | custom-call | flops 2415919104 | bytes 3178496 | tf_op jit(solution)/shard_map/pallas_call | solution.py:47
  77.8 19.5 %all_to_all.20.got = f32[8,264,128]{2,1,0:T(8,128)S(1)} all-to-all(f32[8,264,128]{2,1,0:T(8,128)S(1)} %shard_map.54), channel_id=1, replica_groups=mesh['planes_0'=4,'planes_1'=2,'planes_2'=2,'rows_0'=2,'rows_1'=4] {'row..., dimensions={0} | all-to-all | bytes 2162688 | tf_op jit(solution)/shard_map/all_to_all | solution.py:487
  97.3 2.3 %shard_map.55 = (f32[1,128,1024]{2,1,0:T(8,128)S(1)}, f32[128,1024]{1,0:T(8,128)S(1)}, f32[8,1024]{1,0:T(8,128)S(1)}) custom-call(f32[8,264,128]{2,1,0:T(8,128)S(1)} %all_to_all.20.got), custom_call_target="tpu_custom_call" | custom-call | flops 1610612736 | bytes 2162688 | tf_op jit(solution)/shard_map/pallas_call | solution.py:47
  99.6 1.9 %collective-permute-start.4 = (f32[1,128,1024]{2,1,0:T(8,128)S(1)}, f32[1,128,1024]{2,1,0:T(8,128)S(1)}, u32[]{:S(2)}, u32[]{:S(2)}) collective-permute-start(f32[1,128,1024]{2,1,0:T(8,128)S(1)} %get-tuple-element.20.residual), channel_id=1, source_target_pairs={{8,0},{16,8},{24,16},{32,24},{40,32},{48,40},{56,48},{64,56},{72,6... | collective-permute-start | bytes 1572872 | tf_op jit(solution)/shard_map/ppermute | solution.py:560
  101.5 14.3 %collective-permute-done.4.ahead = f32[1,128,1024]{2,1,0:T(8,128)S(1)} collective-permute-done((f32[1,128,1024]{2,1,0:T(8,128)S(1)}, f32[1,128,1024]{2,1,0:T(8,128)S(1)}, u32[]{:S(2)}, u32[]{:S(2)}) %collective-permute-start.4) | collective-permute-done | bytes 524320 | tf_op jit(solution)/shard_map/ppermute | solution.py:560
  115.9 1.9 %collective-permute-start.5 = (f32[1,128,1024]{2,1,0:T(8,128)S(1)}, f32[1,128,1024]{2,1,0:T(8,128)S(1)}, u32[]{:S(2)}, u32[]{:S(2)}) collective-permute-start(f32[1,128,1024]{2,1,0:T(8,128)S(1)} %get-tuple-element.20.residual), channel_id=1, source_target_pairs={{0,8},{8,16},{16,24},{24,32},{32,40},{40,48},{48,56},{56,64},{64,7... | collective-permute-start | bytes 1572872 | tf_op jit(solution)/shard_map/ppermute | solution.py:565
  117.8 0.9 shard_map.56.parts
  118.7 1.4 shard_map.57
  120.1 11.2 %all-to-all-start.3 = ((f32[128,1,128]{2,1,0:T(1,128)}), f32[128,1,128]{2,1,0:T(1,128)S(1)}, u32[]{:S(2)}, u32[]{:S(2)}) async-start(f32[128,1,128]{2,1,0:T(1,128)} %shard_map.57), calls=%async_computation.3 | async-start | bytes 131072 | tf_op jit(solution)/shard_map/all_to_all | solution.py:487
  131.2 0.0 collective-permute-done.5.behind
  131.2 0.0 copy-start.4
  131.3 0.8 copy-done.4
  132.0 0.0 copy-start.3
  132.0 1.0 copy-done.3
  133.1 0.0 copy-start.5
  133.1 1.0 copy-done.5
  134.1 0.0 copy-start.1
  134.1 1.3 shard_map.58.image
  135.4 5.7 %all-to-all-done.3.sums = f32[128,1,128]{2,1,0:T(1,128)S(1)} async-done(((f32[128,1,128]{2,1,0:T(1,128)}), f32[128,1,128]{2,1,0:T(1,128)S(1)}, u32[]{:S(2)}, u32[]{:S(2)}) %all-to-all-start.3) | async-done | bytes 65568 | tf_op jit(solution)/shard_map/all_to_all | solution.py:487
  141.1 0.0 copy-done.1
  141.1 1.3 shard_map.59
  (5 shorter events, 0.0 us)
Async XLA Ops:
  4.6 8.5 %copy-start = (f32[1,128,1024]{2,1,0:T(8,128)S(1)}, f32[1,128,1024]{2,1,0:T(8,128)}, u32[]{:S(2)}) copy-start(f32[1,128,1024]{2,1,0:T(8,128)} %estimate.5) | copy-start | bytes 1572868
  4.7 46.3 %all-to-all-start.1 = ((f32[8,2,128,128]{3,2,1,0:T(8,128)}), f32[8,2,128,128]{3,2,1,0:T(8,128)S(1)}, u32[]{:S(2)}, u32[]{:S(2)}) async-start(f32[8,2,128,128]{3,2,1,0:T(8,128)} %shard_map.52), calls=%async_computation.1 | async-start | bytes 2097152 | tf_op jit(solution)/shard_map/all_to_all | solution.py:487
  13.1 23.9 %collective-permute-start = (f32[1,128,1024]{2,1,0:T(8,128)S(1)}, f32[1,128,1024]{2,1,0:T(8,128)S(1)}, u32[]{:S(2)}, u32[]{:S(2)}) collective-permute-start(f32[1,128,1024]{2,1,0:T(8,128)S(1)} %copy-done), channel_id=1, source_target_pairs={{8,0},{16,8},{24,16},{32,24},{40,32},{48,40},{56,48},{64,56},{72,6... | collective-permute-start | bytes 1572872 | tf_op jit(solution)/shard_map/ppermute | solution.py:505
  16.0 24.5 %collective-permute-start.2 = (f32[1,128,1024]{2,1,0:T(8,128)S(1)}, f32[1,128,1024]{2,1,0:T(8,128)S(1)}, u32[]{:S(2)}, u32[]{:S(2)}) collective-permute-start(f32[1,128,1024]{2,1,0:T(8,128)S(1)} %copy-done), channel_id=1, source_target_pairs={{0,8},{8,16},{16,24},{24,32},{32,40},{40,48},{48,56},{56,64},{64,7... | collective-permute-start | bytes 1572872 | tf_op jit(solution)/shard_map/ppermute | solution.py:504
  37.1 11.1 %collective-permute-start.1 = (f32[2,1,1024]{2,1,0:T(1,128)S(1)}, f32[2,1,1024]{2,1,0:T(1,128)S(1)}, u32[]{:S(2)}, u32[]{:S(2)}) collective-permute-start(f32[2,1,1024]{2,1,0:T(1,128)S(1)} %pad_maximum_fusion), channel_id=1, source_target_pairs={{0,1},{1,2},{2,3},{3,4},{4,5},{5,6},{6,7},{8,9},{9,10},{10,11},{11... | collective-permute-start | bytes 24584 | tf_op jit(solution)/shard_map/ppermute | solution.py:518
  40.5 7.7 %collective-permute-start.3 = (f32[2,1,1024]{2,1,0:T(1,128)S(1)}, f32[2,1,1024]{2,1,0:T(1,128)S(1)}, u32[]{:S(2)}, u32[]{:S(2)}) collective-permute-start(f32[2,1,1024]{2,1,0:T(1,128)S(1)} %pad_maximum_fusion.1), channel_id=1, source_target_pairs={{1,0},{2,1},{3,2},{4,3},{5,4},{6,5},{7,6},{9,8},{10,9},{11,10},{12... | collective-permute-start | bytes 24584 | tf_op jit(solution)/shard_map/ppermute | solution.py:519
  41.8 1.0 copy-start.6
  47.4 0.8 copy-start.2
  50.9 21.5 %all-to-all-start = ((f32[8,2,128,128]{3,2,1,0:T(8,128)}), f32[8,2,128,128]{3,2,1,0:T(8,128)S(1)}, u32[]{:S(2)}, u32[]{:S(2)}) async-start(f32[8,2,128,128]{3,2,1,0:T(8,128)} %get-tuple-element.14), calls=%async_computation | async-start | bytes 2097152 | tf_op jit(solution)/shard_map/all_to_all | solution.py:487
  62.5 1.0 copy-start.7
  72.5 1.2 copy-start.8
  99.6 16.2 %collective-permute-start.4 = (f32[1,128,1024]{2,1,0:T(8,128)S(1)}, f32[1,128,1024]{2,1,0:T(8,128)S(1)}, u32[]{:S(2)}, u32[]{:S(2)}) collective-permute-start(f32[1,128,1024]{2,1,0:T(8,128)S(1)} %get-tuple-element.20.residual), channel_id=1, source_target_pairs={{8,0},{16,8},{24,16},{32,24},{40,32},{48,40},{56,48},{64,56},{72,6... | collective-permute-start | bytes 1572872 | tf_op jit(solution)/shard_map/ppermute | solution.py:560
  115.9 15.4 %collective-permute-start.5 = (f32[1,128,1024]{2,1,0:T(8,128)S(1)}, f32[1,128,1024]{2,1,0:T(8,128)S(1)}, u32[]{:S(2)}, u32[]{:S(2)}) collective-permute-start(f32[1,128,1024]{2,1,0:T(8,128)S(1)} %get-tuple-element.20.residual), channel_id=1, source_target_pairs={{0,8},{8,16},{16,24},{24,32},{32,40},{40,48},{48,56},{56,64},{64,7... | collective-permute-start | bytes 1572872 | tf_op jit(solution)/shard_map/ppermute | solution.py:565
  120.1 21.0 %all-to-all-start.3 = ((f32[128,1,128]{2,1,0:T(1,128)}), f32[128,1,128]{2,1,0:T(1,128)S(1)}, u32[]{:S(2)}, u32[]{:S(2)}) async-start(f32[128,1,128]{2,1,0:T(1,128)} %shard_map.57), calls=%async_computation.3 | async-start | bytes 131072 | tf_op jit(solution)/shard_map/all_to_all | solution.py:487
  131.2 0.8 copy-start.4
  132.0 1.0 copy-start.3
  133.1 1.0 copy-start.5
  134.1 6.9 %copy-start.1 = (f32[1,128,1024]{2,1,0:T(8,128)S(1)}, f32[1,128,1024]{2,1,0:T(8,128)}, u32[]{:S(2)}) copy-start(f32[1,128,1024]{2,1,0:T(8,128)} %estimate.5) | copy-start | bytes 1572868

commit v4 on v3

--- a/solution.py
+++ b/solution.py
@@ -11,12 +11,12 @@
 
 PLANES = ("planes_0", "planes_1", "planes_2")
 ROWS = ("rows_0", "rows_1")
-ALL = PLANES + ROWS
 N = 1024
 R = 128
 G = 8
-SECOND = R + 8
-BOTH = 2 * R + 8
+EDGE = R + 8
+REG = R + 16
+FULL = 2 * R + 16
 HUBER_EDGE = 0.5
 SMOOTHING = 0.3
 F32 = jnp.float32
@@ -153,18 +153,20 @@
 
 
 def first_kernel(
-    observed, estimate, sent,
-    table_v, observed_v, estimate_v, sent_v, high, low, stack, sems,
+    observed, estimate, spectrum, sent,
+    table_v, observed_v, estimate_v, spectrum_v, sent_v, high, low, stack, sems,
 ):
     copies = [
         start(observed.at[0], observed_v, sems.at[1]),
         start(estimate.at[0], estimate_v, sems.at[2]),
+        start(spectrum.at[0], spectrum_v, sems.at[3]),
     ]
     fill_table(table_v, True)
     copies[0].wait()
     stack[0:R, :], stack[2 * R : 3 * R, :] = split(observed_v[...])
     copies[1].wait()
     stack[R : 2 * R, :], stack[3 * R : 4 * R, :] = split(estimate_v[...])
+    copies[2].wait()
     out_copies = []
     for d in range(G // 2):
         columns = slice(256 * d, 256 * d + 256)
@@ -175,6 +177,7 @@
             e = 2 * d + h
             sent_v[e, 0] = out[:R, lanes]
             sent_v[e, 1] = out[R:, lanes]
+            sent_v[e, 2] = spectrum_v[:, 128 * e : 128 * e + 128]
         out_copies.append(
             start(sent_v.at[2 * d : 2 * d + 2], sent.at[2 * d : 2 * d + 2], sems.at[4 + d])
         )
@@ -205,12 +208,11 @@
 
 
 def weights_kernel(
-    place, estimate, behind, ahead, spectrum,
-    sent, w_all, w_back_all, strip,
-    table_v, ext, ext_back, spectrum_v, sent_v, ext_w,
+    place, estimate, behind, ahead,
+    sent, reg, w_all, w_back_all, strip,
+    table_v, ext, ext_back, sent_v, ext_w,
     high, low, stack, sems,
 ):
-    spectrum_copy = start(spectrum.at[0], spectrum_v, sems.at[0])
     fill_table(table_v, True)
     ok_plane = jnp.where(place[0] < 15, 1.0, 0.0)
     ok_back = jnp.where(place[0] > 0, 1.0, 0.0)
@@ -249,6 +251,7 @@
             ext_w[7 + c : 7 + c + CHUNK, :],
             jnp.where(last, 0.0, w),
         )
+        reg[c : c + CHUNK, :] = out
         stack[c : c + CHUNK, :], stack[R + c : R + c + CHUNK, :] = split(out)
     for i, rows in enumerate((
         estimate[0, 0:2, :], estimate[0, R - 2 : R, :], ahead[0, 0:1, :], ahead[0, R - 1 : R, :],
@@ -257,7 +260,6 @@
     )):
         at = 2 * i if i < 2 else i + 2
         strip[at : at + rows.shape[0], :] = rows
-    spectrum_copy.wait()
     out_copies = []
     for d in range(G // 2):
         columns = slice(256 * d, 256 * d + 256)
@@ -265,10 +267,9 @@
         out = stacked_times(stack, R, high, low, columns)
         for h in range(2):
             e = 2 * d + h
-            sent_v[e, 0] = spectrum_v[:, 128 * e : 128 * e + 128]
-            sent_v[e, 1] = out[:, 128 * h : 128 * h + 128]
+            sent_v[e] = out[:, 128 * h : 128 * h + 128]
         out_copies.append(
-            start(sent_v.at[2 * d : 2 * d + 2], sent.at[2 * d : 2 * d + 2], sems.at[1 + d])
+            start(sent_v.at[2 * d : 2 * d + 2], sent.at[2 * d : 2 * d + 2, REG:], sems.at[1 + d])
         )
     for copy in out_copies:
         copy.wait()
@@ -276,7 +277,7 @@
 
 def edge_kernel(
     place, from_above, from_below, strip, half_sent, sent, w_edge,
-    table_v, high, low, stack, rows_v, sems,
+    table_v, high, low, stack, rows_v, tiles_v, sems,
 ):
     fill_table(table_v, True)
     plane, row = place[0], place[1]
@@ -310,6 +311,11 @@
         tail, line(5), line(7), bottom, before,
         w_tail * ok_plane, w_back_tail, w_tail, line(9), jnp.where(last, 0.0, w_tail),
     )
+    w_edge[3:4, :], w_edge[4:5, :] = first_row, last_row
+    head_tile, tail_tile = as_tile(first_row), as_tile(last_row)
+    for e in range(G):
+        tiles_v[e] = jnp.where(row == e - 1, tail_tile, jnp.where(row == e + 1, head_tile, 0.0))
+    tile_copy = start(tiles_v, sent.at[:, EDGE:REG], sems.at[16])
     pair = jnp.concatenate([first_row, last_row, jnp.zeros((14, N), F32)], axis=0)
     stack[0:16, :], stack[16:32, :] = split(pair)
     out_copies = []
@@ -322,73 +328,106 @@
             rows_v[e] = out[0:8, 128 * h : 128 * h + 128]
             for i, at in enumerate((0, R - 1)):
                 out_copies.append(
-                    start(rows_v.at[e, i : i + 1], sent.at[e, 1, at : at + 1], sems.at[2 * e + i])
+                    start(rows_v.at[e, i : i + 1], sent.at[e, REG + at : REG + at + 1], sems.at[2 * e + i])
                 )
+    tile_copy.wait()
     for copy in out_copies:
         copy.wait()
 
 
-def forward_kernel(got, spectral, table_v, high, low, pair):
-    fill_table(table_v, False)
+def middle_kernel(
+    got, half_sent, sent, spectral, freq_v, sample_v, sent_v, f_high, f_low, s_high, s_low, pair,
+    sems,
+):
+    fill_table(freq_v, False)
+    fill_table(sample_v, True)
     for d in range(G):
         rows = slice(R * d, R * d + R)
         pair[rows, 0:128], pair[rows, 256:384] = split(got[d, 0])
         pair[rows, 128:256], pair[rows, 384:512] = split(got[d, 1])
+        sent_v[d, R:] = jnp.zeros((8, 128), F32)
     for m in range(4):
         rows = slice(256 * m, 256 * m + 256)
-        build_freqs(table_v, high, low, rows)
-        spectral[rows, :] = matrix_times(high, low, rows, pair, 256)
-
-
-def middle_kernel(
-    got, spectral, sent, freq_v, sample_v, f_high, f_low, s_high, s_low, pair,
+        build_freqs(freq_v, f_high, f_low, rows)
+        out = matrix_times(f_high, f_low, rows, pair, 256)
+        gain = jnp.concatenate([got[2 * m, 2], got[2 * m + 1, 2]], axis=0)
+        value = gain * (out[:, :128] - gain * out[:, 128:])
+        spectral[rows, :128] = value
+        spectral[rows, 128:] = gain
+        pair[rows, 512:640], pair[rows, 640:768] = split(value)
+    out_copies = []
+    for m in range(4):
+        rows = slice(256 * m, 256 * m + 256)
+        build_samples(sample_v, s_high, s_low, rows)
+        out = matrix_times(s_high, s_low, rows, pair, 128, 512)
+        for h in range(2):
+            d = 2 * m + h
+            block = out[R * h : R * h + R]
+            sent_v[d, 0:R] = block
+            if d + 1 < G:
+                sent_v[d + 1, R : R + 1] = block[R - 1 : R]
+            if d > 0:
+                sent_v[d - 1, R + 1 : R + 2] = block[0:1]
+                out_copies.append(start(sent_v.at[d - 1], sent.at[d - 1, 0:EDGE], sems.at[d]))
+    out_copies.append(start(sent_v.at[G - 1], sent.at[G - 1, 0:EDGE], sems.at[0]))
+    for copy in out_copies:
+        copy.wait()
+
+
+def residual_kernel(
+    place, got, reg, w_edge, residual, edges, table_v, rows_v, f_high, f_low, stack,
+):
+    row = place[1]
+    fill_table(table_v, False)
+    above = got[jnp.maximum(row - 1, 0), EDGE:REG, :]
+    below = got[jnp.minimum(row + 1, G - 1), EDGE:REG, :]
+    for i in range(G):
+        rows_v[0:1, 128 * i : 128 * i + 128] = above[i : i + 1]
+        rows_v[1:2, 128 * i : 128 * i + 128] = below[i : i + 1]
+    rows = R + 16
+    for d in range(G):
+        lanes = slice(128 * d, 128 * d + 128)
+        stack[0:rows, lanes], stack[rows : 2 * rows, lanes] = split(got[d, 0:rows])
+    for d in range(G // 2):
+        lanes = slice(256 * d, 256 * d + 256)
+        build_freqs(table_v, f_high, f_low, WHOLE, lanes)
+        out = stacked_times(stack, rows, f_high, f_low, lanes)
+        residual[0, :, lanes] = out[:R] - reg[:, lanes]
+        residual[0, 0:1, lanes] = out[0:1] - w_edge[3:4, lanes]
+        residual[0, R - 1 : R, lanes] = out[R - 1 : R] - w_edge[4:5, lanes]
+        edges[0:2, lanes] = out[R : R + 2] - rows_v[0:2, lanes]
+
+
+def curvature_kernel(
+    got, spectral, sent, total, freq_v, sample_v, sent_v, f_high, f_low, s_high, s_low, pair, sems,
 ):
     fill_table(freq_v, False)
     fill_table(sample_v, True)
     for d in range(G):
         rows = slice(R * d, R * d + R)
-        pair[rows, 0:128], pair[rows, 128:256] = split(got[d, 1])
+        pair[rows, 0:128], pair[rows, 128:256] = split(got[d, REG:])
+    acc = jnp.zeros((8, 128), F32)
     for m in range(4):
         rows = slice(256 * m, 256 * m + 256)
         build_freqs(freq_v, f_high, f_low, rows)
-        reg = matrix_times(f_high, f_low, rows, pair, 128)
-        gain = jnp.concatenate([got[2 * m, 0], got[2 * m + 1, 0]], axis=0)
-        value = gain * (spectral[rows, :128] - gain * spectral[rows, 128:]) - reg
-        pair[rows, 256:384], pair[rows, 512:640] = split(value)
-        pair[rows, 384:512], pair[rows, 640:768] = split(gain * gain * value)
-    for d in range(G):
-        sent[d, R:SECOND] = jnp.zeros((8, 128), F32)
+        out = spectral[rows, :128] - matrix_times(f_high, f_low, rows, pair, 128)
+        gain = spectral[rows, 128:]
+        scaled = gain * gain * out
+        acc += jnp.sum((scaled * out).reshape(32, 8, 128), axis=0)
+        pair[rows, 256:384], pair[rows, 384:512] = split(scaled)
+    total[...] = acc
+    out_copies = []
     for m in range(4):
         rows = slice(256 * m, 256 * m + 256)
         build_samples(sample_v, s_high, s_low, rows)
-        out = matrix_times(s_high, s_low, rows, pair, 256, 256)
-        for h in range(2):
-            d = 2 * m + h
-            block = out[R * h : R * h + R]
-            sent[d, 0:R] = block[:, :128]
-            sent[d, SECOND:] = block[:, 128:]
-            if d + 1 < G:
-                sent[d + 1, R : R + 1] = block[R - 1 : R, :128]
-            if d > 0:
-                sent[d - 1, R + 1 : R + 2] = block[0:1, :128]
-
-
-def residual_kernel(got, residual, image, edges, table_v, f_high, f_low, stack):
-    fill_table(table_v, False)
-    rows = BOTH + 8
-    pad = jnp.zeros((8, 128), BF16)
-    for d in range(G):
-        lanes = slice(128 * d, 128 * d + 128)
-        high, low = split(got[d])
-        stack[0:rows, lanes] = jnp.concatenate([high, pad], axis=0)
-        stack[rows : 2 * rows, lanes] = jnp.concatenate([low, pad], axis=0)
-    for d in range(G // 2):
-        lanes = slice(256 * d, 256 * d + 256)
-        build_freqs(table_v, f_high, f_low, WHOLE, lanes)
-        out = stacked_times(stack, rows, f_high, f_low, lanes)
-        residual[0, :, lanes] = out[:R]
-        edges[0:2, lanes] = out[R : R + 2]
-        image[:, lanes] = out[SECOND:BOTH]
+        out = matrix_times(s_high, s_low, rows, pair, 128, 256)
+        sent_v[2 * m] = out[:R]
+        sent_v[2 * m + 1] = out[R:]
+        out_copies.append(
+            start(sent_v.at[2 * m : 2 * m + 2], sent.at[2 * m : 2 * m + 2, 0:R], sems.at[m])
+        )
+    for copy in out_copies:
+        copy.wait()
 
 
 def patched(weights, w_edge, c, line):
@@ -405,7 +444,7 @@
     ext[8 + R : 9 + R, :] = jnp.where(place[1] < G - 1, edges[1:2, :], residual[0, R - 1 : R, :])
 
 
-def partial_kernel(place, residual, edges, w_all, w_edge, image, parts, ext):
+def partial_kernel(place, residual, edges, w_all, w_edge, parts, ext):
     extend(place, residual, edges, ext)
     last = lax.broadcasted_iota(jnp.int32, (CHUNK, N), 1) == N - 1
     norm = jnp.zeros((8, N), F32)
@@ -415,7 +454,6 @@
         row = ext[9 + c : 9 + c + CHUNK, :] - value
         column = jnp.where(last, 0.0, left(value) - value)
         cross = (SMOOTHING * patched(w_all, w_edge, c, 1)) * (row * row + column * column)
-        cross += value * image[c : c + CHUNK, :]
         square = value * value
         norm += square[:8] + square[8:]
         product += cross[:8] + cross[8:]
@@ -423,24 +461,26 @@
     parts[1] = product
 
 
-def product_kernel(place, residual, ahead, w_all, w_edge, parts, sent):
-    total = jnp.zeros((8, N), F32)
+def product_kernel(
+    place, residual, ahead, w_all, w_edge, parts, total, half, sent, tile_v, sems,
+):
+    acc = jnp.zeros((8, N), F32)
     for c in range(0, R, CHUNK):
         plane = ahead[0, c : c + CHUNK, :] - residual[0, c : c + CHUNK, :]
         cross = patched(w_all, w_edge, c, 1) * (plane * plane)
-        total += cross[:8] + cross[8:]
-    product = parts[1] + jnp.where(place[0] < 15, SMOOTHING, 0.0) * total
+        acc += cross[:8] + cross[8:]
+    product = parts[1] + jnp.where(place[0] < 15, SMOOTHING, 0.0) * acc
     norm = jnp.sum(as_tile(jnp.sum(parts[0], axis=0, keepdims=True)), axis=0, keepdims=True)
-    product = jnp.sum(as_tile(jnp.sum(product, axis=0, keepdims=True)), axis=0, keepdims=True)
-    lane = lax.broadcasted_iota(jnp.int32, (1, 128), 1)
-    both = jnp.where(
-        lane < 64, norm + pltpu.roll(norm, 64, 1), product + pltpu.roll(product, 64, 1)
-    )
-    sent[...] = jnp.broadcast_to(both[None], (128, 1, 128))
+    product = as_tile(jnp.sum(product, axis=0, keepdims=True)) + total[...]
+    product = jnp.sum(product, axis=0, keepdims=True)
+    tile_v[...] = jnp.concatenate([norm, product, jnp.zeros((6, 128), F32)], axis=0)
+    out_copies = [start(tile_v, sent.at[d, R:], sems.at[d]) for d in range(G)]
+    for copy in out_copies:
+        copy.wait()
 
 
 def inner_kernel(
-    place, residual, behind, ahead, edges, w_all, w_back_all, w_edge, blurred, image, ext, ext_w,
+    place, residual, behind, ahead, edges, w_all, w_back_all, w_edge, image, ext, ext_w,
 ):
     ok_plane = jnp.where(place[0] < 15, 1.0, 0.0)
     extend(place, residual, edges, ext)
@@ -450,7 +490,7 @@
     last = lax.broadcasted_iota(jnp.int32, (CHUNK, N), 1) == N - 1
     for c in range(0, R, CHUNK):
         w = ext_w[8 + c : 8 + c + CHUNK, :]
-        image[c : c + CHUNK, :] = blurred[c : c + CHUNK, :] + divergence(
+        image[c : c + CHUNK, :] = divergence(
             ext[8 + c : 8 + c + CHUNK, :],
             ahead[0, c : c + CHUNK, :],
             behind[0, c : c + CHUNK, :],
@@ -465,20 +505,25 @@
 
 
 def last_kernel(
-    sums, estimate, residual, image, restored, final, restored_v, final_v, sems,
-):
-    both = jnp.sum(sums[...], axis=0)
-    lane = lax.broadcasted_iota(jnp.int32, (1, 128), 1)
-    norm = jnp.sum(jnp.where(lane < 64, both, 0.0), axis=1, keepdims=True)
-    product = jnp.sum(jnp.where(lane < 64, 0.0, both), axis=1, keepdims=True)
+    sums, got, reg, residual, estimate, restored, final,
+    table_v, restored_v, final_v, f_high, f_low, stack, sems,
+):
+    fill_table(table_v, False)
+    for d in range(G):
+        lanes = slice(128 * d, 128 * d + 128)
+        stack[0:R, lanes], stack[R : 2 * R, lanes] = split(got[d, 0:R])
+    tile = jnp.sum(sums[...], axis=0)
+    norm = jnp.sum(tile[0:1, :], axis=1, keepdims=True)
+    product = jnp.sum(tile[1:2, :], axis=1, keepdims=True)
     step = norm / product
-    out_copies = []
-    for c in range(4):
-        rows = slice(32 * c, 32 * c + 32)
-        restored_v[rows] = estimate[0, rows] + step * residual[0, rows]
-        out_copies.append(start(restored_v.at[rows], restored.at[0, rows], sems.at[2 * c]))
-        final_v[rows] = residual[0, rows] - step * image[rows]
-        out_copies.append(start(final_v.at[rows], final.at[0, rows], sems.at[2 * c + 1]))
+    restored_v[...] = estimate[0] + step * residual[0]
+    out_copies = [start(restored_v, restored.at[0], sems.at[4])]
+    for d in range(G // 2):
+        lanes = slice(256 * d, 256 * d + 256)
+        build_freqs(table_v, f_high, f_low, WHOLE, lanes)
+        image = stacked_times(stack, R, f_high, f_low, lanes) + reg[:, lanes]
+        final_v[:, lanes] = residual[0, :, lanes] - step * image
+        out_copies.append(start(final_v.at[:, lanes], final.at[0, :, lanes], sems.at[d]))
     for copy in out_copies:
         copy.wait()
 
@@ -505,79 +550,86 @@
     ahead = lax.ppermute(estimate, PLANES, down)
     sent = call(
         first_kernel,
-        (shape(G, 2, R, 128),),
+        (shape(G, 3, R, 128),),
         6 * big,
-        (TABLE, field(), field(), pltpu.VMEM((G, 2, R, 128), F32), MATRIX, MATRIX,
+        (TABLE, field(), field(), field(), pltpu.VMEM((G, 3, R, 128), F32), MATRIX, MATRIX,
          pltpu.VMEM((4 * R, N), BF16), DMA((8,))),
         (ANY,), limit=60,
-    )(observed, estimate)[0]
+    )(observed, estimate, spectrum)[0]
     first = across(sent, ROWS)
 
     tails = jnp.concatenate([estimate[:, R - 1 :], ahead[:, R - 1 :]], axis=0)
     heads = jnp.concatenate([estimate[:, :1], behind[:, :1]], axis=0)
     from_above = lax.ppermute(tails, ROWS, row_up)
     from_below = lax.ppermute(heads, ROWS, row_down)
-    half_sent, w_all, w_back, strip = call(
+    wide = shape(G, FULL, 128)
+    half_sent, reg, w_all, w_back, strip = call(
         weights_kernel,
-        (shape(G, 2, R, 128), block, block, shape(16, N)),
+        (wide, block, block, block, shape(16, N)),
         3 * big,
-        (TABLE, field(R + 16), field(R + 8), field(), pltpu.VMEM((G, 2, R, 128), F32),
+        (TABLE, field(R + 16), field(R + 8), pltpu.VMEM((G, R, 128), F32),
          field(R + 16), MATRIX, MATRIX, pltpu.VMEM((2 * R, N), BF16), DMA((5,))),
-        (ANY, VMEM, VMEM, VMEM), direct=4,
-    )(place, estimate, behind, ahead, spectrum)
-    sent, w_edge = call(
+        (ANY, VMEM, VMEM, VMEM, VMEM), direct=4,
+    )(place, estimate, behind, ahead)
+    half_sent, w_edge = call(
         edge_kernel,
-        (shape(G, 2, R, 128), shape(8, N)),
+        (wide, shape(8, N)),
         big,
         (TABLE, MATRIX, MATRIX, pltpu.VMEM((32, N), BF16), pltpu.VMEM((G, 8, 128), F32),
-         DMA((16,))),
+         pltpu.VMEM((G, 8, 128), F32), DMA((17,))),
         (ANY, VMEM), {4: 0}, direct=4,
     )(place, from_above, from_below, strip, half_sent)
+    sent, spectral = call(
+        middle_kernel,
+        (wide, shape(N, 256)),
+        9 * big,
+        (TABLE, TABLE, pltpu.VMEM((G, EDGE, 128), F32), MATRIX, MATRIX, MATRIX, MATRIX,
+         pltpu.VMEM((N, 768), BF16), DMA((8,))),
+        (ANY, VMEM), {1: 0}, direct=1,
+    )(first, half_sent)
     second = across(sent, ROWS)
-    spectral = call(
-        forward_kernel,
-        (shape(N, 256),),
-        6 * big,
-        (TABLE, MATRIX, MATRIX, pltpu.VMEM((N, 512), BF16)),
+
+    residual, edges = call(
+        residual_kernel,
+        (shape(1, R, N), shape(8, N)),
+        3 * big,
+        (TABLE, field(8), MATRIX, MATRIX, pltpu.VMEM((2 * R + 32, N), BF16)),
         direct=9,
-    )(first)[0]
-    sent = call(
-        middle_kernel,
-        (shape(G, BOTH, 128),),
-        9 * big,
-        (TABLE, TABLE, MATRIX, MATRIX, MATRIX, MATRIX, pltpu.VMEM((N, 768), BF16)),
-        direct=9,
-    )(second, spectral)[0]
-    third = across(sent, ROWS)
-
-    residual, blurred, edges = call(
-        residual_kernel,
-        (shape(1, R, N), block, shape(8, N)),
-        6 * big,
-        (TABLE, MATRIX, MATRIX, pltpu.VMEM((2 * BOTH + 16, N), BF16)),
-        direct=9,
-    )(third)
+    )(place, second, reg, w_edge)
     ahead = lax.ppermute(residual, PLANES, down)
     parts = call(
         partial_kernel, (shape(2, 8, N),), big // 16, (field(R + 16),), direct=9
-    )(place, residual, edges, w_all, w_edge, blurred)[0]
+    )(place, residual, edges, w_all, w_edge)[0]
+    half_sent, total = call(
+        curvature_kernel,
+        (shape(G, EDGE, 128), shape(8, 128)),
+        6 * big,
+        (TABLE, TABLE, pltpu.VMEM((G, R, 128), F32), MATRIX, MATRIX, MATRIX, MATRIX,
+         pltpu.VMEM((N, 512), BF16), DMA((4,))),
+        (ANY, VMEM), direct=2,
+    )(second, spectral)
     late, _ = lax.optimization_barrier((residual, ahead))
     behind = lax.ppermute(late, PLANES, up)
     sent = call(
-        product_kernel, (shape(128, 1, 128),), big // 64, direct=9
-    )(place, residual, ahead, w_all, w_edge, parts)[0]
-    sums = across(sent, ALL)
-    image = call(
+        product_kernel,
+        (shape(G, EDGE, 128),),
+        big // 64,
+        (pltpu.VMEM((8, 128), F32), DMA((8,))),
+        (ANY,), {7: 0}, direct=7,
+    )(place, residual, ahead, w_all, w_edge, parts, total, half_sent)[0]
+    third = across(sent, ROWS)
+    reg_residual = call(
         inner_kernel, (block,), big // 16, (field(R + 16), field(R + 16)), direct=9
-    )(place, residual, behind, ahead, edges, w_all, w_back, w_edge, blurred)[0]
+    )(place, residual, behind, ahead, edges, w_all, w_back, w_edge)[0]
+    tile = jnp.sum(third[:, R:], axis=0)
+    sums = across(jnp.broadcast_to(tile[None], (planes, 8, 128)), PLANES)
     return call(
         last_kernel,
         (shape(1, R, N), shape(1, R, N)),
-        R * N * 4,
-        (field(), field(), DMA((8,))),
-        (ANY, ANY),
-        direct=9,
-    )(sums, estimate, residual, image)
+        3 * big,
+        (TABLE, field(), field(), MATRIX, MATRIX, pltpu.VMEM((2 * R, N), BF16), DMA((5,))),
+        (ANY, ANY), direct=9,
+    )(sums, third, reg_residual, residual, estimate)
 
 
 def solution(mesh):

time: 143 us -> 140 us (0.979)
  starting transfers between devices: 42.9 us -> 34.6 us
  Pallas kernels: 24.8 us -> 29.5 us
  waiting for transfers between devices: 47.2 us -> 43.2 us
  local copies, waits for them, and re-layouts: 6.93 us -> 9.81 us
  blocking collectives: 19.5 us -> 21.4 us
    all_to_all x3, starting transfers between devices: 28.9 us -> 20.1 us  [across(): return lax.all_to_all(x, axes, split_axis=0, concat_axis=0, tiled=True)]
    ppermute x1, waiting for transfers between devices: 14.3 us -> 8.69 us  [step(): ahead = lax.ppermute(residual, PLANES, down)]
    ppermute x1, waiting for transfers between devices: 18.3 us -> 23.9 us  [step(): ahead = lax.ppermute(estimate, PLANES, down)]
    pallas_call x10, Pallas kernels: 24.8 us -> 29.5 us  [launch(): pl.pallas_call(body, out_shape=tuple(outs), in_specs=[place_of(i, a) for...]
    all_to_all x3, waiting for transfers between devices: 14.6 us -> 10.6 us  [across(): return lax.all_to_all(x, axes, split_axis=0, concat_axis=0, tiled=True)]
    unnamed x18 -> x26, local copies, waits for them, and re-layouts: 6.91 us -> 9.17 us
    all_to_all x1, blocking collectives: 19.5 us -> 21.4 us  [across(): return lax.all_to_all(x, axes, split_axis=0, concat_axis=0, tiled=True)]
  transfers between devices with their start and end apart: 9 -> 9, of which waited for: 4 -> 4; matrix products, arithmetic and copies ran while one was open for 0% -> 1% of each run, Pallas kernels for 9% -> 10%
where the time goes in v4:
time: 140 us
  waiting for transfers between devices  43.2 us (31%)
  starting transfers between devices  34.6 us (25%)
  Pallas kernels  29.5 us (21%)
  blocking collectives  21.4 us (15%)
  local copies, waits for them, and re-layouts  9.81 us (7%)
    pallas_call x10, Pallas kernels, launch(): pl.pallas_call(body, out_shape=tuple(outs), in_specs=[place_of(i, a) for...  29.5 us
    ppermute x1, waiting for transfers between devices, step(): ahead = lax.ppermute(estimate, PLANES, down)  23.9 us
    all_to_all x1, blocking collectives, across(): return lax.all_to_all(x, axes, split_axis=0, concat_axis=0, tiled=True)  21.4 us
    all_to_all x3, starting transfers between devices, across(): return lax.all_to_all(x, axes, split_axis=0, concat_axis=0, tiled=True)  20.1 us
    all_to_all x3, waiting for transfers between devices, across(): return lax.all_to_all(x, axes, split_axis=0, concat_axis=0, tiled=True)  10.6 us
    unnamed x26, local copies, waits for them, and re-layouts  9.17 us
    ppermute x1, waiting for transfers between devices, step(): ahead = lax.ppermute(residual, PLANES, down)  8.69 us
    ppermute x1, starting transfers between devices, step(): from_above = lax.ppermute(tails, ROWS, row_up)  3.37 us
  transfers between devices with their start and end apart: 9, of which 4 were waited for; matrix products, arithmetic and copies ran while one was open for 1% of the time, Pallas kernels for 10%

profile of v4, /device:TPU:1, one launch (start us, length us, event | category | flops | bytes accessed | tf_op | source)
XLA Modules:
  0.0 139.6 jit_solution(12757950895853808590)
XLA Ops:
  0.6 4.3 %shard_map.50 = f32[8,3,128,128]{3,2,1,0:T(8,128)} custom-call(f32[1,128,1024]{2,1,0:T(8,128)} %observed.1, f32[1,128,1024]{2,1,0:T(8,128)} %estimate.5, f32[1,128,1024]{2,1,0:T(8,128)} %spectrum.1), custom_call_target="tpu_custom_call" | custom-call | flops 1610612736 | bytes 3145728 | tf_op jit(solution)/shard_map/pallas_call | solution.py:47
  4.9 0.0 copy-start.4
  4.9 8.4 %all-to-all-start = ((f32[8,3,128,128]{3,2,1,0:T(8,128)}), f32[8,3,128,128]{3,2,1,0:T(8,128)S(1)}, u32[]{:S(2)}, u32[]{:S(2)}) async-start(f32[8,3,128,128]{3,2,1,0:T(8,128)} %shard_map.50), calls=%async_computation | async-start | bytes 3145728 | tf_op jit(solution)/shard_map/all_to_all | solution.py:532
  13.4 2.9 %collective-permute-start = (f32[1,128,1024]{2,1,0:T(8,128)S(1)}, f32[1,128,1024]{2,1,0:T(8,128)S(1)}, u32[]{:S(2)}, u32[]{:S(2)}) collective-permute-start(f32[1,128,1024]{2,1,0:T(8,128)S(1)} %copy-done.4), channel_id=1, source_target_pairs={{8,0},{16,8},{24,16},{32,24},{40,32},{48,40},{56,48},{64,56},{72,6... | collective-permute-start | bytes 1572872 | tf_op jit(solution)/shard_map/ppermute | solution.py:550
  16.2 2.7 %collective-permute-start.2 = (f32[1,128,1024]{2,1,0:T(8,128)S(1)}, f32[1,128,1024]{2,1,0:T(8,128)S(1)}, u32[]{:S(2)}, u32[]{:S(2)}) collective-permute-start(f32[1,128,1024]{2,1,0:T(8,128)S(1)} %copy-done.4), channel_id=1, source_target_pairs={{0,8},{8,16},{16,24},{24,32},{32,40},{40,48},{48,56},{56,64},{64,7... | collective-permute-start | bytes 1572872 | tf_op jit(solution)/shard_map/ppermute | solution.py:549
  19.0 0.1 pad_add_fusion.place
  19.0 23.9 %collective-permute-done.ahead = f32[1,128,1024]{2,1,0:T(8,128)S(1)} collective-permute-done((f32[1,128,1024]{2,1,0:T(8,128)S(1)}, f32[1,128,1024]{2,1,0:T(8,128)S(1)}, u32[]{:S(2)}, u32[]{:S(2)}) %collective-permute-start) | collective-permute-done | bytes 524320 | tf_op jit(solution)/shard_map/ppermute | solution.py:550
  42.9 0.8 copy-done.7
  43.7 3.4 %collective-permute-start.1 = (f32[2,1,1024]{2,1,0:T(1,128)S(1)}, f32[2,1,1024]{2,1,0:T(1,128)S(1)}, u32[]{:S(2)}, u32[]{:S(2)}) collective-permute-start(f32[2,1,1024]{2,1,0:T(1,128)S(1)} %pad_maximum_fusion), channel_id=1, source_target_pairs={{0,1},{1,2},{2,3},{3,4},{4,5},{5,6},{6,7},{8,9},{9,10},{10,11},{11... | collective-permute-start | bytes 24584 | tf_op jit(solution)/shard_map/ppermute | solution.py:563
  47.1 0.0 collective-permute-done.2.behind
  47.1 0.0 copy-start.9
  47.1 0.8 copy-done.9
  47.9 1.5 %collective-permute-start.3 = (f32[2,1,1024]{2,1,0:T(1,128)S(1)}, f32[2,1,1024]{2,1,0:T(1,128)S(1)}, u32[]{:S(2)}, u32[]{:S(2)}) collective-permute-start(f32[2,1,1024]{2,1,0:T(1,128)S(1)} %pad_maximum_fusion.1), channel_id=1, source_target_pairs={{1,0},{2,1},{3,2},{4,3},{5,4},{6,5},{7,6},{9,8},{10,9},{11,10},{12... | collective-permute-start | bytes 24584 | tf_op jit(solution)/shard_map/ppermute | solution.py:564
  49.4 0.0 copy-start.5
  49.4 1.0 copy-done.5
  50.5 1.0 copy-done.8
  51.5 1.0 copy-done.10
  52.6 4.9 %shard_map.51 = (f32[8,272,128]{2,1,0:T(8,128)S(1)}, f32[128,1024]{1,0:T(8,128)S(1)}, f32[128,1024]{1,0:T(8,128)S(1)}, f32[128,1024]{1,0:T(8,128)S(1)}, f32[16,1024]{1,0:T(8,128)S(1)}) custom-call(s32[2]{0:T(128)S(1)} %pad_add_fusion.place, f32[1,128,1024]{2,1,0:T(8,128)S(1)} %copy-done.5, f32[1,128,1024]{2,1,0:T(8,128)S(1)} %copy-done.10, ...), custom_call_target="tpu_custom_call" | custom-call | flops 805306368 | bytes 4325384 | tf_op jit(solution)/shard_map/pallas_call | solution.py:47
  57.5 0.0 copy-start
  57.5 0.8 copy-done
  58.3 0.8 copy-done.11
  59.1 0.0 collective-permute-done.1.from_above
  59.1 0.0 collective-permute-done.3.from_below
  59.1 2.9 %shard_map.52 = (f32[8,272,128]{2,1,0:T(8,128)S(1)}, f32[8,1024]{1,0:T(8,128)S(1)}) custom-call(s32[2]{0:T(128)S(1)} %pad_add_fusion.place, f32[2,1,1024]{2,1,0:T(1,128)S(1)} %collective-permute-done.1.from_above, f32[2,1,1024]{2,1,0:T(1,128)S(1)} %collective-permute-done.3.from_below, ...), custom_call_target="tpu_custom_call", output_to_operand_aliasing={{0}: (4, {})} | custom-call | flops 268435456 | bytes 2342920 | tf_op jit(solution)/shard_map/pallas_call | solution.py:47
  62.0 0.0 all-to-all-done.got
  62.0 5.1 %shard_map.53 = (f32[8,272,128]{2,1,0:T(8,128)S(1)}, f32[1024,256]{1,0:T(8,128)S(1)}) custom-call(f32[8,3,128,128]{3,2,1,0:T(8,128)S(1)} %all-to-all-done.got, f32[8,272,128]{2,1,0:T(8,128)S(1)} %get-tuple-element.18.half_sent), custom_call_target="tpu_custom_call", output_to_operand_aliasing={{0}: (1, {})} | custom-call | flops 2415919104 | bytes 4849664 | tf_op jit(solution)/shard_map/pallas_call | solution.py:47
  67.1 0.0 copy-start.12
  67.1 21.4 %all_to_all.20.got = f32[8,272,128]{2,1,0:T(8,128)S(1)} all-to-all(f32[8,272,128]{2,1,0:T(8,128)S(1)} %get-tuple-element.19), channel_id=1, replica_groups=mesh['planes_0'=4,'planes_1'=2,'planes_2'=2,'rows_0'=2,'rows_1'=4] {'row..., dimensions={0} | all-to-all | bytes 2228224 | tf_op jit(solution)/shard_map/all_to_all | solution.py:532
  88.5 2.3 %shard_map.54 = (f32[1,128,1024]{2,1,0:T(8,128)S(1)}, f32[8,1024]{1,0:T(8,128)S(1)}) custom-call(s32[2]{0:T(128)S(1)} %pad_add_fusion.place, f32[8,272,128]{2,1,0:T(8,128)S(1)} %all_to_all.20.got, f32[128,1024]{1,0:T(8,128)S(1)} %copy-done.12, f32[8,1024]{1,0:T(8,128)S(1)} %get-tuple-element.21.w_edge), custom_call_target="tpu_custom_call" | custom-call | flops 805306368 | bytes 2228232 | tf_op jit(solution)/shard_map/pallas_call | solution.py:47
  90.8 2.1 %collective-permute-start.4 = (f32[1,128,1024]{2,1,0:T(8,128)S(1)}, f32[1,128,1024]{2,1,0:T(8,128)S(1)}, u32[]{:S(2)}, u32[]{:S(2)}) collective-permute-start(f32[1,128,1024]{2,1,0:T(8,128)S(1)} %get-tuple-element.28.residual), channel_id=1, source_target_pairs={{8,0},{16,8},{24,16},{32,24},{40,32},{48,40},{56,48},{64,56},{72,6... | collective-permute-start | bytes 1572872 | tf_op jit(solution)/shard_map/ppermute | solution.py:599
  93.0 0.9 shard_map.55.parts
  93.9 4.0 %shard_map.56 = (f32[8,136,128]{2,1,0:T(8,128)}, f32[8,128]{1,0:T(8,128)S(1)}) custom-call(f32[8,272,128]{2,1,0:T(8,128)S(1)} %all_to_all.20.got, f32[1024,256]{1,0:T(8,128)S(1)} %get-tuple-element.25.spectral), custom_call_target="tpu_custom_call" | custom-call | flops 1610612736 | bytes 2723840 | tf_op jit(solution)/shard_map/pallas_call | solution.py:47
  97.9 8.7 %collective-permute-done.4.ahead = f32[1,128,1024]{2,1,0:T(8,128)S(1)} collective-permute-done((f32[1,128,1024]{2,1,0:T(8,128)S(1)}, f32[1,128,1024]{2,1,0:T(8,128)S(1)}, u32[]{:S(2)}, u32[]{:S(2)}) %collective-permute-start.4) | collective-permute-done | bytes 524320 | tf_op jit(solution)/shard_map/ppermute | solution.py:599
  106.6 1.3 shard_map.57
  108.0 0.0 copy-start.1
  108.0 3.7 %all-to-all-start.2 = ((f32[8,136,128]{2,1,0:T(8,128)}), f32[8,136,128]{2,1,0:T(8,128)S(1)}, u32[]{:S(2)}, u32[]{:S(2)}) async-start(f32[8,136,128]{2,1,0:T(8,128)} %shard_map.57), calls=%async_computation.2 | async-start | bytes 1114112 | tf_op jit(solution)/shard_map/all_to_all | solution.py:532
  111.7 1.9 %collective-permute-start.5 = (f32[1,128,1024]{2,1,0:T(8,128)S(1)}, f32[1,128,1024]{2,1,0:T(8,128)S(1)}, u32[]{:S(2)}, u32[]{:S(2)}) collective-permute-start(f32[1,128,1024]{2,1,0:T(8,128)S(1)} %get-tuple-element.28.residual), channel_id=1, source_target_pairs={{0,8},{8,16},{16,24},{24,32},{32,40},{40,48},{48,56},{56,64},{64,7... | collective-permute-start | bytes 1572872 | tf_op jit(solution)/shard_map/ppermute | solution.py:612
  113.6 6.8 %all-to-all-done.2.got = f32[8,136,128]{2,1,0:T(8,128)S(1)} async-done(((f32[8,136,128]{2,1,0:T(8,128)}), f32[8,136,128]{2,1,0:T(8,128)S(1)}, u32[]{:S(2)}, u32[]{:S(2)}) %all-to-all-start.2) | async-done | bytes 557088 | tf_op jit(solution)/shard_map/all_to_all | solution.py:532
  120.4 0.6 broadcast_in_dim.2
  121.0 8.0 %all-to-all-start.3 = ((f32[16,8,128]{2,1,0:T(8,128)}), f32[16,8,128]{2,1,0:T(8,128)S(1)}, u32[]{:S(2)}, u32[]{:S(2)}) async-start(f32[16,8,128]{2,1,0:T(8,128)} %broadcast_in_dim.2), calls=%async_computation.3 | async-start | bytes 131072 | tf_op jit(solution)/shard_map/all_to_all | solution.py:532
  129.0 0.0 collective-permute-done.5.behind
  129.0 1.2 shard_map.58.reg
  130.2 0.0 copy-start.2
  130.2 0.8 copy-done.2
  131.0 3.8 %all-to-all-done.3.sums = f32[16,8,128]{2,1,0:T(8,128)S(1)} async-done(((f32[16,8,128]{2,1,0:T(8,128)}), f32[16,8,128]{2,1,0:T(8,128)S(1)}, u32[]{:S(2)}, u32[]{:S(2)}) %all-to-all-start.3) | async-done | bytes 65568 | tf_op jit(solution)/shard_map/all_to_all | solution.py:532
  134.8 1.0 copy-done.3
  135.9 1.0 copy-done.6
  136.9 2.5 %shard_map.59 = (f32[1,128,1024]{2,1,0:T(8,128)}, f32[1,128,1024]{2,1,0:T(8,128)}) custom-call(f32[16,8,128]{2,1,0:T(8,128)S(1)} %all-to-all-done.3.sums, f32[8,136,128]{2,1,0:T(8,128)S(1)} %all-to-all-done.2.got, f32[128,1024]{1,0:T(8,128)S(1)} %copy-done.3, f32[1,128,1024]{2,1,0:T(8,128)S(1)} %get-tuple-element.28.residual, f32[1,128,1024]{2,1,0:T(8,128)S(1)} %copy-done.6), custom_call_target="tpu_custom_call" | custom-call | flops 805306368 | bytes 3244032 | tf_op jit(solution)/shard_map/pallas_call | solution.py:47
  (15 shorter events, 0.1 us)
Async XLA Ops:
  4.9 8.5 %copy-start.4 = (f32[1,128,1024]{2,1,0:T(8,128)S(1)}, f32[1,128,1024]{2,1,0:T(8,128)}, u32[]{:S(2)}) copy-start(f32[1,128,1024]{2,1,0:T(8,128)} %estimate.5) | copy-start | bytes 1572868
  4.9 57.1 %all-to-all-start = ((f32[8,3,128,128]{3,2,1,0:T(8,128)}), f32[8,3,128,128]{3,2,1,0:T(8,128)S(1)}, u32[]{:S(2)}, u32[]{:S(2)}) async-start(f32[8,3,128,128]{3,2,1,0:T(8,128)} %shard_map.50), calls=%async_computation | async-start | bytes 3145728 | tf_op jit(solution)/shard_map/all_to_all | solution.py:532
  13.4 29.6 %collective-permute-start = (f32[1,128,1024]{2,1,0:T(8,128)S(1)}, f32[1,128,1024]{2,1,0:T(8,128)S(1)}, u32[]{:S(2)}, u32[]{:S(2)}) collective-permute-start(f32[1,128,1024]{2,1,0:T(8,128)S(1)} %copy-done.4), channel_id=1, source_target_pairs={{8,0},{16,8},{24,16},{32,24},{40,32},{48,40},{56,48},{64,56},{72,6... | collective-permute-start | bytes 1572872 | tf_op jit(solution)/shard_map/ppermute | solution.py:550
  16.2 30.9 %collective-permute-start.2 = (f32[1,128,1024]{2,1,0:T(8,128)S(1)}, f32[1,128,1024]{2,1,0:T(8,128)S(1)}, u32[]{:S(2)}, u32[]{:S(2)}) collective-permute-start(f32[1,128,1024]{2,1,0:T(8,128)S(1)} %copy-done.4), channel_id=1, source_target_pairs={{0,8},{8,16},{16,24},{24,32},{32,40},{40,48},{48,56},{56,64},{64,7... | collective-permute-start | bytes 1572872 | tf_op jit(solution)/shard_map/ppermute | solution.py:549
  42.9 0.8 copy-start.7
  43.7 15.4 %collective-permute-start.1 = (f32[2,1,1024]{2,1,0:T(1,128)S(1)}, f32[2,1,1024]{2,1,0:T(1,128)S(1)}, u32[]{:S(2)}, u32[]{:S(2)}) collective-permute-start(f32[2,1,1024]{2,1,0:T(1,128)S(1)} %pad_maximum_fusion), channel_id=1, source_target_pairs={{0,1},{1,2},{2,3},{3,4},{4,5},{5,6},{6,7},{8,9},{9,10},{10,11},{11... | collective-permute-start | bytes 24584 | tf_op jit(solution)/shard_map/ppermute | solution.py:563
  47.1 0.8 copy-start.9
  47.9 11.2 %collective-permute-start.3 = (f32[2,1,1024]{2,1,0:T(1,128)S(1)}, f32[2,1,1024]{2,1,0:T(1,128)S(1)}, u32[]{:S(2)}, u32[]{:S(2)}) collective-permute-start(f32[2,1,1024]{2,1,0:T(1,128)S(1)} %pad_maximum_fusion.1), channel_id=1, source_target_pairs={{1,0},{2,1},{3,2},{4,3},{5,4},{6,5},{7,6},{9,8},{10,9},{11,10},{12... | collective-permute-start | bytes 24584 | tf_op jit(solution)/shard_map/ppermute | solution.py:564
  49.4 1.0 copy-start.5
  50.5 1.0 copy-start.8
  51.5 1.0 copy-start.10
  57.5 0.8 copy-start
  58.3 0.8 copy-start.11
  67.1 21.4 %copy-start.12 = (f32[128,1024]{1,0:T(8,128)S(1)}, f32[128,1024]{1,0:T(8,128)}, u32[]{:S(2)}) copy-start(f32[128,1024]{1,0:T(8,128)} %copy-done.11) | copy-start | bytes 1572868
  90.8 15.8 %collective-permute-start.4 = (f32[1,128,1024]{2,1,0:T(8,128)S(1)}, f32[1,128,1024]{2,1,0:T(8,128)S(1)}, u32[]{:S(2)}, u32[]{:S(2)}) collective-permute-start(f32[1,128,1024]{2,1,0:T(8,128)S(1)} %get-tuple-element.28.residual), channel_id=1, source_target_pairs={{8,0},{16,8},{24,16},{32,24},{40,32},{48,40},{56,48},{64,56},{72,6... | collective-permute-start | bytes 1572872 | tf_op jit(solution)/shard_map/ppermute | solution.py:599
  108.0 21.1 %copy-start.1 = (f32[128,1024]{1,0:T(8,128)S(1)}, f32[128,1024]{1,0:T(8,128)}, u32[]{:S(2)}) copy-start(f32[128,1024]{1,0:T(8,128)} %copy-done) | copy-start | bytes 1572868
  108.0 12.4 %all-to-all-start.2 = ((f32[8,136,128]{2,1,0:T(8,128)}), f32[8,136,128]{2,1,0:T(8,128)S(1)}, u32[]{:S(2)}, u32[]{:S(2)}) async-start(f32[8,136,128]{2,1,0:T(8,128)} %shard_map.57), calls=%async_computation.2 | async-start | bytes 1114112 | tf_op jit(solution)/shard_map/all_to_all | solution.py:532
  111.7 17.4 %collective-permute-start.5 = (f32[1,128,1024]{2,1,0:T(8,128)S(1)}, f32[1,128,1024]{2,1,0:T(8,128)S(1)}, u32[]{:S(2)}, u32[]{:S(2)}) collective-permute-start(f32[1,128,1024]{2,1,0:T(8,128)S(1)} %get-tuple-element.28.residual), channel_id=1, source_target_pairs={{0,8},{8,16},{16,24},{24,32},{32,40},{40,48},{48,56},{56,64},{64,7... | collective-permute-start | bytes 1572872 | tf_op jit(solution)/shard_map/ppermute | solution.py:612
  121.0 13.8 %all-to-all-start.3 = ((f32[16,8,128]{2,1,0:T(8,128)}), f32[16,8,128]{2,1,0:T(8,128)S(1)}, u32[]{:S(2)}, u32[]{:S(2)}) async-start(f32[16,8,128]{2,1,0:T(8,128)} %broadcast_in_dim.2), calls=%async_computation.3 | async-start | bytes 131072 | tf_op jit(solution)/shard_map/all_to_all | solution.py:532
  130.2 0.8 copy-start.2
  134.8 1.0 copy-start.3
  135.9 1.0 copy-start.6

commit v5 on v4

--- a/solution.py
+++ b/solution.py
@@ -275,11 +275,7 @@
         copy.wait()
 
 
-def edge_kernel(
-    place, from_above, from_below, strip, half_sent, sent, w_edge,
-    table_v, high, low, stack, rows_v, tiles_v, sems,
-):
-    fill_table(table_v, True)
+def fill_edges(place, from_above, from_below, strip, sent, w_edge, stack, tiles_v, sem):
     plane, row = place[0], place[1]
     ok_plane = jnp.where(plane < 15, 1.0, 0.0)
     ok_back = jnp.where(plane > 0, 1.0, 0.0)
@@ -315,30 +311,19 @@
     head_tile, tail_tile = as_tile(first_row), as_tile(last_row)
     for e in range(G):
         tiles_v[e] = jnp.where(row == e - 1, tail_tile, jnp.where(row == e + 1, head_tile, 0.0))
-    tile_copy = start(tiles_v, sent.at[:, EDGE:REG], sems.at[16])
+    tile_copy = start(tiles_v, sent.at[:, EDGE:REG], sem)
     pair = jnp.concatenate([first_row, last_row, jnp.zeros((14, N), F32)], axis=0)
     stack[0:16, :], stack[16:32, :] = split(pair)
-    out_copies = []
-    for d in range(G // 2):
-        columns = slice(256 * d, 256 * d + 256)
-        build_samples(table_v, high, low, WHOLE, columns)
-        out = stacked_times(stack, 16, high, low, columns)
-        for h in range(2):
-            e = 2 * d + h
-            rows_v[e] = out[0:8, 128 * h : 128 * h + 128]
-            for i, at in enumerate((0, R - 1)):
-                out_copies.append(
-                    start(rows_v.at[e, i : i + 1], sent.at[e, REG + at : REG + at + 1], sems.at[2 * e + i])
-                )
-    tile_copy.wait()
-    for copy in out_copies:
-        copy.wait()
+    return tile_copy
 
 
 def middle_kernel(
-    got, half_sent, sent, spectral, freq_v, sample_v, sent_v, f_high, f_low, s_high, s_low, pair,
-    sems,
-):
+    place, got, from_above, from_below, strip, half_sent, sent, spectral, w_edge,
+    freq_v, sample_v, sent_v, f_high, f_low, s_high, s_low, pair, stack, rows_v, tiles_v, sems,
+):
+    tile_copy = fill_edges(
+        place, from_above, from_below, strip, sent, w_edge, stack, tiles_v, sems.at[8]
+    )
     fill_table(freq_v, False)
     fill_table(sample_v, True)
     for d in range(G):
@@ -370,6 +355,16 @@
                 sent_v[d - 1, R + 1 : R + 2] = block[0:1]
                 out_copies.append(start(sent_v.at[d - 1], sent.at[d - 1, 0:EDGE], sems.at[d]))
     out_copies.append(start(sent_v.at[G - 1], sent.at[G - 1, 0:EDGE], sems.at[0]))
+    for d in range(G // 2):
+        out = stacked_times(stack, 16, s_high, s_low, slice(256 * d, 256 * d + 256))
+        for h in range(2):
+            e = 2 * d + h
+            rows_v[e] = out[0:8, 128 * h : 128 * h + 128]
+            for i, at in enumerate((0, R - 1)):
+                out_copies.append(
+                    start(rows_v.at[e, i : i + 1], sent.at[e, REG + at : REG + at + 1], sems.at[9 + 2 * e + i])
+                )
+    tile_copy.wait()
     for copy in out_copies:
         copy.wait()
 
@@ -571,22 +566,15 @@
          field(R + 16), MATRIX, MATRIX, pltpu.VMEM((2 * R, N), BF16), DMA((5,))),
         (ANY, VMEM, VMEM, VMEM, VMEM), direct=4,
     )(place, estimate, behind, ahead)
-    half_sent, w_edge = call(
-        edge_kernel,
-        (wide, shape(8, N)),
-        big,
-        (TABLE, MATRIX, MATRIX, pltpu.VMEM((32, N), BF16), pltpu.VMEM((G, 8, 128), F32),
-         pltpu.VMEM((G, 8, 128), F32), DMA((17,))),
-        (ANY, VMEM), {4: 0}, direct=4,
-    )(place, from_above, from_below, strip, half_sent)
-    sent, spectral = call(
+    sent, spectral, w_edge = call(
         middle_kernel,
-        (wide, shape(N, 256)),
+        (wide, shape(N, 256), shape(8, N)),
         9 * big,
         (TABLE, TABLE, pltpu.VMEM((G, EDGE, 128), F32), MATRIX, MATRIX, MATRIX, MATRIX,
-         pltpu.VMEM((N, 768), BF16), DMA((8,))),
-        (ANY, VMEM), {1: 0}, direct=1,
-    )(first, half_sent)
+         pltpu.VMEM((N, 768), BF16), pltpu.VMEM((32, N), BF16), pltpu.VMEM((G, 8, 128), F32),
+         pltpu.VMEM((G, 8, 128), F32), DMA((25,))),
+        (ANY, VMEM, VMEM), {5: 0}, direct=5,
+    )(place, first, from_above, from_below, strip, half_sent)
     second = across(sent, ROWS)
 
     residual, edges = call(

time: 140 us -> 140 us (level)
    pallas_call x10 -> x9, Pallas kernels: 29.5 us -> 29.2 us  [launch(): pl.pallas_call(body, out_shape=tuple(outs), in_specs=[place_of(i, a) for...]
  transfers between devices with their start and end apart: 9 -> 9, of which waited for: 4 -> 4; matrix products, arithmetic and copies ran while one was open for 1% -> 1% of each run, Pallas kernels for 10% -> 8%
where the time goes in v5:
time: 140 us; the launch traced here: 139 us
  waiting for transfers between devices  43.4 us (31%)
  starting transfers between devices  34.4 us (25%)
  Pallas kernels  29.2 us (21%)
  blocking collectives  21.4 us (15%)
  local copies, waits for them, and re-layouts  9.81 us (7%)
    pallas_call x9, Pallas kernels, launch(): pl.pallas_call(body, out_shape=tuple(outs), in_specs=[place_of(i, a) for...  29.2 us
    ppermute x1, waiting for transfers between devices, step(): ahead = lax.ppermute(estimate, PLANES, down)  23.9 us
    all_to_all x1, blocking collectives, across(): return lax.all_to_all(x, axes, split_axis=0, concat_axis=0, tiled=True)  21.4 us
    all_to_all x3, starting transfers between devices, across(): return lax.all_to_all(x, axes, split_axis=0, concat_axis=0, tiled=True)  20.4 us
    all_to_all x3, waiting for transfers between devices, across(): return lax.all_to_all(x, axes, split_axis=0, concat_axis=0, tiled=True)  10.6 us
    unnamed x26, local copies, waits for them, and re-layouts  9.17 us
    ppermute x1, waiting for transfers between devices, step(): ahead = lax.ppermute(residual, PLANES, down)  8.93 us
    ppermute x1, starting transfers between devices, step(): from_above = lax.ppermute(tails, ROWS, row_up)  3.37 us
  transfers between devices with their start and end apart: 9, of which 4 were waited for; matrix products, arithmetic and copies ran while one was open for 1% of the time, Pallas kernels for 8%

profile of v5, /device:TPU:1, one launch (start us, length us, event | category | flops | bytes accessed | tf_op | source)
XLA Modules:
  0.0 139.3 jit_solution(4037487813721613264)
XLA Ops:
  0.6 4.3 %shard_map.50 = f32[8,3,128,128]{3,2,1,0:T(8,128)} custom-call(f32[1,128,1024]{2,1,0:T(8,128)} %observed.1, f32[1,128,1024]{2,1,0:T(8,128)} %estimate.5, f32[1,128,1024]{2,1,0:T(8,128)} %spectrum.1), custom_call_target="tpu_custom_call" | custom-call | flops 1610612736 | bytes 3145728 | tf_op jit(solution)/shard_map/pallas_call | solution.py:47
  4.9 0.0 copy-start.4
  4.9 8.4 %all-to-all-start = ((f32[8,3,128,128]{3,2,1,0:T(8,128)}), f32[8,3,128,128]{3,2,1,0:T(8,128)S(1)}, u32[]{:S(2)}, u32[]{:S(2)}) async-start(f32[8,3,128,128]{3,2,1,0:T(8,128)} %shard_map.50), calls=%async_computation | async-start | bytes 3145728 | tf_op jit(solution)/shard_map/all_to_all | solution.py:527
  13.4 2.9 %collective-permute-start = (f32[1,128,1024]{2,1,0:T(8,128)S(1)}, f32[1,128,1024]{2,1,0:T(8,128)S(1)}, u32[]{:S(2)}, u32[]{:S(2)}) collective-permute-start(f32[1,128,1024]{2,1,0:T(8,128)S(1)} %copy-done.4), channel_id=1, source_target_pairs={{8,0},{16,8},{24,16},{32,24},{40,32},{48,40},{56,48},{64,56},{72,6... | collective-permute-start | bytes 1572872 | tf_op jit(solution)/shard_map/ppermute | solution.py:545
  16.3 2.7 %collective-permute-start.2 = (f32[1,128,1024]{2,1,0:T(8,128)S(1)}, f32[1,128,1024]{2,1,0:T(8,128)S(1)}, u32[]{:S(2)}, u32[]{:S(2)}) collective-permute-start(f32[1,128,1024]{2,1,0:T(8,128)S(1)} %copy-done.4), channel_id=1, source_target_pairs={{0,8},{8,16},{16,24},{24,32},{32,40},{40,48},{48,56},{56,64},{64,7... | collective-permute-start | bytes 1572872 | tf_op jit(solution)/shard_map/ppermute | solution.py:544
  19.0 0.1 pad_add_fusion.place
  19.1 23.9 %collective-permute-done.ahead = f32[1,128,1024]{2,1,0:T(8,128)S(1)} collective-permute-done((f32[1,128,1024]{2,1,0:T(8,128)S(1)}, f32[1,128,1024]{2,1,0:T(8,128)S(1)}, u32[]{:S(2)}, u32[]{:S(2)}) %collective-permute-start) | collective-permute-done | bytes 524320 | tf_op jit(solution)/shard_map/ppermute | solution.py:545
  42.9 0.8 copy-done.7
  43.7 3.4 %collective-permute-start.1 = (f32[2,1,1024]{2,1,0:T(1,128)S(1)}, f32[2,1,1024]{2,1,0:T(1,128)S(1)}, u32[]{:S(2)}, u32[]{:S(2)}) collective-permute-start(f32[2,1,1024]{2,1,0:T(1,128)S(1)} %pad_maximum_fusion), channel_id=1, source_target_pairs={{0,1},{1,2},{2,3},{3,4},{4,5},{5,6},{6,7},{8,9},{9,10},{10,11},{11... | collective-permute-start | bytes 24584 | tf_op jit(solution)/shard_map/ppermute | solution.py:558
  47.1 0.0 collective-permute-done.2.behind
  47.1 0.0 copy-start.9
  47.2 0.8 copy-done.9
  47.9 1.3 collective-permute-start.3
  49.2 0.0 copy-start.5
  49.3 1.0 copy-done.5
  50.3 1.0 copy-done.8
  51.3 1.0 copy-done.10
  52.4 4.9 %shard_map.51 = (f32[8,272,128]{2,1,0:T(8,128)S(1)}, f32[128,1024]{1,0:T(8,128)S(1)}, f32[128,1024]{1,0:T(8,128)S(1)}, f32[128,1024]{1,0:T(8,128)S(1)}, f32[16,1024]{1,0:T(8,128)S(1)}) custom-call(s32[2]{0:T(128)S(1)} %pad_add_fusion.place, f32[1,128,1024]{2,1,0:T(8,128)S(1)} %copy-done.5, f32[1,128,1024]{2,1,0:T(8,128)S(1)} %copy-done.10, ...), custom_call_target="tpu_custom_call" | custom-call | flops 805306368 | bytes 4325384 | tf_op jit(solution)/shard_map/pallas_call | solution.py:47
  57.3 0.0 copy-start
  57.3 0.8 copy-done
  58.1 0.8 copy-done.11
  58.9 0.0 collective-permute-done.1.from_above
  58.9 0.0 collective-permute-done.3.from_below
  58.9 0.0 all-to-all-done.got
  58.9 7.7 %shard_map.52 = (f32[8,272,128]{2,1,0:T(8,128)S(1)}, f32[1024,256]{1,0:T(8,128)S(1)}, f32[8,1024]{1,0:T(8,128)S(1)}) custom-call(s32[2]{0:T(128)S(1)} %pad_add_fusion.place, f32[8,3,128,128]{3,2,1,0:T(8,128)S(1)} %all-to-all-done.got, f32[2,1,1024]{2,1,0:T(1,128)S(1)} %collective-permute-done.1.from_above, ...), custom_call_target="tpu_custom_call", output_to_operand_aliasing={{0}: (5, {})} | custom-call | flops 2415919104 | bytes 4964360 | tf_op jit(solution)/shard_map/pallas_call | solution.py:47
  66.6 0.0 copy-start.12
  66.6 21.4 %all_to_all.20.got = f32[8,272,128]{2,1,0:T(8,128)S(1)} all-to-all(f32[8,272,128]{2,1,0:T(8,128)S(1)} %get-tuple-element.17), channel_id=1, replica_groups=mesh['planes_0'=4,'planes_1'=2,'planes_2'=2,'rows_0'=2,'rows_1'=4] {'row..., dimensions={0} | all-to-all | bytes 2228224 | tf_op jit(solution)/shard_map/all_to_all | solution.py:527
  88.0 0.0 copy-done.12
  88.0 2.3 %shard_map.53 = (f32[1,128,1024]{2,1,0:T(8,128)S(1)}, f32[8,1024]{1,0:T(8,128)S(1)}) custom-call(s32[2]{0:T(128)S(1)} %pad_add_fusion.place, f32[8,272,128]{2,1,0:T(8,128)S(1)} %all_to_all.20.got, f32[128,1024]{1,0:T(8,128)S(1)} %copy-done.12, f32[8,1024]{1,0:T(8,128)S(1)} %get-tuple-element.19.w_edge), custom_call_target="tpu_custom_call" | custom-call | flops 805306368 | bytes 2228232 | tf_op jit(solution)/shard_map/pallas_call | solution.py:47
  90.3 1.9 %collective-permute-start.4 = (f32[1,128,1024]{2,1,0:T(8,128)S(1)}, f32[1,128,1024]{2,1,0:T(8,128)S(1)}, u32[]{:S(2)}, u32[]{:S(2)}) collective-permute-start(f32[1,128,1024]{2,1,0:T(8,128)S(1)} %get-tuple-element.26.residual), channel_id=1, source_target_pairs={{8,0},{16,8},{24,16},{32,24},{40,32},{48,40},{56,48},{64,56},{72,6... | collective-permute-start | bytes 1572872 | tf_op jit(solution)/shard_map/ppermute | solution.py:587
  92.3 0.9 shard_map.54.parts
  93.2 4.0 %shard_map.55 = (f32[8,136,128]{2,1,0:T(8,128)}, f32[8,128]{1,0:T(8,128)S(1)}) custom-call(f32[8,272,128]{2,1,0:T(8,128)S(1)} %all_to_all.20.got, f32[1024,256]{1,0:T(8,128)S(1)} %get-tuple-element.23.spectral), custom_call_target="tpu_custom_call" | custom-call | flops 1610612736 | bytes 2723840 | tf_op jit(solution)/shard_map/pallas_call | solution.py:47
  97.2 8.9 %collective-permute-done.4.ahead = f32[1,128,1024]{2,1,0:T(8,128)S(1)} collective-permute-done((f32[1,128,1024]{2,1,0:T(8,128)S(1)}, f32[1,128,1024]{2,1,0:T(8,128)S(1)}, u32[]{:S(2)}, u32[]{:S(2)}) %collective-permute-start.4) | collective-permute-done | bytes 524320 | tf_op jit(solution)/shard_map/ppermute | solution.py:587
  106.1 1.3 shard_map.56
  107.5 0.0 copy-start.1
  107.5 3.7 %all-to-all-start.2 = ((f32[8,136,128]{2,1,0:T(8,128)}), f32[8,136,128]{2,1,0:T(8,128)S(1)}, u32[]{:S(2)}, u32[]{:S(2)}) async-start(f32[8,136,128]{2,1,0:T(8,128)} %shard_map.56), calls=%async_computation.2 | async-start | bytes 1114112 | tf_op jit(solution)/shard_map/all_to_all | solution.py:527
  111.2 1.9 %collective-permute-start.5 = (f32[1,128,1024]{2,1,0:T(8,128)S(1)}, f32[1,128,1024]{2,1,0:T(8,128)S(1)}, u32[]{:S(2)}, u32[]{:S(2)}) collective-permute-start(f32[1,128,1024]{2,1,0:T(8,128)S(1)} %get-tuple-element.26.residual), channel_id=1, source_target_pairs={{0,8},{8,16},{16,24},{24,32},{32,40},{40,48},{48,56},{56,64},{64,7... | collective-permute-start | bytes 1572872 | tf_op jit(solution)/shard_map/ppermute | solution.py:600
  113.1 6.8 %all-to-all-done.2.got = f32[8,136,128]{2,1,0:T(8,128)S(1)} async-done(((f32[8,136,128]{2,1,0:T(8,128)}), f32[8,136,128]{2,1,0:T(8,128)S(1)}, u32[]{:S(2)}, u32[]{:S(2)}) %all-to-all-start.2) | async-done | bytes 557088 | tf_op jit(solution)/shard_map/all_to_all | solution.py:527
  119.9 0.6 broadcast_in_dim.2
  120.5 8.2 %all-to-all-start.3 = ((f32[16,8,128]{2,1,0:T(8,128)}), f32[16,8,128]{2,1,0:T(8,128)S(1)}, u32[]{:S(2)}, u32[]{:S(2)}) async-start(f32[16,8,128]{2,1,0:T(8,128)} %broadcast_in_dim.2), calls=%async_computation.3 | async-start | bytes 131072 | tf_op jit(solution)/shard_map/all_to_all | solution.py:527
  128.7 0.0 collective-permute-done.5.behind
  128.8 1.2 shard_map.57.reg
  130.0 0.0 copy-start.2
  130.0 0.8 copy-done.2
  130.8 3.8 %all-to-all-done.3.sums = f32[16,8,128]{2,1,0:T(8,128)S(1)} async-done(((f32[16,8,128]{2,1,0:T(8,128)}), f32[16,8,128]{2,1,0:T(8,128)S(1)}, u32[]{:S(2)}, u32[]{:S(2)}) %all-to-all-start.3) | async-done | bytes 65568 | tf_op jit(solution)/shard_map/all_to_all | solution.py:527
  134.6 1.0 copy-done.3
  135.6 1.0 copy-done.6
  136.6 2.5 %shard_map.58 = (f32[1,128,1024]{2,1,0:T(8,128)}, f32[1,128,1024]{2,1,0:T(8,128)}) custom-call(f32[16,8,128]{2,1,0:T(8,128)S(1)} %all-to-all-done.3.sums, f32[8,136,128]{2,1,0:T(8,128)S(1)} %all-to-all-done.2.got, f32[128,1024]{1,0:T(8,128)S(1)} %copy-done.3, f32[1,128,1024]{2,1,0:T(8,128)S(1)} %get-tuple-element.26.residual, f32[1,128,1024]{2,1,0:T(8,128)S(1)} %copy-done.6), custom_call_target="tpu_custom_call" | custom-call | flops 805306368 | bytes 3244032 | tf_op jit(solution)/shard_map/pallas_call | solution.py:47
  (14 shorter events, 0.1 us)
Async XLA Ops:
  4.9 8.5 %copy-start.4 = (f32[1,128,1024]{2,1,0:T(8,128)S(1)}, f32[1,128,1024]{2,1,0:T(8,128)}, u32[]{:S(2)}) copy-start(f32[1,128,1024]{2,1,0:T(8,128)} %estimate.5) | copy-start | bytes 1572868
  4.9 54.0 %all-to-all-start = ((f32[8,3,128,128]{3,2,1,0:T(8,128)}), f32[8,3,128,128]{3,2,1,0:T(8,128)S(1)}, u32[]{:S(2)}, u32[]{:S(2)}) async-start(f32[8,3,128,128]{3,2,1,0:T(8,128)} %shard_map.50), calls=%async_computation | async-start | bytes 3145728 | tf_op jit(solution)/shard_map/all_to_all | solution.py:527
  13.4 29.6 %collective-permute-start = (f32[1,128,1024]{2,1,0:T(8,128)S(1)}, f32[1,128,1024]{2,1,0:T(8,128)S(1)}, u32[]{:S(2)}, u32[]{:S(2)}) collective-permute-start(f32[1,128,1024]{2,1,0:T(8,128)S(1)} %copy-done.4), channel_id=1, source_target_pairs={{8,0},{16,8},{24,16},{32,24},{40,32},{48,40},{56,48},{64,56},{72,6... | collective-permute-start | bytes 1572872 | tf_op jit(solution)/shard_map/ppermute | solution.py:545
  16.3 30.9 %collective-permute-start.2 = (f32[1,128,1024]{2,1,0:T(8,128)S(1)}, f32[1,128,1024]{2,1,0:T(8,128)S(1)}, u32[]{:S(2)}, u32[]{:S(2)}) collective-permute-start(f32[1,128,1024]{2,1,0:T(8,128)S(1)} %copy-done.4), channel_id=1, source_target_pairs={{0,8},{8,16},{16,24},{24,32},{32,40},{40,48},{48,56},{56,64},{64,7... | collective-permute-start | bytes 1572872 | tf_op jit(solution)/shard_map/ppermute | solution.py:544
  42.9 0.8 copy-start.7
  43.7 15.2 %collective-permute-start.1 = (f32[2,1,1024]{2,1,0:T(1,128)S(1)}, f32[2,1,1024]{2,1,0:T(1,128)S(1)}, u32[]{:S(2)}, u32[]{:S(2)}) collective-permute-start(f32[2,1,1024]{2,1,0:T(1,128)S(1)} %pad_maximum_fusion), channel_id=1, source_target_pairs={{0,1},{1,2},{2,3},{3,4},{4,5},{5,6},{6,7},{8,9},{9,10},{10,11},{11... | collective-permute-start | bytes 24584 | tf_op jit(solution)/shard_map/ppermute | solution.py:558
  47.1 0.8 copy-start.9
  47.9 11.0 %collective-permute-start.3 = (f32[2,1,1024]{2,1,0:T(1,128)S(1)}, f32[2,1,1024]{2,1,0:T(1,128)S(1)}, u32[]{:S(2)}, u32[]{:S(2)}) collective-permute-start(f32[2,1,1024]{2,1,0:T(1,128)S(1)} %pad_maximum_fusion.1), channel_id=1, source_target_pairs={{1,0},{2,1},{3,2},{4,3},{5,4},{6,5},{7,6},{9,8},{10,9},{11,10},{12... | collective-permute-start | bytes 24584 | tf_op jit(solution)/shard_map/ppermute | solution.py:559
  49.2 1.0 copy-start.5
  50.3 1.0 copy-start.8
  51.3 1.0 copy-start.10
  57.3 0.8 copy-start
  58.1 0.8 copy-start.11
  66.6 21.4 %copy-start.12 = (f32[128,1024]{1,0:T(8,128)S(1)}, f32[128,1024]{1,0:T(8,128)}, u32[]{:S(2)}) copy-start(f32[128,1024]{1,0:T(8,128)} %copy-done.11) | copy-start | bytes 1572868
  90.3 15.8 %collective-permute-start.4 = (f32[1,128,1024]{2,1,0:T(8,128)S(1)}, f32[1,128,1024]{2,1,0:T(8,128)S(1)}, u32[]{:S(2)}, u32[]{:S(2)}) collective-permute-start(f32[1,128,1024]{2,1,0:T(8,128)S(1)} %get-tuple-element.26.residual), channel_id=1, source_target_pairs={{8,0},{16,8},{24,16},{32,24},{40,32},{48,40},{56,48},{64,56},{72,6... | collective-permute-start | bytes 1572872 | tf_op jit(solution)/shard_map/ppermute | solution.py:587
  107.5 21.3 %copy-start.1 = (f32[128,1024]{1,0:T(8,128)S(1)}, f32[128,1024]{1,0:T(8,128)}, u32[]{:S(2)}) copy-start(f32[128,1024]{1,0:T(8,128)} %copy-done) | copy-start | bytes 1572868
  107.5 12.4 %all-to-all-start.2 = ((f32[8,136,128]{2,1,0:T(8,128)}), f32[8,136,128]{2,1,0:T(8,128)S(1)}, u32[]{:S(2)}, u32[]{:S(2)}) async-start(f32[8,136,128]{2,1,0:T(8,128)} %shard_map.56), calls=%async_computation.2 | async-start | bytes 1114112 | tf_op jit(solution)/shard_map/all_to_all | solution.py:527
  111.2 17.6 %collective-permute-start.5 = (f32[1,128,1024]{2,1,0:T(8,128)S(1)}, f32[1,128,1024]{2,1,0:T(8,128)S(1)}, u32[]{:S(2)}, u32[]{:S(2)}) collective-permute-start(f32[1,128,1024]{2,1,0:T(8,128)S(1)} %get-tuple-element.26.residual), channel_id=1, source_target_pairs={{0,8},{8,16},{16,24},{24,32},{32,40},{40,48},{48,56},{56,64},{64,7... | collective-permute-start | bytes 1572872 | tf_op jit(solution)/shard_map/ppermute | solution.py:600
  120.5 14.1 %all-to-all-start.3 = ((f32[16,8,128]{2,1,0:T(8,128)}), f32[16,8,128]{2,1,0:T(8,128)S(1)}, u32[]{:S(2)}, u32[]{:S(2)}) async-start(f32[16,8,128]{2,1,0:T(8,128)} %broadcast_in_dim.2), calls=%async_computation.3 | async-start | bytes 131072 | tf_op jit(solution)/shard_map/all_to_all | solution.py:527
  130.0 0.8 copy-start.2
  134.6 1.0 copy-start.3
  135.6 1.0 copy-start.6
